TPU v7x, 32 devices: a whole 2x2x4 slice. The times are simulated.
32 devices in a mesh: ens: 4 (over x, core), space: 8 (over z, y).
Axes of the slice: x: 2, y: 2, z: 4, core: 2. Of those that a mesh axis runs over, the one named last changes fastest.
Arguments:
- checkpoints: bfloat16 [32, 2, 3, 256, 2048], P('ens', None, None, 'space'), may hold values from -6 to 6
- section_index: int32 [32], P('ens'), may hold values from 0 to 1
- targets: bfloat16 [32, 256, 2048], P('ens', 'space'), may hold values from -6 to 6
- sea_mask: int32 [256, 2048], P('space'), may hold values 0 or 1
- basis_rows: bfloat16 [256, 1024], P('space'), may hold values from -0.25 to 0.25
- basis_cols: bfloat16 [2048, 1024], replicated, may hold values from -0.1875 to 0.1875
- control: float32 [1024, 1024], P('space'), may hold values from -6 to 6
Outputs:
- control_next: float32 [1024, 1024], P('space')
Inputs may be any that keep to these rules, and one draw needn't show every extreme that they name: `section_index`: selects one of the 2 slots.
All inputs are finite; a program needn't handle non-finite values. No bound on the sum of `sea_mask` on one device may be relied on, other than what follows from the above.
Results may differ from a plain program's by a relative error of at most 0.0014.
The roundings to bfloat16 on the way count: a program that leaves them out, or rounds other values in their place, can miss the bound.
Values may be sent and summed in bfloat16 or wider, within the bound.
No kernel may reach another device: no remote copies, remote signals or barrier semaphores. Data moves between devices by JAX's collectives and lax.ppermute only.
A program may use at most 128 MiB of HBM per device.

v0:
```python
import jax
import jax.numpy as jnp
from jax import lax
from jax.experimental import pallas as pl
from jax.experimental.pallas import tpu as pltpu
from jax.sharding import PartitionSpec as P


DEPTH = 1.0
GRAVITY = 1.0
CORIOLIS = 0.5
FRICTION = 0.1
TIME_STEP = 0.3
STEP_SIZE = 1.0
EPSILON = 1e-06

F32 = jnp.float32
BF16 = jnp.bfloat16
TILE = 8
LANES = 128
MIB = 1 << 20


VMEM = pl.BlockSpec(memory_space=pltpu.VMEM)
SMEM = pl.BlockSpec(memory_space=pltpu.SMEM)
HBM = pl.BlockSpec(memory_space=pltpu.HBM)


def limit(mib):
    return pltpu.CompilerParams(vmem_limit_bytes=mib * MIB)


def tile_rows(shape):
    return lax.broadcasted_iota(jnp.int32, shape, 0)


def shift_cols(field, step):
    count = field.shape[1]
    turned = pltpu.roll(field, (-step) % count, 1)
    lane = lax.broadcasted_iota(jnp.int32, (field.shape[0], LANES), 1)
    if step > 0:
        edge = jnp.where(lane >= LANES - step, 0.0, turned[:, count - LANES :])
        return jnp.concatenate([turned[:, : count - LANES], edge], axis=1)
    edge = jnp.where(lane < -step, 0.0, turned[:, :LANES])
    return jnp.concatenate([edge, turned[:, LANES:]], axis=1)


def shift_rows(field, step):
    return pltpu.roll(field, (-step) % field.shape[0], 0)


def dx(field):
    return shift_cols(field, 1) - shift_cols(field, -1)


def dy(field):
    return shift_rows(field, 1) - shift_rows(field, -1)


def pack(index_ref, member_ref, states_ref, targets_ref, sea_ref, basis_ref, control_ref, up_ref, down_ref, out_ref, rows_ref, last, first, seen, sea, basis, own, sems):
    count, _, _, rows, cols = states_ref.shape
    width = basis_ref.shape[1]
    rows_out = control_ref.shape[0]
    quarter = out_ref.shape[2]
    at = pl.multiple_of(member_ref[0] * quarter, quarter)

    def fetch(source, target, sem):
        copy = pltpu.make_async_copy(source, target, sem)
        copy.start()
        return copy

    states = []
    for s in range(count):
        slot = index_ref[s]
        for side, (buffer, row) in enumerate(((last, rows - TILE), (first, 0))):
            source = states_ref.at[s, slot, :, pl.ds(row, TILE), :]
            states.append(fetch(source, buffer.at[s], sems.at[side, s]))
    others = [
        fetch(targets_ref.at[:, pl.ds(rows - TILE, TILE), :], seen.at[0], sems.at[0, count]),
        fetch(targets_ref.at[:, pl.ds(0, TILE), :], seen.at[1], sems.at[1, count]),
        fetch(sea_ref.at[pl.ds(rows - TILE, TILE), :], sea.at[0], sems.at[0, count + 1]),
        fetch(sea_ref.at[pl.ds(0, TILE), :], sea.at[1], sems.at[1, count + 1]),
        fetch(basis_ref, basis, sems.at[0, count + 2]),
        fetch(control_ref.at[:, pl.ds(at, quarter)], own, sems.at[1, count + 2]),
    ]
    row = tile_rows((TILE, cols))
    for s in range(count):
        states[2 * s].wait()
        height, east, north = (last[s, f].astype(F32) for f in range(3))
        up_ref[s] = jnp.where(
            row >= 5, height, jnp.where(row >= 2, pltpu.roll(north, 5, 0), pltpu.roll(east, 2, 0))
        ).astype(BF16)
        states[2 * s + 1].wait()
        height, east, north = (first[s, f].astype(F32) for f in range(3))
        down_ref[s] = jnp.where(
            row < 3, height, jnp.where(row < 6, pltpu.roll(north, 3, 0), pltpu.roll(east, 6, 0))
        ).astype(BF16)
    for copy in others:
        copy.wait()
    targets_up = jnp.zeros((TILE, cols), F32)
    targets_down = jnp.zeros((TILE, cols), F32)
    for s in range(count):
        targets_up = jnp.where(row == s, seen[0, s].astype(F32)[TILE - 1 :, :], targets_up)
        targets_down = jnp.where(row == s, seen[1, s].astype(F32)[:1, :], targets_down)
    up_ref[count] = targets_up.astype(BF16)
    down_ref[count] = targets_down.astype(BF16)
    basis_last = pltpu.roll(basis[rows - TILE :, :].astype(F32), 4, 0)
    basis_first = pltpu.roll(basis[:TILE, :].astype(F32), 2, 0)
    rest = jnp.zeros((TILE, cols - width), F32)
    up_ref[count + 1] = jnp.where(
        row >= 6, sea[0].astype(F32), jnp.concatenate([basis_last, rest], axis=1)
    ).astype(BF16)
    down_ref[count + 1] = jnp.where(
        row < 2, sea[1].astype(F32), jnp.concatenate([basis_first, rest], axis=1)
    ).astype(BF16)
    part = own[...].astype(BF16)
    part_basis = basis[:, pl.ds(at, quarter)]
    rows_ref[...] = basis[...]
    for k in range(out_ref.shape[0]):
        out_ref[k, :rows_out] = part
        out_ref[k, rows_out:] = part_basis


def packed(section_index, member, checkpoints, targets, sea_mask, basis_rows, control, slabs, quarter):
    count, _, fields, rows, cols = checkpoints.shape
    rows_out, width = control.shape
    edges = jax.ShapeDtypeStruct((count + 2, TILE, cols), BF16)
    return pl.pallas_call(
        pack,
        name="pack",
        out_shape=(
            edges,
            edges,
            jax.ShapeDtypeStruct((slabs, rows_out + rows, quarter), BF16),
            jax.ShapeDtypeStruct((rows, width), BF16),
        ),
        in_specs=[SMEM, SMEM] + [HBM] * 5,
        out_specs=(VMEM, VMEM, VMEM, VMEM),
        scratch_shapes=[
            pltpu.VMEM((count, fields, TILE, cols), BF16),
            pltpu.VMEM((count, fields, TILE, cols), BF16),
            pltpu.VMEM((2, count, TILE, cols), BF16),
            pltpu.VMEM((2, TILE, cols), jnp.int32),
            pltpu.VMEM((rows, width), BF16),
            pltpu.VMEM((rows_out, quarter), F32),
            pltpu.SemaphoreType.DMA((2, count + 3)),
        ],
        compiler_params=limit(14),
    )(
        section_index,
        member.reshape(1),
        *map(in_hbm, (checkpoints, targets, sea_mask, basis_rows, control)),
    )


def hold(source_ref, out_ref, sem):
    copy = pltpu.make_async_copy(source_ref, out_ref, sem)
    copy.start()
    copy.wait()


def in_hbm(array):
    return pltpu.with_memory_space_constraint(array, pltpu.HBM)


def held(array):
    size = array.size * array.dtype.itemsize
    return pl.pallas_call(
        hold,
        name="hold",
        out_shape=jax.ShapeDtypeStruct(array.shape, array.dtype),
        in_specs=[HBM],
        out_specs=VMEM,
        scratch_shapes=[pltpu.SemaphoreType.DMA],
        compiler_params=limit(size // MIB + 2),
    )(in_hbm(array))


def run_states(index_ref, state_ref, before_ref, after_ref, seen_before_ref, seen_after_ref, targets_ref, sea_ref, base_ref, pairs_ref, out_mask_ref, mask_ref, gx, gy, seen_edge):
    s = pl.program_id(0)
    _, cols = sea_ref.shape
    row = tile_rows((TILE, cols))

    @pl.when(s == 0)
    def _():
        edge = jnp.where(
            row < 2,
            seen_after_ref[1].astype(F32),
            jnp.where(row >= 6, seen_before_ref[1].astype(F32), 0.0),
        )
        mask_ref[...] = jnp.concatenate([sea_ref[...].astype(F32), edge], axis=0)
        out_mask_ref[...] = mask_ref[...].astype(BF16)
        seen_edge[0] = seen_before_ref[0].astype(F32)
        seen_edge[1] = seen_after_ref[0].astype(F32)
        gx[...] = jnp.zeros_like(gx)
        gy[...] = jnp.zeros_like(gy)
        pairs_ref[...] = jnp.zeros_like(pairs_ref)

    mask = mask_ref[...]
    before = before_ref[0].astype(F32)
    after = after_ref[0].astype(F32)
    top = row < 4

    def extended(field, forward, back):
        edge = jnp.where(top, pltpu.roll(after, forward, 0), pltpu.roll(before, back, 0))
        return jnp.concatenate([state_ref[0, 0, field].astype(F32), edge], axis=0)

    height = jnp.concatenate(
        [state_ref[0, 0, 0].astype(F32), jnp.where(top, after, before)], axis=0
    )
    east = extended(1, 2, 6)
    north = extended(2, 5, 3)
    seen = jnp.concatenate(
        [
            targets_ref[0].astype(F32),
            jnp.where(top, seen_edge[1, pl.ds(s, 1), :], seen_edge[0, pl.ds(s, 1), :]),
        ],
        axis=0,
    )
    half = 0.5 * TIME_STEP
    keep = 1.0 - TIME_STEP * FRICTION
    deep = DEPTH + height
    height_mid = mask * (height - half * (dx(deep * east) + dy(deep * north)))
    east_mid = mask * (
        keep * east + TIME_STEP * CORIOLIS * north - half * GRAVITY * dx(height)
    )
    north_mid = mask * (
        keep * north - TIME_STEP * CORIOLIS * east - half * GRAVITY * dy(height)
    )
    deep = DEPTH + height_mid
    height_end = 0.5 * (height + height_mid) - 0.5 * half * (
        dx(deep * east_mid) + dy(deep * north_mid)
    )
    misfit = mask * (height_end - seen)
    weight = mask * deep
    gx[...] += weight * dx(misfit)
    gy[...] += weight * dy(misfit)
    beside = shift_cols(weight, 1)
    pairs_ref[0] += weight * weight
    pairs_ref[1] += weight * shift_cols(weight, 2)
    pairs_ref[2] += weight * shift_rows(weight, 2)
    pairs_ref[3] += weight * shift_rows(beside, 1)
    pairs_ref[4] += weight * shift_rows(beside, -1)

    @pl.when(s == pl.num_programs(0) - 1)
    def _():
        scale = 0.125 * TIME_STEP * TIME_STEP
        base_ref[...] = scale * (dy(gx[...]) - dx(gy[...]))


def states_pass(section_index, checkpoints, before, after, targets, sea_mask):
    count, _, fields, rows, cols = checkpoints.shape
    ring = rows + TILE
    field = jax.ShapeDtypeStruct((ring, cols), F32)
    edge = pl.BlockSpec((1, TILE, cols), lambda s, index: (s, 0, 0))
    shared = pl.BlockSpec((2, TILE, cols), lambda s, index: (count // 2, 0, 0))
    return pl.pallas_call(
        run_states,
        name="run_states",
        out_shape=(
            field,
            jax.ShapeDtypeStruct((5, ring, cols), F32),
            jax.ShapeDtypeStruct((ring, cols), BF16),
        ),
        grid_spec=pltpu.PrefetchScalarGridSpec(
            num_scalar_prefetch=1,
            grid=(count,),
            in_specs=[
                pl.BlockSpec((1, 1, fields, rows, cols), lambda s, index: (s, index[s], 0, 0, 0)),
                edge,
                edge,
                shared,
                shared,
                pl.BlockSpec((1, rows, cols), lambda s, index: (s, 0, 0)),
                pl.BlockSpec((rows, cols), lambda s, index: (0, 0)),
            ],
            out_specs=(
                pl.BlockSpec((ring, cols), lambda s, index: (0, 0)),
                pl.BlockSpec((5, ring, cols), lambda s, index: (0, 0, 0)),
                pl.BlockSpec((ring, cols), lambda s, index: (0, 0)),
            ),
            scratch_shapes=[
                pltpu.VMEM((ring, cols), F32),
                pltpu.VMEM((ring, cols), F32),
                pltpu.VMEM((ring, cols), F32),
                pltpu.VMEM((2, TILE, cols), F32),
            ],
        ),
        compiler_params=limit(32),
    )(
        section_index,
        in_hbm(checkpoints),
        before,
        after,
        before,
        after,
        in_hbm(targets),
        sea_mask,
    )


def make_coeffs(basis_ref, before_ref, after_ref, pieces_ref, out_ref):
    slabs, _, quarter = pieces_ref.shape
    _, width = basis_ref.shape
    rows_out = width // slabs
    row = tile_rows((TILE, width))
    after = pltpu.roll(after_ref[0, :, :width].astype(F32), 6, 0)
    before = pltpu.roll(before_ref[0, :, :width].astype(F32), 4, 0)
    edge = jnp.where(row < 2, after, jnp.where(row >= 6, before, 0.0))
    basis = jnp.concatenate([basis_ref[...].astype(F32), edge], axis=0).astype(BF16)
    part = pieces_ref[:, :rows_out, :].reshape(slabs * rows_out, quarter)
    out_ref[...] = jnp.dot(basis, part, preferred_element_type=F32).astype(BF16)


def coeffs_part(basis_rows, before, after, pieces):
    rows, width = basis_rows.shape
    last = before.shape[0] - 1
    edge = pl.BlockSpec((1, TILE, before.shape[2]), lambda i: (last, 0, 0))
    return pl.pallas_call(
        make_coeffs,
        name="make_coeffs",
        out_shape=jax.ShapeDtypeStruct((rows + TILE, pieces.shape[2]), BF16),
        grid=(1,),
        in_specs=[
            pl.BlockSpec((rows, width), lambda i: (0, 0)),
            edge,
            edge,
            pl.BlockSpec(pieces.shape, lambda i: (0, 0, 0)),
        ],
        out_specs=pl.BlockSpec((rows + TILE, pieces.shape[2]), lambda i: (0, 0)),
        compiler_params=limit(12),
    )(basis_rows, before, after, pieces)


def apply_potential(member_ref, own_ref, near_ref, far_ref, both_ref, cols_ref, base_ref, pairs_ref, mask_ref, keep_ref, give_ref, coeffs, total, held_cols, field, sems):
    member = member_ref[0]
    blocks = held_cols.shape[0]
    block = held_cols.shape[1]
    copies = []
    for k in range(blocks):
        copy = pltpu.make_async_copy(
            cols_ref.at[pl.ds(k * block, block), :], held_cols.at[k], sems.at[k]
        )
        copy.start()
        copies.append(copy)
    quarter = own_ref.shape[1]
    for bits, ref in enumerate((own_ref, near_ref, far_ref, both_ref)):
        at = pl.multiple_of((member ^ bits) * quarter, quarter)
        coeffs[:, pl.ds(at, quarter)] = ref[...]
    for k, copy in enumerate(copies):
        copy.wait()
        field[:, k * block : (k + 1) * block] = lax.dot_general(
            coeffs[...], held_cols[k], (((1,), (1,)), ((), ())), preferred_element_type=F32
        )
    potential = field[...]
    sx = -dy(potential)
    sy = dx(potential)
    mask = mask_ref[...].astype(F32)
    same, two_x, two_y, up, down = (pairs_ref[k] for k in range(5))
    same_x = same * sx
    same_y = same * sy
    up_x = up * shift_rows(shift_cols(sx, 1), 1)
    up_y = up * shift_rows(shift_cols(sy, 1), 1)
    down_x = down * shift_rows(shift_cols(sx, 1), -1)
    down_y = down * shift_rows(shift_cols(sy, 1), -1)
    back_up_x = shift_rows(shift_cols(up * sx, -1), -1)
    back_up_y = shift_rows(shift_cols(up * sy, -1), -1)
    back_down_x = shift_rows(shift_cols(down * sx, -1), 1)
    back_down_y = shift_rows(shift_cols(down * sy, -1), 1)
    gx = shift_cols(mask, 1) * (
        two_x * shift_cols(sx, 2) - same_x + up_y - down_y
    ) - shift_cols(mask, -1) * (same_x - shift_cols(two_x * sx, -2) + back_down_y - back_up_y)
    gy = shift_rows(mask, 1) * (
        up_x - back_down_x + two_y * shift_rows(sy, 2) - same_y
    ) - shift_rows(mask, -1) * (down_x - back_up_x + same_y - shift_rows(two_y * sy, -2))
    scale = -(TIME_STEP**4) / 64.0
    grad = base_ref[...] + scale * (dy(gx) - dx(gy))
    pair = keep_ref.shape[0]
    total[...] = grad[: 2 * pair]
    core = member % 2
    keep_ref[...] = total[pl.ds(pl.multiple_of(core * pair, pair), pair), :]
    give_ref[...] = total[pl.ds(pl.multiple_of((1 - core) * pair, pair), pair), :]


def gradient_halves(member, parts, basis_cols, base, pairs, mask):
    ring, cols = base.shape
    width = basis_cols.shape[1]
    pair = (ring - TILE) // 2
    half = jax.ShapeDtypeStruct((pair, cols), F32)
    return pl.pallas_call(
        apply_potential,
        name="apply_potential",
        out_shape=(half, half),
        in_specs=[SMEM] + [VMEM] * 4 + [HBM] + [VMEM] * 3,
        out_specs=(VMEM, VMEM),
        scratch_shapes=[
            pltpu.VMEM((ring, width), BF16),
            pltpu.VMEM((2 * pair, cols), F32),
            pltpu.VMEM((4, cols // 4, width), BF16),
            pltpu.VMEM((ring, cols), F32),
            pltpu.SemaphoreType.DMA((4,)),
        ],
        compiler_params=limit(24),
    )(member.reshape(1), *parts, in_hbm(basis_cols), base, pairs, mask)


def project(own_ref, other_ref, cols_ref, out_ref):
    total = (own_ref[...] + other_ref[...]).astype(BF16)
    projected = jnp.dot(total, cols_ref[...], preferred_element_type=F32).astype(BF16)
    half = out_ref.shape[3]
    for core in range(2):
        part = projected[:, core * half : (core + 1) * half]
        for chip in range(out_ref.shape[0] // 2):
            for k in range(out_ref.shape[1]):
                out_ref[2 * chip + core, k] = part


def projected_pieces(own, other, basis_cols, members, slabs):
    single = own.shape[0]
    half = basis_cols.shape[1] // 2
    return pl.pallas_call(
        project,
        name="project",
        out_shape=jax.ShapeDtypeStruct((members, slabs, single, half), BF16),
        in_specs=[VMEM] * 3,
        out_specs=VMEM,
        compiler_params=limit(16),
    )(own, other, basis_cols)


def assemble(member_ref, own_ref, far_ref, near_ref, control_ref, basis_ref, kept_ref, sem):
    copy = pltpu.make_async_copy(control_ref, kept_ref, sem)
    copy.start()
    member = member_ref[0]
    quarter = own_ref.shape[1]
    parts = (own_ref[...], near_ref[0], far_ref[...], near_ref[1])
    for bits, part in enumerate(parts):
        at = pl.multiple_of((member ^ bits) * quarter, quarter)
        basis_ref[pl.ds(at, quarter), :] = part.astype(F32).T.astype(BF16)
    copy.wait()


def assembled(member, own, far, near, control):
    rows, _ = own.shape
    width = control.shape[1]
    return pl.pallas_call(
        assemble,
        name="assemble",
        out_shape=(
            jax.ShapeDtypeStruct((width, rows), BF16),
            jax.ShapeDtypeStruct(control.shape, F32),
        ),
        in_specs=[SMEM, VMEM, VMEM, VMEM, HBM],
        out_specs=(VMEM, VMEM),
        scratch_shapes=[pltpu.SemaphoreType.DMA],
        compiler_params=limit(24),
    )(member.reshape(1), own, far, near, in_hbm(control))


def gradient(slab_ref, basis_ref, projected_ref, out_ref):
    rows_out = out_ref.shape[0] - TILE
    width = basis_ref.shape[0]
    half = out_ref.shape[1]
    projected = projected_ref[...]
    block = width // 4
    squares = jnp.zeros((TILE, half), F32)
    for k in range(4):
        part = jnp.dot(
            basis_ref[k * block : (k + 1) * block, :], projected, preferred_element_type=F32
        )
        squares += jnp.sum((part * part).reshape(block // TILE, TILE, half), axis=0)
    at = pl.multiple_of(slab_ref[0] * rows_out, rows_out)
    out_ref[:rows_out] = jnp.dot(
        basis_ref[pl.ds(at, rows_out), :], projected, preferred_element_type=F32
    )
    out_ref[rows_out:] = squares


def gradient_block(slab, basis, projected, rows_out):
    half = projected.shape[1]
    return pl.pallas_call(
        gradient,
        name="gradient",
        out_shape=jax.ShapeDtypeStruct((rows_out + TILE, half), F32),
        in_specs=[SMEM, VMEM, VMEM],
        out_specs=VMEM,
        compiler_params=limit(24),
    )(slab.reshape(1), basis, projected)


def update(core_ref, control_ref, own_ref, other_ref, out_ref):
    rows_out, width = control_ref.shape
    half = width // 2
    total = jnp.sum(own_ref[rows_out:] + other_ref[rows_out:])
    scale = STEP_SIZE * lax.rsqrt(total / (width * width) + EPSILON)
    for turn, ref in enumerate((own_ref, other_ref)):
        at = pl.multiple_of((core_ref[0] ^ turn) * half, half)
        out_ref[:, pl.ds(at, half)] = control_ref[:, pl.ds(at, half)] - ref[:rows_out] * scale


def updated(core, control, own, other):
    return pl.pallas_call(
        update,
        name="update",
        out_shape=jax.ShapeDtypeStruct(control.shape, F32),
        in_specs=[SMEM, VMEM, VMEM, VMEM],
        out_specs=VMEM,
        compiler_params=limit(8),
    )(core.reshape(1), control, own, other)


def partner(value, bit):
    count = lax.axis_size("ens")
    return lax.ppermute(value, "ens", [(i, i ^ bit) for i in range(count)])


def on_device(checkpoints, section_index, targets, sea_mask, basis_rows, basis_cols, control):
    members = lax.axis_size("ens")
    slabs = lax.axis_size("space")
    member = lax.axis_index("ens").astype(jnp.int32)
    slab = lax.axis_index("space").astype(jnp.int32)
    core = member & 1
    chip = member >> 1
    rows_out, width = control.shape
    rows = basis_rows.shape[0]
    quarter = width // members
    half = width // 2
    single = rows // 4

    up, down, pieces, near_rows = packed(
        section_index, member, checkpoints, targets, sea_mask, basis_rows, control, slabs, quarter
    )
    before = lax.ppermute(up, "space", [(i, i + 1) for i in range(slabs - 1)])
    after = lax.ppermute(down, "space", [(i + 1, i) for i in range(slabs - 1)])
    pieces = lax.all_to_all(pieces, "space", 0, 0)
    base, pairs, mask = states_pass(section_index, checkpoints, before, after, targets, sea_mask)
    own = coeffs_part(near_rows, before, after, pieces)
    parts = [own] + [partner(own, bits) for bits in (1, 2, 3)]
    keep, give = gradient_halves(member, parts, basis_cols, base, pairs, mask)

    keep = keep + partner(give, 1)
    own_rows = lax.dynamic_slice_in_dim(keep, chip * single, single, 0)
    give = lax.dynamic_slice_in_dim(keep, (1 - chip) * single, single, 0)
    arriving = partner(give, 2)
    cols = held(basis_cols)
    send = projected_pieces(own_rows, arriving, cols, members, slabs)
    got = lax.all_to_all(send.reshape(members * slabs, single, half), ("ens", "space"), 0, 0)
    projected_half = got.reshape(slabs * rows, half)

    part = pieces[:, rows_out:, :].reshape(slabs, 2, members // 2, single, quarter)
    part = part.transpose(2, 1, 0, 3, 4).reshape(slabs * rows, quarter)
    far = partner(part, 2)
    near = partner(jnp.stack([part, far]), 1)
    basis, kept = assembled(member, part, far, near, control)
    block = gradient_block(slab, basis, projected_half, rows_out)
    other = partner(block, 1)
    return updated(core, kept, block, other)


def solution(mesh):
    return jax.shard_map(
        on_device,
        mesh=mesh,
        in_specs=(
            P("ens", None, None, "space", None),
            P("ens"),
            P("ens", "space", None),
            P("space", None),
            P("space", None),
            P(),
            P("space", None),
        ),
        out_specs=P("space", None),
        check_vma=False,
    )
```

profile of v0, /device:TPU:0, one launch (start us, length us, event | category | flops | bytes accessed | tf_op | source)
XLA Modules:
  0.0 81.3 jit_solution(17566271621817183306)
XLA Ops:
  0.0 0.7 copy-done.1
  0.7 3.4 %pack.1 = (bf16[10,8,2048]{2,1,0:T(8,128)(2,1)S(1)}, bf16[10,8,2048]{2,1,0:T(8,128)(2,1)S(1)}, bf16[8,160,256]{2,1,0:T(8,128)(2,1)}, bf16[32,1024]{1,0:T(8,128)(2,1)S(1)}) custom-call(s32[8]{0:T(128)S(1)} %copy-done.1, s32[1]{0:T(128)} %bitcast.1.member_ref, bf16[8,2,3,32,2048]{4,3,2,1,0:T(8,128)(2,1)} %state_ref.1, bf16[8,32,2048]{2,1,0:T(8,128)(2,1)} %targets_ref.3, ...), custom_call_target="tpu_custom_call" | custom-call | tf_op jit(solution)/shard_map/pack/pallas_call | solution.py:128
  4.0 7.3 %all-to-all-start = ((bf16[8,160,256]{2,1,0:T(8,128)(2,1)}), bf16[8,160,256]{2,1,0:T(8,128)(2,1)S(1)}, u32[]{:S(2)}, u32[]{:S(2)}) async-start(bf16[8,160,256]{2,1,0:T(8,128)(2,1)} %get-tuple-element.16), calls=%async_computation | async-start | bytes 1310720 | tf_op jit(solution)/shard_map/all_to_all | solution.py:535
  11.4 3.9 %collective-permute-start.2 = (bf16[10,8,2048]{2,1,0:T(8,128)(2,1)S(1)}, bf16[10,8,2048]{2,1,0:T(8,128)(2,1)S(1)}, u32[]{:S(2)}, u32[]{:S(2)}) collective-permute-start(bf16[10,8,2048]{2,1,0:T(8,128)(2,1)S(1)} %get-tuple-element.20), channel_id=1, source_target_pairs={{0,1},{1,2},{2,3},{3,4},{4,5},{5,6},{6,7},{8,9},{9,10},{10,11},{11... | collective-permute-start | bytes 983048 | tf_op jit(solution)/shard_map/ppermute | solution.py:533
  15.3 1.3 %collective-permute-start.3 = (bf16[10,8,2048]{2,1,0:T(8,128)(2,1)S(1)}, bf16[10,8,2048]{2,1,0:T(8,128)(2,1)S(1)}, u32[]{:S(2)}, u32[]{:S(2)}) collective-permute-start(bf16[10,8,2048]{2,1,0:T(8,128)(2,1)S(1)} %get-tuple-element.21), channel_id=1, source_target_pairs={{1,0},{2,1},{3,2},{4,3},{5,4},{6,5},{7,6},{9,8},{10,9},{11,10},{12... | collective-permute-start | bytes 983048 | tf_op jit(solution)/shard_map/ppermute | solution.py:534
  16.6 16.2 %collective-permute-done.2.before_ref.seen_before_ref = bf16[10,8,2048]{2,1,0:T(8,128)(2,1)S(1)} collective-permute-done((bf16[10,8,2048]{2,1,0:T(8,128)(2,1)S(1)}, bf16[10,8,2048]{2,1,0:T(8,128)(2,1)S(1)}, u32[]{:S(2)}, u32[]{:S(2)}) %collective-permute-start.2) | collective-permute-done | bytes 327712 | tf_op jit(solution)/shard_map/ppermute | solution.py:533
  32.8 0.0 collective-permute-done.3.after_ref.seen_after_ref
  32.8 0.0 all-to-all-done.pieces_ref
  32.8 0.2 make_coeffs.1.own_ref
  33.1 0.1 collective-permute-start.4
  33.1 1.6 %collective-permute-start.5 = (bf16[40,256]{1,0:T(8,128)(2,1)S(1)}, bf16[40,256]{1,0:T(8,128)(2,1)S(1)}, u32[]{:S(2)}, u32[]{:S(2)}) collective-permute-start(bf16[40,256]{1,0:T(8,128)(2,1)S(1)} %make_coeffs.1.own_ref), channel_id=1, source_target_pairs={{0,16},{8,24},{16,0},{24,8},{1,17},{9,25},{17,1},{25,9},{2,18},{10... | collective-permute-start | bytes 61448 | tf_op jit(solution)/shard_map/ppermute | solution.py:514
  34.7 0.3 collective-permute-start.6
  35.0 12.9 %run_states.1 = (f32[40,2048]{1,0:T(8,128)S(1)}, f32[5,40,2048]{2,1,0:T(8,128)S(1)}, bf16[40,2048]{1,0:T(8,128)(2,1)S(1)}) custom-call(s32[8]{0:T(128)S(1)} %copy-done.2, bf16[8,2,3,32,2048]{4,3,2,1,0:T(8,128)(2,1)} %state_ref.1, bf16[10,8,2048]{2,1,0:T(8,128)(2,1)S(1)} %collective-permute-done.2.before_ref.seen_before_ref, ...), custom_call_target="tpu_custom_call" | custom-call | tf_op jit(solution)/shard_map/run_states/pallas_call | solution.py:257
  47.9 0.0 collective-permute-done.5.far_ref
  47.9 0.0 collective-permute-done.6.both_ref
  47.9 4.2 %apply_potential.1 = (f32[16,2048]{1,0:T(8,128)S(1)}, f32[16,2048]{1,0:T(8,128)S(1)}) custom-call(s32[1]{0:T(128)} %bitcast.1.member_ref, bf16[40,256]{1,0:T(8,128)(2,1)S(1)} %make_coeffs.1.own_ref, bf16[40,256]{1,0:T(8,128)(2,1)S(1)} %collective-permute-done.4.near_ref, bf16[40,256]{1,0:T(8,128)(2,1)S(1)} %collective-permute-done.5.far_ref, ...), custom_call_target="tpu_custom_call" | custom-call | tf_op jit(solution)/shard_map/apply_potential/pallas_call | solution.py:390
  52.2 0.4 collective-permute-start.7
  52.6 1.0 %collective-permute-done.7 = f32[16,2048]{1,0:T(8,128)S(1)} collective-permute-done((f32[16,2048]{1,0:T(8,128)S(1)}, f32[16,2048]{1,0:T(8,128)S(1)}, u32[]{:S(2)}, u32[]{:S(2)}) %collective-permute-start.7) | collective-permute-done | bytes 131104 | tf_op jit(solution)/shard_map/ppermute | solution.py:514
  53.6 1.6 %collective-permute-start.8 = (f32[8,2048]{1,0:T(8,128)S(1)}, f32[8,2048]{1,0:T(8,128)S(1)}, u32[]{:S(2)}, u32[]{:S(2)}) collective-permute-start(f32[8,2048]{1,0:T(8,128)S(1)} %get-tuple-element.27), channel_id=1, source_target_pairs={{0,16},{8,24},{16,0},{24,8},{1,17},{9,25},{17,1},{25,9},{2,18},{10... | collective-permute-start | bytes 196616 | tf_op jit(solution)/shard_map/ppermute | solution.py:514
  55.2 0.6 collective-permute-start
  55.8 2.2 %hold.1.cols_ref = bf16[2048,1024]{1,0:T(8,128)(2,1)S(1)} custom-call(bf16[2048,1024]{1,0:T(8,128)(2,1)} %source_ref.1), custom_call_target="tpu_custom_call" | custom-call | tf_op jit(solution)/shard_map/hold/pallas_call | solution.py:168
  58.0 0.1 collective-permute-done.8.other_ref
  58.1 1.4 %project.1 = bf16[4,8,8,512]{3,2,1,0:T(8,128)(2,1)} custom-call(f32[8,2048]{1,0:T(8,128)S(1)} %get-tuple-element.28.own_ref, f32[8,2048]{1,0:T(8,128)S(1)} %collective-permute-done.8.other_ref, bf16[2048,1024]{1,0:T(8,128)(2,1)S(1)} %hold.1.cols_ref), custom_call_target="tpu_custom_call" | custom-call | tf_op jit(solution)/shard_map/project/pallas_call | solution.py:421
  59.5 8.3 %all-to-all-start.1 = ((bf16[32,8,512]{2,1,0:T(8,128)(2,1)}), bf16[32,8,512]{2,1,0:T(8,128)(2,1)S(1)}, u32[]{:S(2)}, u32[]{:S(2)}) async-start(bf16[32,8,512]{2,1,0:T(8,128)(2,1)} %bitcast.8), calls=%async_computation.1 | async-start | bytes 524288 | tf_op jit(solution)/shard_map/all_to_all | solution.py:547
  67.8 0.3 collective-permute-start.1
  68.2 1.3 %collective-permute-done.1.near_ref = bf16[2,256,256]{2,1,0:T(8,128)(2,1)S(1)} collective-permute-done((bf16[2,256,256]{2,1,0:T(8,128)(2,1)S(1)}, bf16[2,256,256]{2,1,0:T(8,128)(2,1)S(1)}, u32[]{:S(2)}, u32[]{:S(2)}) %collective-permute-start.1) | collective-permute-done | bytes 262176 | tf_op jit(solution)/shard_map/ppermute | solution.py:514
  69.4 1.1 %assemble.1 = (bf16[1024,256]{1,0:T(8,128)(2,1)S(1)}, f32[128,1024]{1,0:T(8,128)S(1)}) custom-call(s32[1]{0:T(128)} %bitcast.1.member_ref, bf16[256,256]{1,0:T(8,128)(2,1)S(1)} %bitcast.13, bf16[256,256]{1,0:T(8,128)(2,1)S(1)} %collective-permute-done.far_ref, bf16[2,256,256]{2,1,0:T(8,128)(2,1)S(1)} %collective-permute-done.1.near_ref, f32[128,1024]{1,0:T(8,128)} %control_ref.3), custom_call_target="tpu_custom_call" | custom-call | tf_op jit(solution)/shard_map/assemble/pallas_call | solution.py:446
  70.5 7.7 %all-to-all-done.1 = bf16[32,8,512]{2,1,0:T(8,128)(2,1)S(1)} async-done(((bf16[32,8,512]{2,1,0:T(8,128)(2,1)}), bf16[32,8,512]{2,1,0:T(8,128)(2,1)S(1)}, u32[]{:S(2)}, u32[]{:S(2)}) %all-to-all-start.1) | async-done | bytes 262176 | tf_op jit(solution)/shard_map/all_to_all | solution.py:547
  78.2 0.5 gradient.1.own_ref
  78.7 0.1 collective-permute-start.9
  78.8 1.5 %collective-permute-done.9.other_ref = f32[136,512]{1,0:T(8,128)S(1)} collective-permute-done((f32[136,512]{1,0:T(8,128)S(1)}, f32[136,512]{1,0:T(8,128)S(1)}, u32[]{:S(2)}, u32[]{:S(2)}) %collective-permute-start.9) | collective-permute-done | bytes 278560 | tf_op jit(solution)/shard_map/ppermute | solution.py:514
  80.3 1.0 %update.1 = f32[128,1024]{1,0:T(8,128)} custom-call(s32[1]{0:T(128)} %bitcast.core_ref, f32[128,1024]{1,0:T(8,128)S(1)} %get-tuple-element.17.control_ref, f32[136,512]{1,0:T(8,128)S(1)} %gradient.1.own_ref, f32[136,512]{1,0:T(8,128)S(1)} %collective-permute-done.9.other_ref), custom_call_target="tpu_custom_call" | custom-call | tf_op jit(solution)/shard_map/update/pallas_call | solution.py:502
  (12 shorter events, 0.1 us)
Async XLA Ops:
  0.0 0.7 copy-start.1
  0.7 34.3 %copy-start = (s32[32,2048]{1,0:T(8,128)S(1)}, s32[32,2048]{1,0:T(8,128)}, u32[]{:S(2)}) copy-start(s32[32,2048]{1,0:T(8,128)} %sea_ref.3) | copy-start | bytes 786436
  0.7 34.3 %copy-start.2 = (s32[8]{0:T(128)S(1)}, s32[8]{0:T(128)}, u32[]{:S(2)}) copy-start(s32[8]{0:T(128)} %index_ref.3) | copy-start | bytes 100
  4.0 28.8 %all-to-all-start = ((bf16[8,160,256]{2,1,0:T(8,128)(2,1)}), bf16[8,160,256]{2,1,0:T(8,128)(2,1)S(1)}, u32[]{:S(2)}, u32[]{:S(2)}) async-start(bf16[8,160,256]{2,1,0:T(8,128)(2,1)} %get-tuple-element.16), calls=%async_computation | async-start | bytes 1310720 | tf_op jit(solution)/shard_map/all_to_all | solution.py:535
  11.4 21.5 %collective-permute-start.2 = (bf16[10,8,2048]{2,1,0:T(8,128)(2,1)S(1)}, bf16[10,8,2048]{2,1,0:T(8,128)(2,1)S(1)}, u32[]{:S(2)}, u32[]{:S(2)}) collective-permute-start(bf16[10,8,2048]{2,1,0:T(8,128)(2,1)S(1)} %get-tuple-element.20), channel_id=1, source_target_pairs={{0,1},{1,2},{2,3},{3,4},{4,5},{5,6},{6,7},{8,9},{9,10},{10,11},{11... | collective-permute-start | bytes 983048 | tf_op jit(solution)/shard_map/ppermute | solution.py:533
  15.3 17.5 %collective-permute-start.3 = (bf16[10,8,2048]{2,1,0:T(8,128)(2,1)S(1)}, bf16[10,8,2048]{2,1,0:T(8,128)(2,1)S(1)}, u32[]{:S(2)}, u32[]{:S(2)}) collective-permute-start(bf16[10,8,2048]{2,1,0:T(8,128)(2,1)S(1)} %get-tuple-element.21), channel_id=1, source_target_pairs={{1,0},{2,1},{3,2},{4,3},{5,4},{6,5},{7,6},{9,8},{10,9},{11,10},{12... | collective-permute-start | bytes 983048 | tf_op jit(solution)/shard_map/ppermute | solution.py:534
  33.1 14.9 %collective-permute-start.4 = (bf16[40,256]{1,0:T(8,128)(2,1)S(1)}, bf16[40,256]{1,0:T(8,128)(2,1)S(1)}, u32[]{:S(2)}, u32[]{:S(2)}) collective-permute-start(bf16[40,256]{1,0:T(8,128)(2,1)S(1)} %make_coeffs.1.own_ref), channel_id=1, source_target_pairs={{0,8},{8,0},{16,24},{24,16},{1,9},{9,1},{17,25},{25,17},{2,10},{10... | collective-permute-start | bytes 61448 | tf_op jit(solution)/shard_map/ppermute | solution.py:514
  33.1 14.8 %collective-permute-start.5 = (bf16[40,256]{1,0:T(8,128)(2,1)S(1)}, bf16[40,256]{1,0:T(8,128)(2,1)S(1)}, u32[]{:S(2)}, u32[]{:S(2)}) collective-permute-start(bf16[40,256]{1,0:T(8,128)(2,1)S(1)} %make_coeffs.1.own_ref), channel_id=1, source_target_pairs={{0,16},{8,24},{16,0},{24,8},{1,17},{9,25},{17,1},{25,9},{2,18},{10... | collective-permute-start | bytes 61448 | tf_op jit(solution)/shard_map/ppermute | solution.py:514
  34.7 13.2 %collective-permute-start.6 = (bf16[40,256]{1,0:T(8,128)(2,1)S(1)}, bf16[40,256]{1,0:T(8,128)(2,1)S(1)}, u32[]{:S(2)}, u32[]{:S(2)}) collective-permute-start(bf16[40,256]{1,0:T(8,128)(2,1)S(1)} %make_coeffs.1.own_ref), channel_id=1, source_target_pairs={{0,24},{8,16},{16,8},{24,0},{1,25},{9,17},{17,9},{25,1},{2,26},{10... | collective-permute-start | bytes 61448 | tf_op jit(solution)/shard_map/ppermute | solution.py:514
  52.2 1.4 %collective-permute-start.7 = (f32[16,2048]{1,0:T(8,128)S(1)}, f32[16,2048]{1,0:T(8,128)S(1)}, u32[]{:S(2)}, u32[]{:S(2)}) collective-permute-start(f32[16,2048]{1,0:T(8,128)S(1)} %get-tuple-element.26), channel_id=1, source_target_pairs={{0,8},{8,0},{16,24},{24,16},{1,9},{9,1},{17,25},{25,17},{2,10},{10... | collective-permute-start | bytes 393224 | tf_op jit(solution)/shard_map/ppermute | solution.py:514
  53.6 4.5 %collective-permute-start.8 = (f32[8,2048]{1,0:T(8,128)S(1)}, f32[8,2048]{1,0:T(8,128)S(1)}, u32[]{:S(2)}, u32[]{:S(2)}) collective-permute-start(f32[8,2048]{1,0:T(8,128)S(1)} %get-tuple-element.27), channel_id=1, source_target_pairs={{0,16},{8,24},{16,0},{24,8},{1,17},{9,25},{17,1},{25,9},{2,18},{10... | collective-permute-start | bytes 196616 | tf_op jit(solution)/shard_map/ppermute | solution.py:514
  55.2 12.6 %collective-permute-start = (bf16[256,256]{1,0:T(8,128)(2,1)S(1)}, bf16[256,256]{1,0:T(8,128)(2,1)S(1)}, u32[]{:S(2)}, u32[]{:S(2)}) collective-permute-start(bf16[256,256]{1,0:T(8,128)(2,1)S(1)} %bitcast.11), channel_id=1, source_target_pairs={{0,16},{8,24},{16,0},{24,8},{1,17},{9,25},{17,1},{25,9},{2,18},{10... | collective-permute-start | bytes 393224 | tf_op jit(solution)/shard_map/ppermute | solution.py:514
  59.5 18.7 %all-to-all-start.1 = ((bf16[32,8,512]{2,1,0:T(8,128)(2,1)}), bf16[32,8,512]{2,1,0:T(8,128)(2,1)S(1)}, u32[]{:S(2)}, u32[]{:S(2)}) async-start(bf16[32,8,512]{2,1,0:T(8,128)(2,1)} %bitcast.8), calls=%async_computation.1 | async-start | bytes 524288 | tf_op jit(solution)/shard_map/all_to_all | solution.py:547
  67.8 1.6 %collective-permute-start.1 = (bf16[2,256,256]{2,1,0:T(8,128)(2,1)S(1)}, bf16[2,256,256]{2,1,0:T(8,128)(2,1)S(1)}, u32[]{:S(2)}, u32[]{:S(2)}) collective-permute-start(bf16[2,256,256]{2,1,0:T(8,128)(2,1)S(1)} %pad_maximum_fusion), channel_id=1, source_target_pairs={{0,8},{8,0},{16,24},{24,16},{1,9},{9,1},{17,25},{25,17},{2,10},{10... | collective-permute-start | bytes 786440 | tf_op jit(solution)/shard_map/ppermute | solution.py:514
  78.7 1.6 %collective-permute-start.9 = (f32[136,512]{1,0:T(8,128)S(1)}, f32[136,512]{1,0:T(8,128)S(1)}, u32[]{:S(2)}, u32[]{:S(2)}) collective-permute-start(f32[136,512]{1,0:T(8,128)S(1)} %gradient.1.own_ref), channel_id=1, source_target_pairs={{0,8},{8,0},{16,24},{24,16},{1,9},{9,1},{17,25},{25,17},{2,10},{10... | collective-permute-start | bytes 835592 | tf_op jit(solution)/shard_map/ppermute | solution.py:514
where the time goes:
time: 81.8 us; the launch traced here: 81.3 us
  waiting for transfers between devices  27.9 us (34%)
  Pallas kernels  26.8 us (33%)
  starting transfers between devices  25.7 us (31%)
    ppermute x1, waiting for transfers between devices, on_device(): before = lax.ppermute(up, 'space', [(i, i + 1) for i in range(slabs - 1)])  16.2 us
    pallas_call x1, Pallas kernels, states_pass(): pl.pallas_call(run_states, name='run_states', out_shape=(field, jax.Shape...  12.9 us
    all_to_all x1, starting transfers between devices, on_device(): lax.all_to_all(send.reshape(members * slabs, single, half), ('ens', 'spac...  8.27 us
    all_to_all x1, waiting for transfers between devices, on_device(): lax.all_to_all(send.reshape(members * slabs, single, half), ('ens', 'spac...  7.73 us
    all_to_all x1, starting transfers between devices, on_device(): pieces = lax.all_to_all(pieces, 'space', 0, 0)  7.32 us
    ppermute x8, starting transfers between devices, partner(): return lax.ppermute(value, 'ens', [(i, i ^ bit) for i in range(count)])  4.89 us
    pallas_call x1, Pallas kernels, gradient_halves(): pl.pallas_call(apply_potential, name='apply_potential', out_shape=(half,...  4.22 us
    ppermute x8, waiting for transfers between devices, partner(): return lax.ppermute(value, 'ens', [(i, i ^ bit) for i in range(count)])  3.95 us
  transfers between devices with their start and end apart: 12, of which 6 were waited for; matrix products, arithmetic and copies ran while one was open for 0% of the time, Pallas kernels for 22%

commit v1 on v0

--- a/solution.py
+++ b/solution.py
@@ -34,19 +34,27 @@
     return lax.broadcasted_iota(jnp.int32, shape, 0)
 
 
+def split_lanes(field):
+    return jnp.stack([field[:, k : k + LANES] for k in range(0, field.shape[1], LANES)])
+
+
+def join_lanes(field):
+    return jnp.concatenate([field[k] for k in range(field.shape[0])], axis=1)
+
+
 def shift_cols(field, step):
-    count = field.shape[1]
-    turned = pltpu.roll(field, (-step) % count, 1)
-    lane = lax.broadcasted_iota(jnp.int32, (field.shape[0], LANES), 1)
+    turned = pltpu.roll(field, (-step) % LANES, 2)
+    lane = lax.broadcasted_iota(jnp.int32, field.shape, 2)
+    outside = jnp.zeros_like(turned[:1])
     if step > 0:
-        edge = jnp.where(lane >= LANES - step, 0.0, turned[:, count - LANES :])
-        return jnp.concatenate([turned[:, : count - LANES], edge], axis=1)
-    edge = jnp.where(lane < -step, 0.0, turned[:, :LANES])
-    return jnp.concatenate([edge, turned[:, LANES:]], axis=1)
+        beside = jnp.concatenate([turned[1:], outside], axis=0)
+        return jnp.where(lane >= LANES - step, beside, turned)
+    beside = jnp.concatenate([outside, turned[:-1]], axis=0)
+    return jnp.where(lane < -step, beside, turned)
 
 
 def shift_rows(field, step):
-    return pltpu.roll(field, (-step) % field.shape[0], 0)
+    return pltpu.roll(field, (-step) % field.shape[1], 1)
 
 
 def dx(field):
@@ -57,7 +65,7 @@
     return shift_rows(field, 1) - shift_rows(field, -1)
 
 
-def pack(index_ref, member_ref, states_ref, targets_ref, sea_ref, basis_ref, control_ref, up_ref, down_ref, out_ref, rows_ref, last, first, seen, sea, basis, own, sems):
+def pack(index_ref, member_ref, states_ref, targets_ref, sea_ref, basis_ref, control_ref, up_ref, down_ref, out_ref, last, first, seen, sea, basis, own, sems):
     count, _, _, rows, cols = states_ref.shape
     width = basis_ref.shape[1]
     rows_out = control_ref.shape[0]
@@ -115,7 +123,6 @@
     ).astype(BF16)
     part = own[...].astype(BF16)
     part_basis = basis[:, pl.ds(at, quarter)]
-    rows_ref[...] = basis[...]
     for k in range(out_ref.shape[0]):
         out_ref[k, :rows_out] = part
         out_ref[k, rows_out:] = part_basis
@@ -132,10 +139,9 @@
             edges,
             edges,
             jax.ShapeDtypeStruct((slabs, rows_out + rows, quarter), BF16),
-            jax.ShapeDtypeStruct((rows, width), BF16),
         ),
         in_specs=[SMEM, SMEM] + [HBM] * 5,
-        out_specs=(VMEM, VMEM, VMEM, VMEM),
+        out_specs=(VMEM, VMEM, VMEM),
         scratch_shapes=[
             pltpu.VMEM((count, fields, TILE, cols), BF16),
             pltpu.VMEM((count, fields, TILE, cols), BF16),
@@ -147,7 +153,7 @@
         ],
         compiler_params=limit(14),
     )(
-        section_index,
+        in_hbm(section_index),
         member.reshape(1),
         *map(in_hbm, (checkpoints, targets, sea_mask, basis_rows, control)),
     )
@@ -167,7 +173,6 @@
     size = array.size * array.dtype.itemsize
     return pl.pallas_call(
         hold,
-        name="hold",
         out_shape=jax.ShapeDtypeStruct(array.shape, array.dtype),
         in_specs=[HBM],
         out_specs=VMEM,
@@ -176,92 +181,140 @@
     )(in_hbm(array))
 
 
-def run_states(index_ref, state_ref, before_ref, after_ref, seen_before_ref, seen_after_ref, targets_ref, sea_ref, base_ref, pairs_ref, out_mask_ref, mask_ref, gx, gy, seen_edge):
+def run_states(index_ref, state_ref, before_ref, after_ref, shared_before_ref, shared_after_ref, targets_ref, sea_ref, basis_ref, base_ref, pairs_ref, mask_ref, rows_ref, mask, seen_edge, heights, fluxes, mid_fluxes, weights, besides, misfits, partial, gx, gy):
     s = pl.program_id(0)
-    _, cols = sea_ref.shape
+    rows, cols = sea_ref.shape
+    width = basis_ref.shape[1]
+    tiles = rows // TILE + 1
     row = tile_rows((TILE, cols))
+    top = row < 4
+
+    def put(ref, tile, value):
+        ref[:, TILE * (tile + 1) : TILE * (tile + 2), :] = value
+        if tile == tiles - 1:
+            ref[:, :TILE, :] = value
+        if tile == 0:
+            ref[:, TILE * (tiles + 1) :, :] = value
+
+    def get(ref, tile, step=0):
+        start = TILE * (tile + 1) + step
+        return ref[:, start : start + TILE, :]
+
+    def rows_of(tile):
+        return slice(TILE * tile, TILE * (tile + 1))
 
     @pl.when(s == 0)
     def _():
-        edge = jnp.where(
-            row < 2,
-            seen_after_ref[1].astype(F32),
-            jnp.where(row >= 6, seen_before_ref[1].astype(F32), 0.0),
-        )
-        mask_ref[...] = jnp.concatenate([sea_ref[...].astype(F32), edge], axis=0)
-        out_mask_ref[...] = mask_ref[...].astype(BF16)
-        seen_edge[0] = seen_before_ref[0].astype(F32)
-        seen_edge[1] = seen_after_ref[0].astype(F32)
+        after = shared_after_ref[1].astype(F32)
+        before = shared_before_ref[1].astype(F32)
+        edge = jnp.where(row < 2, after, jnp.where(row >= 6, before, 0.0))
+        for tile in range(tiles - 1):
+            mask[:, rows_of(tile), :] = split_lanes(sea_ref[rows_of(tile), :].astype(F32))
+        mask[:, rows:, :] = split_lanes(edge)
+        mask_ref[...] = mask[...].astype(BF16)
+        seen_edge[0] = shared_before_ref[0].astype(F32)
+        seen_edge[1] = shared_after_ref[0].astype(F32)
         gx[...] = jnp.zeros_like(gx)
         gy[...] = jnp.zeros_like(gy)
         pairs_ref[...] = jnp.zeros_like(pairs_ref)
-
-    mask = mask_ref[...]
+        after = pltpu.roll(after[:, :width], 6, 0)
+        before = pltpu.roll(before[:, :width], 4, 0)
+        edge = jnp.where(row[:, :width] < 2, after, jnp.where(row[:, :width] >= 6, before, 0.0))
+        rows_ref[...] = jnp.concatenate(
+            [basis_ref[...].astype(F32), edge], axis=0
+        ).astype(BF16)
+
+    after = after_ref[0].astype(F32)
     before = before_ref[0].astype(F32)
-    after = after_ref[0].astype(F32)
-    top = row < 4
-
-    def extended(field, forward, back):
-        edge = jnp.where(top, pltpu.roll(after, forward, 0), pltpu.roll(before, back, 0))
-        return jnp.concatenate([state_ref[0, 0, field].astype(F32), edge], axis=0)
-
-    height = jnp.concatenate(
-        [state_ref[0, 0, 0].astype(F32), jnp.where(top, after, before)], axis=0
-    )
-    east = extended(1, 2, 6)
-    north = extended(2, 5, 3)
-    seen = jnp.concatenate(
-        [
-            targets_ref[0].astype(F32),
-            jnp.where(top, seen_edge[1, pl.ds(s, 1), :], seen_edge[0, pl.ds(s, 1), :]),
-        ],
-        axis=0,
-    )
+    edges = (
+        jnp.where(top, after, before),
+        jnp.where(top, pltpu.roll(after, 2, 0), pltpu.roll(before, 6, 0)),
+        jnp.where(top, pltpu.roll(after, 5, 0), pltpu.roll(before, 3, 0)),
+    )
+
+    def load(field, tile):
+        if tile == tiles - 1:
+            return split_lanes(edges[field])
+        return split_lanes(state_ref[0, 0, field, rows_of(tile), :].astype(F32))
+
     half = 0.5 * TIME_STEP
     keep = 1.0 - TIME_STEP * FRICTION
-    deep = DEPTH + height
-    height_mid = mask * (height - half * (dx(deep * east) + dy(deep * north)))
-    east_mid = mask * (
-        keep * east + TIME_STEP * CORIOLIS * north - half * GRAVITY * dx(height)
-    )
-    north_mid = mask * (
-        keep * north - TIME_STEP * CORIOLIS * east - half * GRAVITY * dy(height)
-    )
-    deep = DEPTH + height_mid
-    height_end = 0.5 * (height + height_mid) - 0.5 * half * (
-        dx(deep * east_mid) + dy(deep * north_mid)
-    )
-    misfit = mask * (height_end - seen)
-    weight = mask * deep
-    gx[...] += weight * dx(misfit)
-    gy[...] += weight * dy(misfit)
-    beside = shift_cols(weight, 1)
-    pairs_ref[0] += weight * weight
-    pairs_ref[1] += weight * shift_cols(weight, 2)
-    pairs_ref[2] += weight * shift_rows(weight, 2)
-    pairs_ref[3] += weight * shift_rows(beside, 1)
-    pairs_ref[4] += weight * shift_rows(beside, -1)
+    turn = TIME_STEP * CORIOLIS / keep
+    slope = half * GRAVITY / keep
+
+    for tile in range(tiles):
+        height = load(0, tile)
+        put(heights, tile, height)
+        put(fluxes, tile, (DEPTH + height) * load(2, tile))
+
+    for tile in range(tiles):
+        height = get(heights, tile)
+        east = load(1, tile)
+        north = load(2, tile)
+        flux = dx((DEPTH + height) * east) + (get(fluxes, tile, 1) - get(fluxes, tile, -1))
+        sea = mask[:, rows_of(tile), :]
+        height_mid = sea * (height - half * flux)
+        weight = DEPTH * sea + height_mid
+        east_mid = east + turn * north - slope * dx(height)
+        north_mid = (
+            north - turn * east - slope * (get(heights, tile, 1) - get(heights, tile, -1))
+        )
+        if tile == tiles - 1:
+            seen = split_lanes(
+                jnp.where(top, seen_edge[1, pl.ds(s, 1), :], seen_edge[0, pl.ds(s, 1), :])
+            )
+        else:
+            seen = split_lanes(targets_ref[0, rows_of(tile), :].astype(F32))
+        put(mid_fluxes, tile, weight * north_mid)
+        put(weights, tile, weight)
+        put(besides, tile, shift_cols(weight, 1))
+        partial[:, rows_of(tile), :] = (
+            height + height_mid - 2.0 * seen - half * keep * dx(weight * east_mid)
+        )
+
+    for tile in range(tiles):
+        change = get(mid_fluxes, tile, 1) - get(mid_fluxes, tile, -1)
+        misfit = mask[:, rows_of(tile), :] * (
+            partial[:, rows_of(tile), :] - half * keep * change
+        )
+        put(misfits, tile, misfit)
+        gx[:, rows_of(tile), :] += get(weights, tile) * dx(misfit)
+
+    for tile in range(tiles):
+        here = rows_of(tile)
+        weight = get(weights, tile)
+        gy[:, here, :] += weight * (get(misfits, tile, 1) - get(misfits, tile, -1))
+        pairs_ref[0, :, here, :] += weight * weight
+        pairs_ref[1, :, here, :] += weight * shift_cols(weight, 2)
+        pairs_ref[2, :, here, :] += weight * get(weights, tile, 2)
+        pairs_ref[3, :, here, :] += weight * get(besides, tile, 1)
+        pairs_ref[4, :, here, :] += weight * get(besides, tile, -1)
 
     @pl.when(s == pl.num_programs(0) - 1)
     def _():
-        scale = 0.125 * TIME_STEP * TIME_STEP
+        scale = 0.0625 * TIME_STEP * TIME_STEP
         base_ref[...] = scale * (dy(gx[...]) - dx(gy[...]))
 
 
-def states_pass(section_index, checkpoints, before, after, targets, sea_mask):
+def states_pass(section_index, checkpoints, before, after, targets, sea_mask, basis_rows):
     count, _, fields, rows, cols = checkpoints.shape
+    width = basis_rows.shape[1]
     ring = rows + TILE
-    field = jax.ShapeDtypeStruct((ring, cols), F32)
+    lanes = cols // LANES
+    padded = pltpu.VMEM((lanes, ring + 2 * TILE, LANES), F32)
+    plain = pltpu.VMEM((lanes, ring, LANES), F32)
     edge = pl.BlockSpec((1, TILE, cols), lambda s, index: (s, 0, 0))
     shared = pl.BlockSpec((2, TILE, cols), lambda s, index: (count // 2, 0, 0))
+    outs = (
+        jax.ShapeDtypeStruct((lanes, ring, LANES), F32),
+        jax.ShapeDtypeStruct((5, lanes, ring, LANES), F32),
+        jax.ShapeDtypeStruct((lanes, ring, LANES), BF16),
+        jax.ShapeDtypeStruct((ring, width), BF16),
+    )
     return pl.pallas_call(
         run_states,
         name="run_states",
-        out_shape=(
-            field,
-            jax.ShapeDtypeStruct((5, ring, cols), F32),
-            jax.ShapeDtypeStruct((ring, cols), BF16),
-        ),
+        out_shape=outs,
         grid_spec=pltpu.PrefetchScalarGridSpec(
             num_scalar_prefetch=1,
             grid=(count,),
@@ -273,20 +326,16 @@
                 shared,
                 pl.BlockSpec((1, rows, cols), lambda s, index: (s, 0, 0)),
                 pl.BlockSpec((rows, cols), lambda s, index: (0, 0)),
+                pl.BlockSpec((rows, width), lambda s, index: (0, 0)),
             ],
-            out_specs=(
-                pl.BlockSpec((ring, cols), lambda s, index: (0, 0)),
-                pl.BlockSpec((5, ring, cols), lambda s, index: (0, 0, 0)),
-                pl.BlockSpec((ring, cols), lambda s, index: (0, 0)),
+            out_specs=tuple(
+                pl.BlockSpec(out.shape, lambda s, index, n=len(out.shape): (0,) * n) for out in outs
             ),
-            scratch_shapes=[
-                pltpu.VMEM((ring, cols), F32),
-                pltpu.VMEM((ring, cols), F32),
-                pltpu.VMEM((ring, cols), F32),
-                pltpu.VMEM((2, TILE, cols), F32),
-            ],
+            scratch_shapes=[plain, pltpu.VMEM((2, TILE, cols), F32)]
+            + [padded] * 6
+            + [plain] * 3,
         ),
-        compiler_params=limit(32),
+        compiler_params=limit(20),
     )(
         section_index,
         in_hbm(checkpoints),
@@ -295,64 +344,40 @@
         before,
         after,
         in_hbm(targets),
-        sea_mask,
-    )
-
-
-def make_coeffs(basis_ref, before_ref, after_ref, pieces_ref, out_ref):
+        in_hbm(sea_mask),
+        in_hbm(basis_rows),
+    )
+
+
+def make_coeffs(basis_ref, pieces_ref, out_ref):
     slabs, _, quarter = pieces_ref.shape
-    _, width = basis_ref.shape
-    rows_out = width // slabs
-    row = tile_rows((TILE, width))
-    after = pltpu.roll(after_ref[0, :, :width].astype(F32), 6, 0)
-    before = pltpu.roll(before_ref[0, :, :width].astype(F32), 4, 0)
-    edge = jnp.where(row < 2, after, jnp.where(row >= 6, before, 0.0))
-    basis = jnp.concatenate([basis_ref[...].astype(F32), edge], axis=0).astype(BF16)
-    part = pieces_ref[:, :rows_out, :].reshape(slabs * rows_out, quarter)
-    out_ref[...] = jnp.dot(basis, part, preferred_element_type=F32).astype(BF16)
-
-
-def coeffs_part(basis_rows, before, after, pieces):
-    rows, width = basis_rows.shape
-    last = before.shape[0] - 1
-    edge = pl.BlockSpec((1, TILE, before.shape[2]), lambda i: (last, 0, 0))
+    width = basis_ref.shape[1]
+    part = pieces_ref[:, : width // slabs, :].reshape(width, quarter)
+    out_ref[...] = jnp.dot(basis_ref[...], part, preferred_element_type=F32).astype(BF16)
+
+
+def coeffs_part(basis, pieces):
     return pl.pallas_call(
         make_coeffs,
         name="make_coeffs",
-        out_shape=jax.ShapeDtypeStruct((rows + TILE, pieces.shape[2]), BF16),
-        grid=(1,),
-        in_specs=[
-            pl.BlockSpec((rows, width), lambda i: (0, 0)),
-            edge,
-            edge,
-            pl.BlockSpec(pieces.shape, lambda i: (0, 0, 0)),
-        ],
-        out_specs=pl.BlockSpec((rows + TILE, pieces.shape[2]), lambda i: (0, 0)),
+        out_shape=jax.ShapeDtypeStruct((basis.shape[0], pieces.shape[2]), BF16),
+        in_specs=[VMEM, VMEM],
+        out_specs=VMEM,
         compiler_params=limit(12),
-    )(basis_rows, before, after, pieces)
-
-
-def apply_potential(member_ref, own_ref, near_ref, far_ref, both_ref, cols_ref, base_ref, pairs_ref, mask_ref, keep_ref, give_ref, coeffs, total, held_cols, field, sems):
+    )(basis, pieces)
+
+
+def apply_potential(member_ref, own_ref, near_ref, far_ref, both_ref, cols_ref, base_ref, pairs_ref, mask_ref, keep_ref, give_ref, coeffs, total):
     member = member_ref[0]
-    blocks = held_cols.shape[0]
-    block = held_cols.shape[1]
-    copies = []
-    for k in range(blocks):
-        copy = pltpu.make_async_copy(
-            cols_ref.at[pl.ds(k * block, block), :], held_cols.at[k], sems.at[k]
-        )
-        copy.start()
-        copies.append(copy)
     quarter = own_ref.shape[1]
     for bits, ref in enumerate((own_ref, near_ref, far_ref, both_ref)):
         at = pl.multiple_of((member ^ bits) * quarter, quarter)
         coeffs[:, pl.ds(at, quarter)] = ref[...]
-    for k, copy in enumerate(copies):
-        copy.wait()
-        field[:, k * block : (k + 1) * block] = lax.dot_general(
-            coeffs[...], held_cols[k], (((1,), (1,)), ((), ())), preferred_element_type=F32
+    potential = split_lanes(
+        lax.dot_general(
+            coeffs[...], cols_ref[...], (((1,), (1,)), ((), ())), preferred_element_type=F32
         )
-    potential = field[...]
+    )
     sx = -dy(potential)
     sy = dx(potential)
     mask = mask_ref[...].astype(F32)
@@ -376,32 +401,29 @@
     scale = -(TIME_STEP**4) / 64.0
     grad = base_ref[...] + scale * (dy(gx) - dx(gy))
     pair = keep_ref.shape[0]
-    total[...] = grad[: 2 * pair]
+    total[...] = join_lanes(grad[:, : 2 * pair, :])
     core = member % 2
     keep_ref[...] = total[pl.ds(pl.multiple_of(core * pair, pair), pair), :]
     give_ref[...] = total[pl.ds(pl.multiple_of((1 - core) * pair, pair), pair), :]
 
 
 def gradient_halves(member, parts, basis_cols, base, pairs, mask):
-    ring, cols = base.shape
-    width = basis_cols.shape[1]
+    _, ring, _ = base.shape
+    cols, width = basis_cols.shape
     pair = (ring - TILE) // 2
     half = jax.ShapeDtypeStruct((pair, cols), F32)
     return pl.pallas_call(
         apply_potential,
         name="apply_potential",
         out_shape=(half, half),
-        in_specs=[SMEM] + [VMEM] * 4 + [HBM] + [VMEM] * 3,
+        in_specs=[SMEM] + [VMEM] * 8,
         out_specs=(VMEM, VMEM),
         scratch_shapes=[
             pltpu.VMEM((ring, width), BF16),
             pltpu.VMEM((2 * pair, cols), F32),
-            pltpu.VMEM((4, cols // 4, width), BF16),
-            pltpu.VMEM((ring, cols), F32),
-            pltpu.SemaphoreType.DMA((4,)),
         ],
         compiler_params=limit(24),
-    )(member.reshape(1), *parts, in_hbm(basis_cols), base, pairs, mask)
+    )(member.reshape(1), *parts, basis_cols, base, pairs, mask)
 
 
 def project(own_ref, other_ref, cols_ref, out_ref):
@@ -527,16 +549,21 @@
     half = width // 2
     single = rows // 4
 
-    up, down, pieces, near_rows = packed(
+    up, down, pieces = packed(
         section_index, member, checkpoints, targets, sea_mask, basis_rows, control, slabs, quarter
     )
     before = lax.ppermute(up, "space", [(i, i + 1) for i in range(slabs - 1)])
     after = lax.ppermute(down, "space", [(i + 1, i) for i in range(slabs - 1)])
     pieces = lax.all_to_all(pieces, "space", 0, 0)
-    base, pairs, mask = states_pass(section_index, checkpoints, before, after, targets, sea_mask)
-    own = coeffs_part(near_rows, before, after, pieces)
-    parts = [own] + [partner(own, bits) for bits in (1, 2, 3)]
-    keep, give = gradient_halves(member, parts, basis_cols, base, pairs, mask)
+    base, pairs, mask, ext_rows = states_pass(
+        section_index, checkpoints, before, after, targets, sea_mask, basis_rows
+    )
+    own = coeffs_part(ext_rows, pieces)
+    parts = [own]
+    for bits in (1, 2, 3):
+        parts.append(partner(own, bits))
+    cols = held(basis_cols)
+    keep, give = gradient_halves(member, parts, cols, base, pairs, mask)
 
     keep = keep + partner(give, 1)
     own_rows = lax.dynamic_slice_in_dim(keep, chip * single, single, 0)

time: 81.8 us -> 85 us (1.039)
  waiting for transfers between devices: 27.9 us -> 31.5 us
  local copies, waits for them, and re-layouts: 0.7 us -> 4.17 us
  Pallas kernels: 26.8 us -> 24.4 us
  starting transfers between devices: 25.7 us -> 24.2 us
    ppermute x8, waiting for transfers between devices: 3.95 us -> 7.54 us  [partner(): return lax.ppermute(value, 'ens', [(i, i ^ bit) for i in range(count)])]
    unnamed x6, local copies, waits for them, and re-layouts: 0.66 us -> 4.13 us
    pallas_call x1, Pallas kernels: 4.22 us -> 2.11 us  [gradient_halves(): pl.pallas_call(apply_potential, name='apply_potential', out_shape=(half,...]
    all_to_all x1, starting transfers between devices: 8.27 us -> 7.08 us  [on_device(): lax.all_to_all(send.reshape(members * slabs, single, half), ('ens', 'spac...]
  transfers between devices with their start and end apart: 12 -> 12, of which waited for: 6 -> 7; matrix products, arithmetic and copies ran while one was open for 0% -> 0% of each run, Pallas kernels for 22% -> 20%
where the time goes in v1:
time: 85 us; the launch traced here: 84.5 us
  waiting for transfers between devices  31.5 us (37%)
  Pallas kernels  24.4 us (29%)
  starting transfers between devices  24.2 us (28%)
  local copies, waits for them, and re-layouts  4.17 us (5%)
    ppermute x1, waiting for transfers between devices, on_device(): before = lax.ppermute(up, 'space', [(i, i + 1) for i in range(slabs - 1)])  16.2 us
    pallas_call x1, Pallas kernels, states_pass(): pl.pallas_call(run_states, name='run_states', out_shape=outs, grid_spec=p...  12.3 us
    all_to_all x1, waiting for transfers between devices, on_device(): lax.all_to_all(send.reshape(members * slabs, single, half), ('ens', 'spac...  7.73 us
    ppermute x8, waiting for transfers between devices, partner(): return lax.ppermute(value, 'ens', [(i, i ^ bit) for i in range(count)])  7.54 us
    all_to_all x1, starting transfers between devices, on_device(): pieces = lax.all_to_all(pieces, 'space', 0, 0)  7.32 us
    all_to_all x1, starting transfers between devices, on_device(): lax.all_to_all(send.reshape(members * slabs, single, half), ('ens', 'spac...  7.08 us
    ppermute x8, starting transfers between devices, partner(): return lax.ppermute(value, 'ens', [(i, i ^ bit) for i in range(count)])  4.62 us
    unnamed x6, local copies, waits for them, and re-layouts  4.13 us
  transfers between devices with their start and end apart: 12, of which 7 were waited for; matrix products, arithmetic and copies ran while one was open for 0% of the time, Pallas kernels for 20%

profile of v1, /device:TPU:0, one launch (start us, length us, event | category | flops | bytes accessed | tf_op | source)
XLA Modules:
  0.0 84.5 jit_solution(8089162876780651710)
XLA Ops:
  0.0 3.6 %pack.1 = (bf16[10,8,2048]{2,1,0:T(8,128)(2,1)S(1)}, bf16[10,8,2048]{2,1,0:T(8,128)(2,1)S(1)}, bf16[8,160,256]{2,1,0:T(8,128)(2,1)}) custom-call(s32[8]{0:T(128)} %index_ref.3, s32[1]{0:T(128)} %bitcast.1.member_ref, bf16[8,2,3,32,2048]{4,3,2,1,0:T(8,128)(2,1)} %state_ref.1, bf16[8,32,2048]{2,1,0:T(8,128)(2,1)} %targets_ref.3, s32[32,2048]{1,0:T(8,128)} %sea_ref.3, ...), custom_call_target="tpu_custom_call" | custom-call | tf_op jit(solution)/shard_map/pack/pallas_call | solution.py:135
  3.6 7.3 %all-to-all-start = ((bf16[8,160,256]{2,1,0:T(8,128)(2,1)}), bf16[8,160,256]{2,1,0:T(8,128)(2,1)S(1)}, u32[]{:S(2)}, u32[]{:S(2)}) async-start(bf16[8,160,256]{2,1,0:T(8,128)(2,1)} %get-tuple-element.16), calls=%async_computation | async-start | bytes 1310720 | tf_op jit(solution)/shard_map/all_to_all | solution.py:557
  11.0 3.9 %collective-permute-start.2 = (bf16[10,8,2048]{2,1,0:T(8,128)(2,1)S(1)}, bf16[10,8,2048]{2,1,0:T(8,128)(2,1)S(1)}, u32[]{:S(2)}, u32[]{:S(2)}) collective-permute-start(bf16[10,8,2048]{2,1,0:T(8,128)(2,1)S(1)} %get-tuple-element.19), channel_id=1, source_target_pairs={{0,1},{1,2},{2,3},{3,4},{4,5},{5,6},{6,7},{8,9},{9,10},{10,11},{11... | collective-permute-start | bytes 983048 | tf_op jit(solution)/shard_map/ppermute | solution.py:555
  14.9 1.3 %collective-permute-start.3 = (bf16[10,8,2048]{2,1,0:T(8,128)(2,1)S(1)}, bf16[10,8,2048]{2,1,0:T(8,128)(2,1)S(1)}, u32[]{:S(2)}, u32[]{:S(2)}) collective-permute-start(bf16[10,8,2048]{2,1,0:T(8,128)(2,1)S(1)} %get-tuple-element.20), channel_id=1, source_target_pairs={{1,0},{2,1},{3,2},{4,3},{5,4},{6,5},{7,6},{9,8},{10,9},{11,10},{12... | collective-permute-start | bytes 983048 | tf_op jit(solution)/shard_map/ppermute | solution.py:556
  16.2 16.2 %collective-permute-done.2.before_ref.shared_before_ref = bf16[10,8,2048]{2,1,0:T(8,128)(2,1)S(1)} collective-permute-done((bf16[10,8,2048]{2,1,0:T(8,128)(2,1)S(1)}, bf16[10,8,2048]{2,1,0:T(8,128)(2,1)S(1)}, u32[]{:S(2)}, u32[]{:S(2)}) %collective-permute-start.2) | collective-permute-done | bytes 327712 | tf_op jit(solution)/shard_map/ppermute | solution.py:555
  32.4 12.3 %run_states.1 = (f32[16,40,128]{2,1,0:T(8,128)S(1)}, f32[5,16,40,128]{3,2,1,0:T(8,128)S(1)}, bf16[16,40,128]{2,1,0:T(8,128)(2,1)S(1)}, bf16[40,1024]{1,0:T(8,128)(2,1)S(1)}) custom-call(s32[8]{0:T(128)S(1)} %copy-done.2, bf16[8,2,3,32,2048]{4,3,2,1,0:T(8,128)(2,1)} %state_ref.1, bf16[10,8,2048]{2,1,0:T(8,128)(2,1)S(1)} %collective-permute-done.2.before_ref.shared_before_ref, ...), custom_call_target="tpu_custom_call" | custom-call | tf_op jit(solution)/shard_map/run_states/pallas_call | solution.py:314
  44.8 0.0 all-to-all-done.pieces_ref
  44.8 0.2 make_coeffs.1.own_ref
  45.0 0.1 collective-permute-start.4
  45.1 1.6 %collective-permute-start.5 = (bf16[40,256]{1,0:T(8,128)(2,1)S(1)}, bf16[40,256]{1,0:T(8,128)(2,1)S(1)}, u32[]{:S(2)}, u32[]{:S(2)}) collective-permute-start(bf16[40,256]{1,0:T(8,128)(2,1)S(1)} %make_coeffs.1.own_ref), channel_id=1, source_target_pairs={{0,16},{8,24},{16,0},{24,8},{1,17},{9,25},{17,1},{25,9},{2,18},{10... | collective-permute-start | bytes 61448 | tf_op jit(solution)/shard_map/ppermute | solution.py:536
  46.6 0.3 collective-permute-start.6
  46.9 2.2 %shard_map.73.cols_ref = bf16[2048,1024]{1,0:T(8,128)(2,1)S(1)} custom-call(bf16[2048,1024]{1,0:T(8,128)(2,1)} %source_ref.1), custom_call_target="tpu_custom_call" | custom-call | tf_op jit(solution)/shard_map/pallas_call | solution.py:174
  49.1 0.0 collective-permute-done.4.near_ref
  49.1 0.7 collective-permute-done.6.both_ref
  49.8 2.1 %apply_potential.1 = (f32[16,2048]{1,0:T(8,128)S(1)}, f32[16,2048]{1,0:T(8,128)S(1)}) custom-call(s32[1]{0:T(128)} %bitcast.1.member_ref, bf16[40,256]{1,0:T(8,128)(2,1)S(1)} %make_coeffs.1.own_ref, bf16[40,256]{1,0:T(8,128)(2,1)S(1)} %collective-permute-done.4.near_ref, bf16[40,256]{1,0:T(8,128)(2,1)S(1)} %collective-permute-done.5.far_ref, ...), custom_call_target="tpu_custom_call" | custom-call | tf_op jit(solution)/shard_map/apply_potential/pallas_call | solution.py:415
  52.0 1.9 %copy-done = bf16[2048,1024]{1,0:T(8,128)(2,1)} copy-done((bf16[2048,1024]{1,0:T(8,128)(2,1)}, bf16[2048,1024]{1,0:T(8,128)(2,1)S(1)}, u32[]{:S(2)}) %copy-start) | copy-done | bytes 4194328
  53.9 0.2 collective-permute-start.7
  54.1 1.2 %collective-permute-done.7 = f32[16,2048]{1,0:T(8,128)S(1)} collective-permute-done((f32[16,2048]{1,0:T(8,128)S(1)}, f32[16,2048]{1,0:T(8,128)S(1)}, u32[]{:S(2)}, u32[]{:S(2)}) %collective-permute-start.7) | collective-permute-done | bytes 131104 | tf_op jit(solution)/shard_map/ppermute | solution.py:536
  55.3 0.9 %collective-permute-start.8 = (f32[8,2048]{1,0:T(8,128)S(1)}, f32[8,2048]{1,0:T(8,128)S(1)}, u32[]{:S(2)}, u32[]{:S(2)}) collective-permute-start(f32[8,2048]{1,0:T(8,128)S(1)} %get-tuple-element.27), channel_id=1, source_target_pairs={{0,16},{8,24},{16,0},{24,8},{1,17},{9,25},{17,1},{25,9},{2,18},{10... | collective-permute-start | bytes 196616 | tf_op jit(solution)/shard_map/ppermute | solution.py:536
  56.2 1.3 %collective-permute-start = (bf16[256,256]{1,0:T(8,128)(2,1)S(1)}, bf16[256,256]{1,0:T(8,128)(2,1)S(1)}, u32[]{:S(2)}, u32[]{:S(2)}) collective-permute-start(bf16[256,256]{1,0:T(8,128)(2,1)S(1)} %bitcast.11), channel_id=1, source_target_pairs={{0,16},{8,24},{16,0},{24,8},{1,17},{9,25},{17,1},{25,9},{2,18},{10... | collective-permute-start | bytes 393224 | tf_op jit(solution)/shard_map/ppermute | solution.py:536
  57.5 2.8 %collective-permute-done.8.other_ref = f32[8,2048]{1,0:T(8,128)S(1)} collective-permute-done((f32[8,2048]{1,0:T(8,128)S(1)}, f32[8,2048]{1,0:T(8,128)S(1)}, u32[]{:S(2)}, u32[]{:S(2)}) %collective-permute-start.8) | collective-permute-done | bytes 65568 | tf_op jit(solution)/shard_map/ppermute | solution.py:536
  60.3 2.2 %copy-done.1 = bf16[2048,1024]{1,0:T(8,128)(2,1)S(1)} copy-done((bf16[2048,1024]{1,0:T(8,128)(2,1)S(1)}, bf16[2048,1024]{1,0:T(8,128)(2,1)}, u32[]{:S(2)}) %copy-start.1) | copy-done | bytes 4194328
  62.5 1.4 %project.1 = bf16[4,8,8,512]{3,2,1,0:T(8,128)(2,1)} custom-call(f32[8,2048]{1,0:T(8,128)S(1)} %get-tuple-element.28.own_ref, f32[8,2048]{1,0:T(8,128)S(1)} %collective-permute-done.8.other_ref, bf16[2048,1024]{1,0:T(8,128)(2,1)S(1)} %copy-done.1), custom_call_target="tpu_custom_call" | custom-call | tf_op jit(solution)/shard_map/project/pallas_call | solution.py:443
  63.9 7.1 %all-to-all-start.1 = ((bf16[32,8,512]{2,1,0:T(8,128)(2,1)}), bf16[32,8,512]{2,1,0:T(8,128)(2,1)S(1)}, u32[]{:S(2)}, u32[]{:S(2)}) async-start(bf16[32,8,512]{2,1,0:T(8,128)(2,1)} %bitcast.8), calls=%async_computation.1 | async-start | bytes 524288 | tf_op jit(solution)/shard_map/all_to_all | solution.py:574
  71.0 0.3 collective-permute-start.1
  71.3 1.3 %collective-permute-done.1.near_ref = bf16[2,256,256]{2,1,0:T(8,128)(2,1)S(1)} collective-permute-done((bf16[2,256,256]{2,1,0:T(8,128)(2,1)S(1)}, bf16[2,256,256]{2,1,0:T(8,128)(2,1)S(1)}, u32[]{:S(2)}, u32[]{:S(2)}) %collective-permute-start.1) | collective-permute-done | bytes 262176 | tf_op jit(solution)/shard_map/ppermute | solution.py:536
  72.6 1.1 %assemble.1 = (bf16[1024,256]{1,0:T(8,128)(2,1)S(1)}, f32[128,1024]{1,0:T(8,128)S(1)}) custom-call(s32[1]{0:T(128)} %bitcast.1.member_ref, bf16[256,256]{1,0:T(8,128)(2,1)S(1)} %bitcast.13, bf16[256,256]{1,0:T(8,128)(2,1)S(1)} %collective-permute-done.far_ref, bf16[2,256,256]{2,1,0:T(8,128)(2,1)S(1)} %collective-permute-done.1.near_ref, f32[128,1024]{1,0:T(8,128)} %control_ref.3), custom_call_target="tpu_custom_call" | custom-call | tf_op jit(solution)/shard_map/assemble/pallas_call | solution.py:468
  73.7 7.7 %all-to-all-done.1 = bf16[32,8,512]{2,1,0:T(8,128)(2,1)S(1)} async-done(((bf16[32,8,512]{2,1,0:T(8,128)(2,1)}), bf16[32,8,512]{2,1,0:T(8,128)(2,1)S(1)}, u32[]{:S(2)}, u32[]{:S(2)}) %all-to-all-start.1) | async-done | bytes 262176 | tf_op jit(solution)/shard_map/all_to_all | solution.py:574
  81.4 0.5 gradient.1.own_ref
  81.9 0.1 collective-permute-start.9
  81.9 1.5 %collective-permute-done.9.other_ref = f32[136,512]{1,0:T(8,128)S(1)} collective-permute-done((f32[136,512]{1,0:T(8,128)S(1)}, f32[136,512]{1,0:T(8,128)S(1)}, u32[]{:S(2)}, u32[]{:S(2)}) %collective-permute-start.9) | collective-permute-done | bytes 278560 | tf_op jit(solution)/shard_map/ppermute | solution.py:536
  83.5 1.0 %update.1 = f32[128,1024]{1,0:T(8,128)} custom-call(s32[1]{0:T(128)} %bitcast.core_ref, f32[128,1024]{1,0:T(8,128)S(1)} %get-tuple-element.17.control_ref, f32[136,512]{1,0:T(8,128)S(1)} %gradient.1.own_ref, f32[136,512]{1,0:T(8,128)S(1)} %collective-permute-done.9.other_ref), custom_call_target="tpu_custom_call" | custom-call | tf_op jit(solution)/shard_map/update/pallas_call | solution.py:524
  (12 shorter events, 0.1 us)
Async XLA Ops:
  0.0 32.4 %copy-start.2 = (s32[8]{0:T(128)S(1)}, s32[8]{0:T(128)}, u32[]{:S(2)}) copy-start(s32[8]{0:T(128)} %index_ref.3) | copy-start | bytes 100
  3.6 41.1 %all-to-all-start = ((bf16[8,160,256]{2,1,0:T(8,128)(2,1)}), bf16[8,160,256]{2,1,0:T(8,128)(2,1)S(1)}, u32[]{:S(2)}, u32[]{:S(2)}) async-start(bf16[8,160,256]{2,1,0:T(8,128)(2,1)} %get-tuple-element.16), calls=%async_computation | async-start | bytes 1310720 | tf_op jit(solution)/shard_map/all_to_all | solution.py:557
  11.0 21.5 %collective-permute-start.2 = (bf16[10,8,2048]{2,1,0:T(8,128)(2,1)S(1)}, bf16[10,8,2048]{2,1,0:T(8,128)(2,1)S(1)}, u32[]{:S(2)}, u32[]{:S(2)}) collective-permute-start(bf16[10,8,2048]{2,1,0:T(8,128)(2,1)S(1)} %get-tuple-element.19), channel_id=1, source_target_pairs={{0,1},{1,2},{2,3},{3,4},{4,5},{5,6},{6,7},{8,9},{9,10},{10,11},{11... | collective-permute-start | bytes 983048 | tf_op jit(solution)/shard_map/ppermute | solution.py:555
  14.9 17.5 %collective-permute-start.3 = (bf16[10,8,2048]{2,1,0:T(8,128)(2,1)S(1)}, bf16[10,8,2048]{2,1,0:T(8,128)(2,1)S(1)}, u32[]{:S(2)}, u32[]{:S(2)}) collective-permute-start(bf16[10,8,2048]{2,1,0:T(8,128)(2,1)S(1)} %get-tuple-element.20), channel_id=1, source_target_pairs={{1,0},{2,1},{3,2},{4,3},{5,4},{6,5},{7,6},{9,8},{10,9},{11,10},{12... | collective-permute-start | bytes 983048 | tf_op jit(solution)/shard_map/ppermute | solution.py:556
  45.0 4.1 %collective-permute-start.4 = (bf16[40,256]{1,0:T(8,128)(2,1)S(1)}, bf16[40,256]{1,0:T(8,128)(2,1)S(1)}, u32[]{:S(2)}, u32[]{:S(2)}) collective-permute-start(bf16[40,256]{1,0:T(8,128)(2,1)S(1)} %make_coeffs.1.own_ref), channel_id=1, source_target_pairs={{0,8},{8,0},{16,24},{24,16},{1,9},{9,1},{17,25},{25,17},{2,10},{10... | collective-permute-start | bytes 61448 | tf_op jit(solution)/shard_map/ppermute | solution.py:536
  45.1 4.1 %collective-permute-start.5 = (bf16[40,256]{1,0:T(8,128)(2,1)S(1)}, bf16[40,256]{1,0:T(8,128)(2,1)S(1)}, u32[]{:S(2)}, u32[]{:S(2)}) collective-permute-start(bf16[40,256]{1,0:T(8,128)(2,1)S(1)} %make_coeffs.1.own_ref), channel_id=1, source_target_pairs={{0,16},{8,24},{16,0},{24,8},{1,17},{9,25},{17,1},{25,9},{2,18},{10... | collective-permute-start | bytes 61448 | tf_op jit(solution)/shard_map/ppermute | solution.py:536
  46.6 3.2 %collective-permute-start.6 = (bf16[40,256]{1,0:T(8,128)(2,1)S(1)}, bf16[40,256]{1,0:T(8,128)(2,1)S(1)}, u32[]{:S(2)}, u32[]{:S(2)}) collective-permute-start(bf16[40,256]{1,0:T(8,128)(2,1)S(1)} %make_coeffs.1.own_ref), channel_id=1, source_target_pairs={{0,24},{8,16},{16,8},{24,0},{1,25},{9,17},{17,9},{25,1},{2,26},{10... | collective-permute-start | bytes 61448 | tf_op jit(solution)/shard_map/ppermute | solution.py:536
  51.9 1.9 %copy-start = (bf16[2048,1024]{1,0:T(8,128)(2,1)}, bf16[2048,1024]{1,0:T(8,128)(2,1)S(1)}, u32[]{:S(2)}) copy-start(bf16[2048,1024]{1,0:T(8,128)(2,1)S(1)} %shard_map.73.cols_ref) | copy-start | bytes 12582916
  53.9 1.3 %collective-permute-start.7 = (f32[16,2048]{1,0:T(8,128)S(1)}, f32[16,2048]{1,0:T(8,128)S(1)}, u32[]{:S(2)}, u32[]{:S(2)}) collective-permute-start(f32[16,2048]{1,0:T(8,128)S(1)} %get-tuple-element.26), channel_id=1, source_target_pairs={{0,8},{8,0},{16,24},{24,16},{1,9},{9,1},{17,25},{25,17},{2,10},{10... | collective-permute-start | bytes 393224 | tf_op jit(solution)/shard_map/ppermute | solution.py:536
  55.3 5.0 %collective-permute-start.8 = (f32[8,2048]{1,0:T(8,128)S(1)}, f32[8,2048]{1,0:T(8,128)S(1)}, u32[]{:S(2)}, u32[]{:S(2)}) collective-permute-start(f32[8,2048]{1,0:T(8,128)S(1)} %get-tuple-element.27), channel_id=1, source_target_pairs={{0,16},{8,24},{16,0},{24,8},{1,17},{9,25},{17,1},{25,9},{2,18},{10... | collective-permute-start | bytes 196616 | tf_op jit(solution)/shard_map/ppermute | solution.py:536
  56.2 14.7 %collective-permute-start = (bf16[256,256]{1,0:T(8,128)(2,1)S(1)}, bf16[256,256]{1,0:T(8,128)(2,1)S(1)}, u32[]{:S(2)}, u32[]{:S(2)}) collective-permute-start(bf16[256,256]{1,0:T(8,128)(2,1)S(1)} %bitcast.11), channel_id=1, source_target_pairs={{0,16},{8,24},{16,0},{24,8},{1,17},{9,25},{17,1},{25,9},{2,18},{10... | collective-permute-start | bytes 393224 | tf_op jit(solution)/shard_map/ppermute | solution.py:536
  60.3 2.2 %copy-start.1 = (bf16[2048,1024]{1,0:T(8,128)(2,1)S(1)}, bf16[2048,1024]{1,0:T(8,128)(2,1)}, u32[]{:S(2)}) copy-start(bf16[2048,1024]{1,0:T(8,128)(2,1)} %copy-done) | copy-start | bytes 12582916
  63.9 17.5 %all-to-all-start.1 = ((bf16[32,8,512]{2,1,0:T(8,128)(2,1)}), bf16[32,8,512]{2,1,0:T(8,128)(2,1)S(1)}, u32[]{:S(2)}, u32[]{:S(2)}) async-start(bf16[32,8,512]{2,1,0:T(8,128)(2,1)} %bitcast.8), calls=%async_computation.1 | async-start | bytes 524288 | tf_op jit(solution)/shard_map/all_to_all | solution.py:574
  71.0 1.6 %collective-permute-start.1 = (bf16[2,256,256]{2,1,0:T(8,128)(2,1)S(1)}, bf16[2,256,256]{2,1,0:T(8,128)(2,1)S(1)}, u32[]{:S(2)}, u32[]{:S(2)}) collective-permute-start(bf16[2,256,256]{2,1,0:T(8,128)(2,1)S(1)} %pad_maximum_fusion), channel_id=1, source_target_pairs={{0,8},{8,0},{16,24},{24,16},{1,9},{9,1},{17,25},{25,17},{2,10},{10... | collective-permute-start | bytes 786440 | tf_op jit(solution)/shard_map/ppermute | solution.py:536
  81.9 1.6 %collective-permute-start.9 = (f32[136,512]{1,0:T(8,128)S(1)}, f32[136,512]{1,0:T(8,128)S(1)}, u32[]{:S(2)}, u32[]{:S(2)}) collective-permute-start(f32[136,512]{1,0:T(8,128)S(1)} %gradient.1.own_ref), channel_id=1, source_target_pairs={{0,8},{8,0},{16,24},{24,16},{1,9},{9,1},{17,25},{25,17},{2,10},{10... | collective-permute-start | bytes 835592 | tf_op jit(solution)/shard_map/ppermute | solution.py:536

commit v2 on v1

--- a/solution.py
+++ b/solution.py
@@ -65,18 +65,14 @@
     return shift_rows(field, 1) - shift_rows(field, -1)
 
 
-def pack(index_ref, member_ref, states_ref, targets_ref, sea_ref, basis_ref, control_ref, up_ref, down_ref, out_ref, last, first, seen, sea, basis, own, sems):
+def fetch(source, target, sem):
+    copy = pltpu.make_async_copy(source, target, sem)
+    copy.start()
+    return copy
+
+
+def pack_edges(index_ref, states_ref, targets_ref, sea_ref, up_ref, down_ref, last, first, seen, sea, sems):
     count, _, _, rows, cols = states_ref.shape
-    width = basis_ref.shape[1]
-    rows_out = control_ref.shape[0]
-    quarter = out_ref.shape[2]
-    at = pl.multiple_of(member_ref[0] * quarter, quarter)
-
-    def fetch(source, target, sem):
-        copy = pltpu.make_async_copy(source, target, sem)
-        copy.start()
-        return copy
-
     states = []
     for s in range(count):
         slot = index_ref[s]
@@ -88,21 +84,24 @@
         fetch(targets_ref.at[:, pl.ds(0, TILE), :], seen.at[1], sems.at[1, count]),
         fetch(sea_ref.at[pl.ds(rows - TILE, TILE), :], sea.at[0], sems.at[0, count + 1]),
         fetch(sea_ref.at[pl.ds(0, TILE), :], sea.at[1], sems.at[1, count + 1]),
-        fetch(basis_ref, basis, sems.at[0, count + 2]),
-        fetch(control_ref.at[:, pl.ds(at, quarter)], own, sems.at[1, count + 2]),
     ]
     row = tile_rows((TILE, cols))
     for s in range(count):
         states[2 * s].wait()
         height, east, north = (last[s, f].astype(F32) for f in range(3))
-        up_ref[s] = jnp.where(
-            row >= 5, height, jnp.where(row >= 2, pltpu.roll(north, 5, 0), pltpu.roll(east, 2, 0))
-        ).astype(BF16)
+        height, east, north = (
+            pltpu.roll(height, 4, 0), pltpu.roll(east, 1, 0), pltpu.roll(north, 7, 0)
+        )
+        low = (row >= 1) & (row < 4)
+        middle = (row >= 4) & (row < 7)
+        up_ref[s] = jnp.where(low, height, jnp.where(middle, north, east)).astype(BF16)
         states[2 * s + 1].wait()
         height, east, north = (first[s, f].astype(F32) for f in range(3))
-        down_ref[s] = jnp.where(
-            row < 3, height, jnp.where(row < 6, pltpu.roll(north, 3, 0), pltpu.roll(east, 6, 0))
-        ).astype(BF16)
+        height, east, north = (
+            pltpu.roll(height, 4, 0), pltpu.roll(east, 2, 0), pltpu.roll(north, 7, 0)
+        )
+        high = (row >= 2) & (row < 4)
+        down_ref[s] = jnp.where(middle, height, jnp.where(high, east, north)).astype(BF16)
     for copy in others:
         copy.wait()
     targets_up = jnp.zeros((TILE, cols), F32)
@@ -112,51 +111,80 @@
         targets_down = jnp.where(row == s, seen[1, s].astype(F32)[:1, :], targets_down)
     up_ref[count] = targets_up.astype(BF16)
     down_ref[count] = targets_down.astype(BF16)
-    basis_last = pltpu.roll(basis[rows - TILE :, :].astype(F32), 4, 0)
-    basis_first = pltpu.roll(basis[:TILE, :].astype(F32), 2, 0)
-    rest = jnp.zeros((TILE, cols - width), F32)
-    up_ref[count + 1] = jnp.where(
-        row >= 6, sea[0].astype(F32), jnp.concatenate([basis_last, rest], axis=1)
-    ).astype(BF16)
-    down_ref[count + 1] = jnp.where(
-        row < 2, sea[1].astype(F32), jnp.concatenate([basis_first, rest], axis=1)
-    ).astype(BF16)
-    part = own[...].astype(BF16)
-    part_basis = basis[:, pl.ds(at, quarter)]
-    for k in range(out_ref.shape[0]):
-        out_ref[k, :rows_out] = part
-        out_ref[k, rows_out:] = part_basis
-
-
-def packed(section_index, member, checkpoints, targets, sea_mask, basis_rows, control, slabs, quarter):
-    count, _, fields, rows, cols = checkpoints.shape
-    rows_out, width = control.shape
+    up_ref[count + 1] = pltpu.roll(sea[0].astype(F32), 4, 0).astype(BF16)
+    down_ref[count + 1] = pltpu.roll(sea[1].astype(F32), 4, 0).astype(BF16)
+
+
+def edge_messages(section_index, checkpoints, targets, sea_mask):
+    count, _, fields, _, cols = checkpoints.shape
     edges = jax.ShapeDtypeStruct((count + 2, TILE, cols), BF16)
     return pl.pallas_call(
-        pack,
-        name="pack",
-        out_shape=(
-            edges,
-            edges,
-            jax.ShapeDtypeStruct((slabs, rows_out + rows, quarter), BF16),
-        ),
-        in_specs=[SMEM, SMEM] + [HBM] * 5,
-        out_specs=(VMEM, VMEM, VMEM),
+        pack_edges,
+        name="pack_edges",
+        out_shape=(edges, edges),
+        in_specs=[SMEM] + [HBM] * 3,
+        out_specs=(VMEM, VMEM),
         scratch_shapes=[
             pltpu.VMEM((count, fields, TILE, cols), BF16),
             pltpu.VMEM((count, fields, TILE, cols), BF16),
             pltpu.VMEM((2, count, TILE, cols), BF16),
             pltpu.VMEM((2, TILE, cols), jnp.int32),
+            pltpu.SemaphoreType.DMA((2, count + 2)),
+        ],
+        compiler_params=limit(12),
+    )(*map(in_hbm, (section_index, checkpoints, targets, sea_mask)))
+
+
+def pack_pieces(member_ref, basis_ref, control_ref, out_ref, basis, own, sems):
+    rows, width = basis_ref.shape
+    rows_out = control_ref.shape[0]
+    slabs, _, quarter = out_ref.shape
+    at = pl.multiple_of(member_ref[0] * quarter, quarter)
+    copies = [
+        fetch(control_ref.at[:, pl.ds(at, quarter)], own, sems.at[0]),
+        fetch(basis_ref, basis, sems.at[1]),
+    ]
+    for copy in copies:
+        copy.wait()
+    part = own[...].astype(BF16)
+    part_basis = basis[:, pl.ds(at, quarter)]
+    row = tile_rows((TILE, width))
+    first = basis[:TILE, :].astype(F32)
+    last = pltpu.roll(basis[rows - TILE :, :].astype(F32), 4, 0)
+    both = jnp.where(row < 2, first, last)
+    tiles = []
+    for q in range(0, width // quarter, 2):
+        here = both[:, q * quarter : (q + 1) * quarter]
+        below = pltpu.roll(both[:, (q + 1) * quarter : (q + 2) * quarter], 4, 0)
+        tiles.append(jnp.where(row[:, :quarter] < 4, here, below))
+    edges = jnp.concatenate(tiles, axis=0).astype(BF16)
+    for k in range(slabs):
+        out_ref[k, :rows_out] = part
+        out_ref[k, rows_out : rows_out + rows] = part_basis
+        out_ref[k, rows_out + rows :] = edges
+
+
+def pieces_for(member, basis_rows, control, slabs, quarter):
+    rows, width = basis_rows.shape
+    rows_out = control.shape[0]
+    edges = 4 * width // quarter
+    return pl.pallas_call(
+        pack_pieces,
+        name="pack_pieces",
+        out_shape=jax.ShapeDtypeStruct((slabs, rows_out + rows + edges, quarter), BF16),
+        in_specs=[SMEM, HBM, HBM],
+        out_specs=VMEM,
+        scratch_shapes=[
             pltpu.VMEM((rows, width), BF16),
             pltpu.VMEM((rows_out, quarter), F32),
-            pltpu.SemaphoreType.DMA((2, count + 3)),
+            pltpu.SemaphoreType.DMA((2,)),
         ],
-        compiler_params=limit(14),
-    )(
-        in_hbm(section_index),
-        member.reshape(1),
-        *map(in_hbm, (checkpoints, targets, sea_mask, basis_rows, control)),
-    )
+        compiler_params=limit(10),
+    )(member.reshape(1), in_hbm(basis_rows), in_hbm(control))
+
+
+def in_hbm(array):
+    return pltpu.with_memory_space_constraint(array, pltpu.HBM)
 
 
 def hold(source_ref, out_ref, sem):
@@ -165,14 +193,11 @@
     copy.wait()
 
 
-def in_hbm(array):
-    return pltpu.with_memory_space_constraint(array, pltpu.HBM)
-
-
 def held(array):
     size = array.size * array.dtype.itemsize
     return pl.pallas_call(
         hold,
+        name="hold",
         out_shape=jax.ShapeDtypeStruct(array.shape, array.dtype),
         in_specs=[HBM],
         out_specs=VMEM,
@@ -181,62 +206,32 @@
     )(in_hbm(array))
 
 
-def run_states(index_ref, state_ref, before_ref, after_ref, shared_before_ref, shared_after_ref, targets_ref, sea_ref, basis_ref, base_ref, pairs_ref, mask_ref, rows_ref, mask, seen_edge, heights, fluxes, mid_fluxes, weights, besides, misfits, partial, gx, gy):
-    s = pl.program_id(0)
-    rows, cols = sea_ref.shape
-    width = basis_ref.shape[1]
-    tiles = rows // TILE + 1
-    row = tile_rows((TILE, cols))
-    top = row < 4
-
-    def put(ref, tile, value):
-        ref[:, TILE * (tile + 1) : TILE * (tile + 2), :] = value
-        if tile == tiles - 1:
-            ref[:, :TILE, :] = value
-        if tile == 0:
-            ref[:, TILE * (tiles + 1) :, :] = value
-
-    def get(ref, tile, step=0):
+PAIRS = 5
+
+
+class Rows:
+    def __init__(self, ref):
+        self.ref = ref
+
+    def put(self, tile, value):
+        self.ref[:, TILE * (tile + 1) : TILE * (tile + 2), :] = value
+
+    def get(self, tile, step=0):
         start = TILE * (tile + 1) + step
-        return ref[:, start : start + TILE, :]
-
-    def rows_of(tile):
-        return slice(TILE * tile, TILE * (tile + 1))
-
-    @pl.when(s == 0)
-    def _():
-        after = shared_after_ref[1].astype(F32)
-        before = shared_before_ref[1].astype(F32)
-        edge = jnp.where(row < 2, after, jnp.where(row >= 6, before, 0.0))
-        for tile in range(tiles - 1):
-            mask[:, rows_of(tile), :] = split_lanes(sea_ref[rows_of(tile), :].astype(F32))
-        mask[:, rows:, :] = split_lanes(edge)
-        mask_ref[...] = mask[...].astype(BF16)
-        seen_edge[0] = shared_before_ref[0].astype(F32)
-        seen_edge[1] = shared_after_ref[0].astype(F32)
-        gx[...] = jnp.zeros_like(gx)
-        gy[...] = jnp.zeros_like(gy)
-        pairs_ref[...] = jnp.zeros_like(pairs_ref)
-        after = pltpu.roll(after[:, :width], 6, 0)
-        before = pltpu.roll(before[:, :width], 4, 0)
-        edge = jnp.where(row[:, :width] < 2, after, jnp.where(row[:, :width] >= 6, before, 0.0))
-        rows_ref[...] = jnp.concatenate(
-            [basis_ref[...].astype(F32), edge], axis=0
-        ).astype(BF16)
-
-    after = after_ref[0].astype(F32)
-    before = before_ref[0].astype(F32)
-    edges = (
-        jnp.where(top, after, before),
-        jnp.where(top, pltpu.roll(after, 2, 0), pltpu.roll(before, 6, 0)),
-        jnp.where(top, pltpu.roll(after, 5, 0), pltpu.roll(before, 3, 0)),
-    )
-
-    def load(field, tile):
-        if tile == tiles - 1:
-            return split_lanes(edges[field])
-        return split_lanes(state_ref[0, 0, field, rows_of(tile), :].astype(F32))
-
+        return self.ref[:, start : start + TILE, :]
+
+
+def rows_of(tile):
+    return slice(TILE * tile, TILE * (tile + 1))
+
+
+def clear(*refs):
+    for ref in refs:
+        ref[...] = jnp.zeros_like(ref)
+
+
+def add_state(tiles, load, seen, mask, live, padded, partial, gx, gy, pairs_ref):
+    heights, fluxes, mid_fluxes, weights, besides, misfits = (Rows(ref) for ref in padded)
     half = 0.5 * TIME_STEP
     keep = 1.0 - TIME_STEP * FRICTION
     turn = TIME_STEP * CORIOLIS / keep
@@ -244,86 +239,85 @@
 
     for tile in range(tiles):
         height = load(0, tile)
-        put(heights, tile, height)
-        put(fluxes, tile, (DEPTH + height) * load(2, tile))
+        heights.put(tile, height)
+        fluxes.put(tile, (DEPTH + height) * load(2, tile))
 
     for tile in range(tiles):
-        height = get(heights, tile)
+        height = heights.get(tile)
         east = load(1, tile)
         north = load(2, tile)
-        flux = dx((DEPTH + height) * east) + (get(fluxes, tile, 1) - get(fluxes, tile, -1))
+        flux = dx((DEPTH + height) * east) + (fluxes.get(tile, 1) - fluxes.get(tile, -1))
         sea = mask[:, rows_of(tile), :]
         height_mid = sea * (height - half * flux)
         weight = DEPTH * sea + height_mid
         east_mid = east + turn * north - slope * dx(height)
-        north_mid = (
-            north - turn * east - slope * (get(heights, tile, 1) - get(heights, tile, -1))
+        north_mid = north - turn * east - slope * (heights.get(tile, 1) - heights.get(tile, -1))
+        mid_fluxes.put(tile, weight * north_mid)
+        weights.put(tile, weight)
+        besides.put(tile, shift_cols(weight, 1))
+        partial[:, rows_of(tile), :] = (
+            height + height_mid - 2.0 * seen(tile) - half * keep * dx(weight * east_mid)
         )
-        if tile == tiles - 1:
-            seen = split_lanes(
-                jnp.where(top, seen_edge[1, pl.ds(s, 1), :], seen_edge[0, pl.ds(s, 1), :])
-            )
-        else:
-            seen = split_lanes(targets_ref[0, rows_of(tile), :].astype(F32))
-        put(mid_fluxes, tile, weight * north_mid)
-        put(weights, tile, weight)
-        put(besides, tile, shift_cols(weight, 1))
-        partial[:, rows_of(tile), :] = (
-            height + height_mid - 2.0 * seen - half * keep * dx(weight * east_mid)
-        )
 
     for tile in range(tiles):
-        change = get(mid_fluxes, tile, 1) - get(mid_fluxes, tile, -1)
-        misfit = mask[:, rows_of(tile), :] * (
-            partial[:, rows_of(tile), :] - half * keep * change
-        )
-        put(misfits, tile, misfit)
-        gx[:, rows_of(tile), :] += get(weights, tile) * dx(misfit)
+        change = mid_fluxes.get(tile, 1) - mid_fluxes.get(tile, -1)
+        misfit = live[:, rows_of(tile), :] * (partial[:, rows_of(tile), :] - half * keep * change)
+        misfits.put(tile, misfit)
+        gx[:, rows_of(tile), :] += weights.get(tile) * dx(misfit)
 
     for tile in range(tiles):
         here = rows_of(tile)
-        weight = get(weights, tile)
-        gy[:, here, :] += weight * (get(misfits, tile, 1) - get(misfits, tile, -1))
+        weight = weights.get(tile)
+        gy[:, here, :] += weight * (misfits.get(tile, 1) - misfits.get(tile, -1))
         pairs_ref[0, :, here, :] += weight * weight
         pairs_ref[1, :, here, :] += weight * shift_cols(weight, 2)
-        pairs_ref[2, :, here, :] += weight * get(weights, tile, 2)
-        pairs_ref[3, :, here, :] += weight * get(besides, tile, 1)
-        pairs_ref[4, :, here, :] += weight * get(besides, tile, -1)
-
-    @pl.when(s == pl.num_programs(0) - 1)
+        pairs_ref[2, :, here, :] += weight * weights.get(tile, 2)
+        pairs_ref[3, :, here, :] += weight * besides.get(tile, 1)
+        pairs_ref[4, :, here, :] += weight * besides.get(tile, -1)
+
+
+def inner_states(index_ref, state_ref, targets_ref, sea_ref, basis_ref, gx_ref, gy_ref, pairs_ref, rows_ref, mask, live, partial, *padded):
+    rows = sea_ref.shape[0]
+    tiles = rows // TILE
+
+    @pl.when(pl.program_id(0) == 0)
     def _():
-        scale = 0.0625 * TIME_STEP * TIME_STEP
-        base_ref[...] = scale * (dy(gx[...]) - dx(gy[...]))
-
-
-def states_pass(section_index, checkpoints, before, after, targets, sea_mask, basis_rows):
+        clear(gx_ref, gy_ref, pairs_ref, *padded)
+        rows_ref[...] = basis_ref[...]
+        for tile in range(tiles):
+            mask[:, rows_of(tile), :] = split_lanes(sea_ref[rows_of(tile), :].astype(F32))
+        row = lax.broadcasted_iota(jnp.int32, live.shape, 1)
+        live[...] = jnp.where((row >= 2) & (row < rows - 2), mask[...], 0.0)
+
+    add_state(
+        tiles,
+        lambda field, tile: split_lanes(state_ref[0, 0, field, rows_of(tile), :].astype(F32)),
+        lambda tile: split_lanes(targets_ref[0, rows_of(tile), :].astype(F32)),
+        mask, live, padded, partial, gx_ref, gy_ref, pairs_ref,
+    )
+
+
+def inner_pass(section_index, checkpoints, targets, sea_mask, basis_rows):
     count, _, fields, rows, cols = checkpoints.shape
     width = basis_rows.shape[1]
-    ring = rows + TILE
     lanes = cols // LANES
-    padded = pltpu.VMEM((lanes, ring + 2 * TILE, LANES), F32)
-    plain = pltpu.VMEM((lanes, ring, LANES), F32)
-    edge = pl.BlockSpec((1, TILE, cols), lambda s, index: (s, 0, 0))
-    shared = pl.BlockSpec((2, TILE, cols), lambda s, index: (count // 2, 0, 0))
+    padded = pltpu.VMEM((lanes, rows + 2 * TILE, LANES), F32)
+    plain = pltpu.VMEM((lanes, rows, LANES), F32)
     outs = (
-        jax.ShapeDtypeStruct((lanes, ring, LANES), F32),
-        jax.ShapeDtypeStruct((5, lanes, ring, LANES), F32),
-        jax.ShapeDtypeStruct((lanes, ring, LANES), BF16),
-        jax.ShapeDtypeStruct((ring, width), BF16),
-    )
-    return pl.pallas_call(
-        run_states,
-        name="run_states",
+        jax.ShapeDtypeStruct((lanes, rows, LANES), F32),
+        jax.ShapeDtypeStruct((lanes, rows, LANES), F32),
+        jax.ShapeDtypeStruct((PAIRS, lanes, rows, LANES), F32),
+        jax.ShapeDtypeStruct((rows, width), BF16),
+    )
+    return pl.pallas_call(
+        inner_states,
+        name="inner_states",
         out_shape=outs,
         grid_spec=pltpu.PrefetchScalarGridSpec(
             num_scalar_prefetch=1,
             grid=(count,),
             in_specs=[
                 pl.BlockSpec((1, 1, fields, rows, cols), lambda s, index: (s, index[s], 0, 0, 0)),
-                edge,
-                edge,
-                shared,
-                shared,
                 pl.BlockSpec((1, rows, cols), lambda s, index: (s, 0, 0)),
                 pl.BlockSpec((rows, cols), lambda s, index: (0, 0)),
                 pl.BlockSpec((rows, width), lambda s, index: (0, 0)),
@@ -331,40 +325,198 @@
             out_specs=tuple(
                 pl.BlockSpec(out.shape, lambda s, index, n=len(out.shape): (0,) * n) for out in outs
             ),
-            scratch_shapes=[plain, pltpu.VMEM((2, TILE, cols), F32)]
-            + [padded] * 6
-            + [plain] * 3,
+            scratch_shapes=[plain] * 3 + [padded] * 6,
+        ),
+        compiler_params=limit(18),
+    )(*map(in_hbm, (section_index, checkpoints, targets, sea_mask, basis_rows)))
+
+
+def seam_states(index_ref, last_ref, first_ref, before_ref, after_ref, shared_before_ref, shared_after_ref, seen_last_ref, seen_first_ref, sea_ref, gx_in_ref, gy_in_ref, pairs_in_ref, base_ref, pairs_ref, mask_ref, seen_edge, mask, live, partial, gx, gy, pairs, ring_x, ring_y, *padded):
+    s = pl.program_id(0)
+    rows, cols = sea_ref.shape
+    row = tile_rows((TILE, cols))
+    top = row < 4
+
+    def seam(ends, beyond_after, beyond_before):
+        own_last, own_first = (pltpu.roll(end, 4, 0) for end in ends)
+        return (
+            split_lanes(jnp.where(top, own_last, beyond_after)),
+            split_lanes(jnp.where(top, beyond_before, own_first)),
+        )
+
+    @pl.when(s == 0)
+    def _():
+        clear(gx, gy, pairs, *padded)
+        seen_edge[0] = shared_before_ref[0].astype(F32)
+        seen_edge[1] = shared_after_ref[0].astype(F32)
+        after = jnp.where(row < 6, shared_after_ref[1].astype(F32), 0.0)
+        before = jnp.where(row >= 2, shared_before_ref[1].astype(F32), 0.0)
+        ends = (sea_ref[rows - TILE :, :].astype(F32), sea_ref[:TILE, :].astype(F32))
+        for tile, value in enumerate(seam(ends, after, before)):
+            mask[:, rows_of(tile), :] = value
+        for tile in range(rows // TILE):
+            mask_ref[:, rows_of(tile), :] = split_lanes(
+                sea_ref[rows_of(tile), :].astype(F32)
+            ).astype(BF16)
+        beyond = jnp.where(top, pltpu.roll(after, 4, 0), pltpu.roll(before, 4, 0))
+        mask_ref[:, rows:, :] = split_lanes(beyond).astype(BF16)
+        place = lax.broadcasted_iota(jnp.int32, live.shape, 1)
+        counts = ((place >= 2) & (place < 5)) | ((place >= 11) & (place < 14))
+        live[...] = jnp.where(counts, mask[...], 0.0)
+
+    after = after_ref[0].astype(F32)
+    before = before_ref[0].astype(F32)
+    turned = ((0, 0), (2, 3), (5, 5))
+    fields = []
+    for field, (forward, back) in enumerate(turned):
+        ends = (last_ref[0, 0, field].astype(F32), first_ref[0, 0, field].astype(F32))
+        fields.append(
+            seam(
+                ends,
+                pltpu.roll(after, forward, 0) if forward else after,
+                pltpu.roll(before, back, 0) if back else before,
+            )
+        )
+    ends = (seen_last_ref[0].astype(F32), seen_first_ref[0].astype(F32))
+    seen = seam(ends, seen_edge[1, pl.ds(s, 1), :], seen_edge[0, pl.ds(s, 1), :])
+    add_state(
+        2,
+        lambda field, tile: fields[field][tile],
+        lambda tile: seen[tile],
+        mask, live, padded, partial, gx, gy, pairs,
+    )
+
+    @pl.when(s == pl.num_programs(0) - 1)
+    def _():
+        place = lax.broadcasted_iota(jnp.int32, (gx.shape[0], TILE, LANES), 1)
+        top = place < 4
+        final = rows // TILE - 1
+
+        def ring(inner, outer, out, low):
+            ending = pltpu.roll(outer[:, :TILE, :], 4, 1)
+            opening = pltpu.roll(outer[:, TILE:, :], 4, 1)
+            for tile in range(1, final):
+                out[:, rows_of(tile), :] = inner[:, rows_of(tile), :]
+            head = inner[:, :TILE, :]
+            tail = inner[:, rows_of(final), :]
+            if low is None:
+                head = head + jnp.where(top, opening, 0.0)
+                tail = tail + jnp.where(top, 0.0, ending)
+            else:
+                head = jnp.where(place < low, opening, head)
+                tail = jnp.where(place > 4, ending, tail)
+            out[:, :TILE, :] = head
+            out[:, rows_of(final), :] = tail
+            out[:, rows:, :] = jnp.where(top, ending, opening)
+
+        ring(gx_in_ref[...], gx[...], ring_x, None)
+        ring(gy_in_ref[...], gy[...], ring_y, None)
+        for k in range(PAIRS):
+            ring(pairs_in_ref[k], pairs[k], pairs_ref.at[k], 2 if k == 4 else 1)
+        scale = 0.0625 * TIME_STEP * TIME_STEP
+        base_ref[...] = scale * (dy(ring_x[...]) - dx(ring_y[...]))
+
+
+def seam_pass(section_index, checkpoints, before, after, targets, sea_mask, gx, gy, pairs):
+    count, _, fields, rows, cols = checkpoints.shape
+    lanes = cols // LANES
+    final = rows // TILE - 1
+    ring = rows + TILE
+    plain = pltpu.VMEM((lanes, 2 * TILE, LANES), F32)
+    padded = pltpu.VMEM((lanes, 4 * TILE, LANES), F32)
+    whole = pltpu.VMEM((lanes, ring, LANES), F32)
+    state = (1, 1, fields, TILE, cols)
+    edge = pl.BlockSpec((1, TILE, cols), lambda s, index: (s, 0, 0))
+    shared = pl.BlockSpec((2, TILE, cols), lambda s, index: (count // 2, 0, 0))
+
+    def fixed(array):
+        return pl.BlockSpec(array.shape, lambda s, index, n=len(array.shape): (0,) * n)
+
+    outs = (
+        jax.ShapeDtypeStruct((lanes, ring, LANES), F32),
+        jax.ShapeDtypeStruct((PAIRS, lanes, ring, LANES), F32),
+        jax.ShapeDtypeStruct((lanes, ring, LANES), BF16),
+    )
+    return pl.pallas_call(
+        seam_states,
+        name="seam_states",
+        out_shape=outs,
+        grid_spec=pltpu.PrefetchScalarGridSpec(
+            num_scalar_prefetch=1,
+            grid=(count,),
+            in_specs=[
+                pl.BlockSpec(state, lambda s, index: (s, index[s], 0, final, 0)),
+                pl.BlockSpec(state, lambda s, index: (s, index[s], 0, 0, 0)),
+                edge,
+                edge,
+                shared,
+                shared,
+                pl.BlockSpec((1, TILE, cols), lambda s, index: (s, final, 0)),
+                pl.BlockSpec((1, TILE, cols), lambda s, index: (s, 0, 0)),
+                fixed(sea_mask),
+                fixed(gx),
+                fixed(gy),
+                fixed(pairs),
+            ],
+            out_specs=tuple(fixed(out) for out in outs),
+            scratch_shapes=[pltpu.VMEM((2, TILE, cols), F32)]
+            + [plain] * 5
+            + [pltpu.VMEM((PAIRS, lanes, 2 * TILE, LANES), F32)]
+            + [whole] * 2
+            + [padded] * 6,
         ),
         compiler_params=limit(20),
     )(
-        section_index,
+        in_hbm(section_index),
+        in_hbm(checkpoints),
         in_hbm(checkpoints),
         before,
         after,
         before,
         after,
         in_hbm(targets),
+        in_hbm(targets),
         in_hbm(sea_mask),
-        in_hbm(basis_rows),
-    )
-
-
-def make_coeffs(basis_ref, pieces_ref, out_ref):
+        gx,
+        gy,
+        pairs,
+    )
+
+
+def make_coeffs(slab_ref, basis_ref, pieces_ref, out_ref):
     slabs, _, quarter = pieces_ref.shape
-    width = basis_ref.shape[1]
-    part = pieces_ref[:, : width // slabs, :].reshape(width, quarter)
-    out_ref[...] = jnp.dot(basis_ref[...], part, preferred_element_type=F32).astype(BF16)
-
-
-def coeffs_part(basis, pieces):
+    rows, width = basis_ref.shape
+    rows_out = width // slabs
+    slab = slab_ref[0]
+
+    def edge_of(k):
+        parts = []
+        for q in range(width // quarter):
+            start = rows_out + rows + TILE * (q // 2)
+            part = pieces_ref[k, start : start + TILE, :].astype(F32)
+            parts.append(pltpu.roll(part, 4, 0) if q % 2 else part)
+        return jnp.concatenate(parts, axis=1)
+
+    after = edge_of(jnp.minimum(slab + 1, slabs - 1))
+    before = pltpu.roll(edge_of(jnp.maximum(slab - 1, 0)), 4, 0)
+    row = tile_rows((TILE, width))
+    use_after = (row < 2) & (slab < slabs - 1)
+    use_before = (row >= 6) & (slab > 0)
+    edge = jnp.where(use_after, after, jnp.where(use_before, before, 0.0))
+    basis = jnp.concatenate([basis_ref[...].astype(F32), edge], axis=0).astype(BF16)
+    part = pieces_ref[:, :rows_out, :].reshape(width, quarter)
+    out_ref[...] = jnp.dot(basis, part, preferred_element_type=F32).astype(BF16)
+
+
+def coeffs_part(slab, basis_rows, pieces):
     return pl.pallas_call(
         make_coeffs,
         name="make_coeffs",
-        out_shape=jax.ShapeDtypeStruct((basis.shape[0], pieces.shape[2]), BF16),
-        in_specs=[VMEM, VMEM],
+        out_shape=jax.ShapeDtypeStruct((basis_rows.shape[0] + TILE, pieces.shape[2]), BF16),
+        in_specs=[SMEM, VMEM, VMEM],
         out_specs=VMEM,
         compiler_params=limit(12),
-    )(basis, pieces)
+    )(slab.reshape(1), basis_rows, pieces)
 
 
 def apply_potential(member_ref, own_ref, near_ref, far_ref, both_ref, cols_ref, base_ref, pairs_ref, mask_ref, keep_ref, give_ref, coeffs, total):
@@ -549,21 +701,20 @@
     half = width // 2
     single = rows // 4
 
-    up, down, pieces = packed(
-        section_index, member, checkpoints, targets, sea_mask, basis_rows, control, slabs, quarter
-    )
+    pieces = pieces_for(member, basis_rows, control, slabs, quarter)
+    pieces = lax.all_to_all(pieces, "space", 0, 0)
+    up, down = edge_messages(section_index, checkpoints, targets, sea_mask)
     before = lax.ppermute(up, "space", [(i, i + 1) for i in range(slabs - 1)])
     after = lax.ppermute(down, "space", [(i + 1, i) for i in range(slabs - 1)])
-    pieces = lax.all_to_all(pieces, "space", 0, 0)
-    base, pairs, mask, ext_rows = states_pass(
-        section_index, checkpoints, before, after, targets, sea_mask, basis_rows
-    )
-    own = coeffs_part(ext_rows, pieces)
+    gx, gy, pairs, near_rows = inner_pass(section_index, checkpoints, targets, sea_mask, basis_rows)
+    own = coeffs_part(slab, near_rows, pieces)
     parts = [own]
     for bits in (1, 2, 3):
         parts.append(partner(own, bits))
-    cols = held(basis_cols)
-    keep, give = gradient_halves(member, parts, cols, base, pairs, mask)
+    base, pairs, mask = seam_pass(
+        section_index, checkpoints, before, after, targets, sea_mask, gx, gy, pairs
+    )
+    keep, give = gradient_halves(member, parts, basis_cols, base, pairs, mask)
 
     keep = keep + partner(give, 1)
     own_rows = lax.dynamic_slice_in_dim(keep, chip * single, single, 0)
@@ -574,7 +725,7 @@
     got = lax.all_to_all(send.reshape(members * slabs, single, half), ("ens", "space"), 0, 0)
     projected_half = got.reshape(slabs * rows, half)
 
-    part = pieces[:, rows_out:, :].reshape(slabs, 2, members // 2, single, quarter)
+    part = pieces[:, rows_out : rows_out + rows, :].reshape(slabs, 2, members // 2, single, quarter)
     part = part.transpose(2, 1, 0, 3, 4).reshape(slabs * rows, quarter)
     far = partner(part, 2)
     near = partner(jnp.stack([part, far]), 1)

time: 85 us -> 73.9 us (0.87)
  waiting for transfers between devices: 31.5 us -> 13.9 us
  Pallas kernels: 24.4 us -> 33.4 us
  local copies, waits for them, and re-layouts: 4.17 us -> 0.04 us
  starting transfers between devices: 24.2 us -> 25.7 us
    ppermute x1, waiting for transfers between devices: 16.2 us -> 1 us  [on_device(): before = lax.ppermute(up, 'space', [(i, i + 1) for i in range(slabs - 1)])]
    pallas_call x3 -> x5, Pallas kernels: 18.1 us -> 27.1 us  [the longest x1 10.6 us: inner_pass(): pl.pallas_call(inner_states, name='inner_states', out_shape=outs, grid_sp...]
    unnamed x6 -> x2, local copies, waits for them, and re-layouts: 4.13 us -> 0.01 us
    ppermute x8, waiting for transfers between devices: 7.54 us -> 4.32 us  [partner(): return lax.ppermute(value, 'ens', [(i, i ^ bit) for i in range(count)])]
    all_to_all x1, starting transfers between devices: 7.08 us -> 8.59 us  [on_device(): lax.all_to_all(send.reshape(members * slabs, single, half), ('ens', 'spac...]
  transfers between devices with their start and end apart: 12 -> 12, of which waited for: 7 -> 7; matrix products, arithmetic and copies ran while one was open for 0% -> 0% of each run, Pallas kernels for 20% -> 38%
where the time goes in v2:
time: 73.9 us; the launch traced here: 73.2 us
  Pallas kernels  33.4 us (45%)
  starting transfers between devices  25.7 us (35%)
  waiting for transfers between devices  13.9 us (19%)
    pallas_call x1, Pallas kernels, inner_pass(): pl.pallas_call(inner_states, name='inner_states', out_shape=outs, grid_sp...  10.6 us
    pallas_call x1, Pallas kernels, seam_pass(): pl.pallas_call(seam_states, name='seam_states', out_shape=outs, grid_spec...  9.03 us
    all_to_all x1, starting transfers between devices, on_device(): lax.all_to_all(send.reshape(members * slabs, single, half), ('ens', 'spac...  8.59 us
    all_to_all x1, waiting for transfers between devices, on_device(): lax.all_to_all(send.reshape(members * slabs, single, half), ('ens', 'spac...  7.73 us
    all_to_all x1, starting transfers between devices, on_device(): pieces = lax.all_to_all(pieces, 'space', 0, 0)  7.32 us
    ppermute x8, starting transfers between devices, partner(): return lax.ppermute(value, 'ens', [(i, i ^ bit) for i in range(count)])  4.53 us
    ppermute x8, waiting for transfers between devices, partner(): return lax.ppermute(value, 'ens', [(i, i ^ bit) for i in range(count)])  4.32 us
    ppermute x1, starting transfers between devices, on_device(): before = lax.ppermute(up, 'space', [(i, i + 1) for i in range(slabs - 1)])  3.94 us
  transfers between devices with their start and end apart: 12, of which 7 were waited for; matrix products, arithmetic and copies ran while one was open for 0% of the time, Pallas kernels for 38%

profile of v2, /device:TPU:0, one launch (start us, length us, event | category | flops | bytes accessed | tf_op | source)
XLA Modules:
  0.0 73.2 jit_solution(6010697229683690992)
XLA Ops:
  0.0 1.9 %pack_pieces.1 = bf16[8,176,256]{2,1,0:T(8,128)(2,1)} custom-call(s32[1]{0:T(128)} %bitcast.1.member_ref, bf16[32,1024]{1,0:T(8,128)(2,1)} %basis_ref.3, f32[128,1024]{1,0:T(8,128)} %control_ref.3), custom_call_target="tpu_custom_call" | custom-call | tf_op jit(solution)/shard_map/pack_pieces/pallas_call | solution.py:171
  1.9 7.3 %all-to-all-start = ((bf16[8,176,256]{2,1,0:T(8,128)(2,1)}), bf16[8,176,256]{2,1,0:T(8,128)(2,1)S(1)}, u32[]{:S(2)}, u32[]{:S(2)}) async-start(bf16[8,176,256]{2,1,0:T(8,128)(2,1)} %pack_pieces.1), calls=%async_computation | async-start | bytes 1441792 | tf_op jit(solution)/shard_map/all_to_all | solution.py:705
  9.2 3.4 %pack_edges.1 = (bf16[10,8,2048]{2,1,0:T(8,128)(2,1)}, bf16[10,8,2048]{2,1,0:T(8,128)(2,1)}) custom-call(s32[8]{0:T(128)} %index_ref.5, bf16[8,2,3,32,2048]{4,3,2,1,0:T(8,128)(2,1)} %first_ref.1, bf16[8,32,2048]{2,1,0:T(8,128)(2,1)} %seen_first_ref.1, s32[32,2048]{1,0:T(8,128)} %sea_ref.5), custom_call_target="tpu_custom_call" | custom-call | tf_op jit(solution)/shard_map/pack_edges/pallas_call | solution.py:121
  12.6 3.9 %collective-permute-start.5 = (bf16[10,8,2048]{2,1,0:T(8,128)(2,1)}, bf16[10,8,2048]{2,1,0:T(8,128)(2,1)S(1)}, u32[]{:S(2)}, u32[]{:S(2)}) collective-permute-start(bf16[10,8,2048]{2,1,0:T(8,128)(2,1)} %get-tuple-element.21), channel_id=1, source_target_pairs={{0,1},{1,2},{2,3},{3,4},{4,5},{5,6},{6,7},{8,9},{9,10},{10,11},{11... | collective-permute-start | bytes 983048 | tf_op jit(solution)/shard_map/ppermute | solution.py:707
  16.6 1.3 %collective-permute-start.6 = (bf16[10,8,2048]{2,1,0:T(8,128)(2,1)}, bf16[10,8,2048]{2,1,0:T(8,128)(2,1)S(1)}, u32[]{:S(2)}, u32[]{:S(2)}) collective-permute-start(bf16[10,8,2048]{2,1,0:T(8,128)(2,1)} %get-tuple-element.22), channel_id=1, source_target_pairs={{1,0},{2,1},{3,2},{4,3},{5,4},{6,5},{7,6},{9,8},{10,9},{11,10},{12... | collective-permute-start | bytes 983048 | tf_op jit(solution)/shard_map/ppermute | solution.py:708
  17.9 10.6 %inner_states.1 = (f32[16,32,128]{2,1,0:T(8,128)S(1)}, f32[16,32,128]{2,1,0:T(8,128)S(1)}, f32[5,16,32,128]{3,2,1,0:T(8,128)S(1)}, bf16[32,1024]{1,0:T(8,128)(2,1)S(1)}) custom-call(s32[8]{0:T(128)} %index_ref.5, bf16[8,2,3,32,2048]{4,3,2,1,0:T(8,128)(2,1)} %first_ref.1, bf16[8,32,2048]{2,1,0:T(8,128)(2,1)} %seen_first_ref.1, s32[32,2048]{1,0:T(8,128)} %sea_ref.5, ...), custom_call_target="tpu_custom_call" | custom-call | tf_op jit(solution)/shard_map/inner_states/pallas_call | solution.py:312
  28.5 0.8 %all-to-all-done.pieces_ref = bf16[8,176,256]{2,1,0:T(8,128)(2,1)S(1)} async-done(((bf16[8,176,256]{2,1,0:T(8,128)(2,1)}), bf16[8,176,256]{2,1,0:T(8,128)(2,1)S(1)}, u32[]{:S(2)}, u32[]{:S(2)}) %all-to-all-start) | async-done | bytes 720928 | tf_op jit(solution)/shard_map/all_to_all | solution.py:705
  29.3 0.2 make_coeffs.1.own_ref
  29.5 0.1 collective-permute-start.2
  29.6 1.6 %collective-permute-start.3 = (bf16[40,256]{1,0:T(8,128)(2,1)S(1)}, bf16[40,256]{1,0:T(8,128)(2,1)S(1)}, u32[]{:S(2)}, u32[]{:S(2)}) collective-permute-start(bf16[40,256]{1,0:T(8,128)(2,1)S(1)} %make_coeffs.1.own_ref), channel_id=1, source_target_pairs={{0,16},{8,24},{16,0},{24,8},{1,17},{9,25},{17,1},{25,9},{2,18},{10... | collective-permute-start | bytes 61448 | tf_op jit(solution)/shard_map/ppermute | solution.py:688
  31.1 0.3 collective-permute-start.4
  31.4 1.0 %collective-permute-done.5.before_ref.shared_before_ref = bf16[10,8,2048]{2,1,0:T(8,128)(2,1)S(1)} collective-permute-done((bf16[10,8,2048]{2,1,0:T(8,128)(2,1)}, bf16[10,8,2048]{2,1,0:T(8,128)(2,1)S(1)}, u32[]{:S(2)}, u32[]{:S(2)}) %collective-permute-start.5) | collective-permute-done | bytes 327712 | tf_op jit(solution)/shard_map/ppermute | solution.py:707
  32.4 9.0 %seam_states.1 = (f32[16,40,128]{2,1,0:T(8,128)S(1)}, f32[5,16,40,128]{3,2,1,0:T(8,128)S(1)}, bf16[16,40,128]{2,1,0:T(8,128)(2,1)S(1)}) custom-call(s32[8]{0:T(128)} %index_ref.5, bf16[8,2,3,32,2048]{4,3,2,1,0:T(8,128)(2,1)} %first_ref.1, bf16[8,2,3,32,2048]{4,3,2,1,0:T(8,128)(2,1)} %first_ref.1, ...), custom_call_target="tpu_custom_call" | custom-call | tf_op jit(solution)/shard_map/seam_states/pallas_call | solution.py:440
  41.5 0.0 collective-permute-done.2.near_ref
  41.5 2.2 %apply_potential.1 = (f32[16,2048]{1,0:T(8,128)S(1)}, f32[16,2048]{1,0:T(8,128)S(1)}) custom-call(s32[1]{0:T(128)} %bitcast.1.member_ref, bf16[40,256]{1,0:T(8,128)(2,1)S(1)} %make_coeffs.1.own_ref, bf16[40,256]{1,0:T(8,128)(2,1)S(1)} %collective-permute-done.2.near_ref, bf16[40,256]{1,0:T(8,128)(2,1)S(1)} %collective-permute-done.3.far_ref, ...), custom_call_target="tpu_custom_call" | custom-call | tf_op jit(solution)/shard_map/apply_potential/pallas_call | solution.py:567
  43.7 0.1 collective-permute-start.7
  43.8 1.3 %collective-permute-done.7 = f32[16,2048]{1,0:T(8,128)S(1)} collective-permute-done((f32[16,2048]{1,0:T(8,128)S(1)}, f32[16,2048]{1,0:T(8,128)S(1)}, u32[]{:S(2)}, u32[]{:S(2)}) %collective-permute-start.7) | collective-permute-done | bytes 131104 | tf_op jit(solution)/shard_map/ppermute | solution.py:688
  45.1 1.6 %collective-permute-start.8 = (f32[8,2048]{1,0:T(8,128)S(1)}, f32[8,2048]{1,0:T(8,128)S(1)}, u32[]{:S(2)}, u32[]{:S(2)}) collective-permute-start(f32[8,2048]{1,0:T(8,128)S(1)} %get-tuple-element.31), channel_id=1, source_target_pairs={{0,16},{8,24},{16,0},{24,8},{1,17},{9,25},{17,1},{25,9},{2,18},{10... | collective-permute-start | bytes 196616 | tf_op jit(solution)/shard_map/ppermute | solution.py:688
  46.7 0.6 collective-permute-start
  47.3 2.2 %hold.1.cols_ref = bf16[2048,1024]{1,0:T(8,128)(2,1)S(1)} custom-call(bf16[2048,1024]{1,0:T(8,128)(2,1)} %source_ref.1), custom_call_target="tpu_custom_call" | custom-call | tf_op jit(solution)/shard_map/hold/pallas_call | solution.py:198
  49.5 0.2 collective-permute-done.8.other_ref
  49.7 1.4 %project.1 = bf16[4,8,8,512]{3,2,1,0:T(8,128)(2,1)} custom-call(f32[8,2048]{1,0:T(8,128)S(1)} %get-tuple-element.32.own_ref, f32[8,2048]{1,0:T(8,128)S(1)} %collective-permute-done.8.other_ref, bf16[2048,1024]{1,0:T(8,128)(2,1)S(1)} %hold.1.cols_ref), custom_call_target="tpu_custom_call" | custom-call | tf_op jit(solution)/shard_map/project/pallas_call | solution.py:595
  51.1 8.6 %all-to-all-start.1 = ((bf16[32,8,512]{2,1,0:T(8,128)(2,1)}), bf16[32,8,512]{2,1,0:T(8,128)(2,1)S(1)}, u32[]{:S(2)}, u32[]{:S(2)}) async-start(bf16[32,8,512]{2,1,0:T(8,128)(2,1)} %bitcast.8), calls=%async_computation.1 | async-start | bytes 524288 | tf_op jit(solution)/shard_map/all_to_all | solution.py:725
  59.6 0.0 collective-permute-done.far_ref
  59.7 0.3 collective-permute-start.1
  60.0 1.3 %collective-permute-done.1.near_ref = bf16[2,256,256]{2,1,0:T(8,128)(2,1)S(1)} collective-permute-done((bf16[2,256,256]{2,1,0:T(8,128)(2,1)S(1)}, bf16[2,256,256]{2,1,0:T(8,128)(2,1)S(1)}, u32[]{:S(2)}, u32[]{:S(2)}) %collective-permute-start.1) | collective-permute-done | bytes 262176 | tf_op jit(solution)/shard_map/ppermute | solution.py:688
  61.3 1.1 %assemble.1 = (bf16[1024,256]{1,0:T(8,128)(2,1)S(1)}, f32[128,1024]{1,0:T(8,128)S(1)}) custom-call(s32[1]{0:T(128)} %bitcast.1.member_ref, bf16[256,256]{1,0:T(8,128)(2,1)S(1)} %bitcast.13, bf16[256,256]{1,0:T(8,128)(2,1)S(1)} %collective-permute-done.far_ref, bf16[2,256,256]{2,1,0:T(8,128)(2,1)S(1)} %collective-permute-done.1.near_ref, f32[128,1024]{1,0:T(8,128)} %control_ref.3), custom_call_target="tpu_custom_call" | custom-call | tf_op jit(solution)/shard_map/assemble/pallas_call | solution.py:620
  62.4 7.7 %all-to-all-done.1 = bf16[32,8,512]{2,1,0:T(8,128)(2,1)S(1)} async-done(((bf16[32,8,512]{2,1,0:T(8,128)(2,1)}), bf16[32,8,512]{2,1,0:T(8,128)(2,1)S(1)}, u32[]{:S(2)}, u32[]{:S(2)}) %all-to-all-start.1) | async-done | bytes 262176 | tf_op jit(solution)/shard_map/all_to_all | solution.py:725
  70.1 0.5 gradient.1.own_ref
  70.6 0.1 collective-permute-start.9
  70.6 1.5 %collective-permute-done.9.other_ref = f32[136,512]{1,0:T(8,128)S(1)} collective-permute-done((f32[136,512]{1,0:T(8,128)S(1)}, f32[136,512]{1,0:T(8,128)S(1)}, u32[]{:S(2)}, u32[]{:S(2)}) %collective-permute-start.9) | collective-permute-done | bytes 278560 | tf_op jit(solution)/shard_map/ppermute | solution.py:688
  72.2 1.0 %update.1 = f32[128,1024]{1,0:T(8,128)} custom-call(s32[1]{0:T(128)} %bitcast.core_ref, f32[128,1024]{1,0:T(8,128)S(1)} %get-tuple-element.18.control_ref, f32[136,512]{1,0:T(8,128)S(1)} %gradient.1.own_ref, f32[136,512]{1,0:T(8,128)S(1)} %collective-permute-done.9.other_ref), custom_call_target="tpu_custom_call" | custom-call | tf_op jit(solution)/shard_map/update/pallas_call | solution.py:676
  (10 shorter events, 0.1 us)
Async XLA Ops:
  1.9 27.4 %all-to-all-start = ((bf16[8,176,256]{2,1,0:T(8,128)(2,1)}), bf16[8,176,256]{2,1,0:T(8,128)(2,1)S(1)}, u32[]{:S(2)}, u32[]{:S(2)}) async-start(bf16[8,176,256]{2,1,0:T(8,128)(2,1)} %pack_pieces.1), calls=%async_computation | async-start | bytes 1441792 | tf_op jit(solution)/shard_map/all_to_all | solution.py:705
  12.6 19.8 %collective-permute-start.5 = (bf16[10,8,2048]{2,1,0:T(8,128)(2,1)}, bf16[10,8,2048]{2,1,0:T(8,128)(2,1)S(1)}, u32[]{:S(2)}, u32[]{:S(2)}) collective-permute-start(bf16[10,8,2048]{2,1,0:T(8,128)(2,1)} %get-tuple-element.21), channel_id=1, source_target_pairs={{0,1},{1,2},{2,3},{3,4},{4,5},{5,6},{6,7},{8,9},{9,10},{10,11},{11... | collective-permute-start | bytes 983048 | tf_op jit(solution)/shard_map/ppermute | solution.py:707
  16.6 15.9 %collective-permute-start.6 = (bf16[10,8,2048]{2,1,0:T(8,128)(2,1)}, bf16[10,8,2048]{2,1,0:T(8,128)(2,1)S(1)}, u32[]{:S(2)}, u32[]{:S(2)}) collective-permute-start(bf16[10,8,2048]{2,1,0:T(8,128)(2,1)} %get-tuple-element.22), channel_id=1, source_target_pairs={{1,0},{2,1},{3,2},{4,3},{5,4},{6,5},{7,6},{9,8},{10,9},{11,10},{12... | collective-permute-start | bytes 983048 | tf_op jit(solution)/shard_map/ppermute | solution.py:708
  29.5 12.0 %collective-permute-start.2 = (bf16[40,256]{1,0:T(8,128)(2,1)S(1)}, bf16[40,256]{1,0:T(8,128)(2,1)S(1)}, u32[]{:S(2)}, u32[]{:S(2)}) collective-permute-start(bf16[40,256]{1,0:T(8,128)(2,1)S(1)} %make_coeffs.1.own_ref), channel_id=1, source_target_pairs={{0,8},{8,0},{16,24},{24,16},{1,9},{9,1},{17,25},{25,17},{2,10},{10... | collective-permute-start | bytes 61448 | tf_op jit(solution)/shard_map/ppermute | solution.py:688
  29.6 11.9 %collective-permute-start.3 = (bf16[40,256]{1,0:T(8,128)(2,1)S(1)}, bf16[40,256]{1,0:T(8,128)(2,1)S(1)}, u32[]{:S(2)}, u32[]{:S(2)}) collective-permute-start(bf16[40,256]{1,0:T(8,128)(2,1)S(1)} %make_coeffs.1.own_ref), channel_id=1, source_target_pairs={{0,16},{8,24},{16,0},{24,8},{1,17},{9,25},{17,1},{25,9},{2,18},{10... | collective-permute-start | bytes 61448 | tf_op jit(solution)/shard_map/ppermute | solution.py:688
  31.1 10.4 %collective-permute-start.4 = (bf16[40,256]{1,0:T(8,128)(2,1)S(1)}, bf16[40,256]{1,0:T(8,128)(2,1)S(1)}, u32[]{:S(2)}, u32[]{:S(2)}) collective-permute-start(bf16[40,256]{1,0:T(8,128)(2,1)S(1)} %make_coeffs.1.own_ref), channel_id=1, source_target_pairs={{0,24},{8,16},{16,8},{24,0},{1,25},{9,17},{17,9},{25,1},{2,26},{10... | collective-permute-start | bytes 61448 | tf_op jit(solution)/shard_map/ppermute | solution.py:688
  32.4 9.1 %copy-start = (bf16[2048,1024]{1,0:T(8,128)(2,1)S(1)}, bf16[2048,1024]{1,0:T(8,128)(2,1)}, u32[]{:S(2)}) copy-start(bf16[2048,1024]{1,0:T(8,128)(2,1)} %source_ref.1) | copy-start | bytes 12582916
  43.7 1.4 %collective-permute-start.7 = (f32[16,2048]{1,0:T(8,128)S(1)}, f32[16,2048]{1,0:T(8,128)S(1)}, u32[]{:S(2)}, u32[]{:S(2)}) collective-permute-start(f32[16,2048]{1,0:T(8,128)S(1)} %get-tuple-element.30), channel_id=1, source_target_pairs={{0,8},{8,0},{16,24},{24,16},{1,9},{9,1},{17,25},{25,17},{2,10},{10... | collective-permute-start | bytes 393224 | tf_op jit(solution)/shard_map/ppermute | solution.py:688
  45.1 4.5 %collective-permute-start.8 = (f32[8,2048]{1,0:T(8,128)S(1)}, f32[8,2048]{1,0:T(8,128)S(1)}, u32[]{:S(2)}, u32[]{:S(2)}) collective-permute-start(f32[8,2048]{1,0:T(8,128)S(1)} %get-tuple-element.31), channel_id=1, source_target_pairs={{0,16},{8,24},{16,0},{24,8},{1,17},{9,25},{17,1},{25,9},{2,18},{10... | collective-permute-start | bytes 196616 | tf_op jit(solution)/shard_map/ppermute | solution.py:688
  46.7 12.9 %collective-permute-start = (bf16[256,256]{1,0:T(8,128)(2,1)S(1)}, bf16[256,256]{1,0:T(8,128)(2,1)S(1)}, u32[]{:S(2)}, u32[]{:S(2)}) collective-permute-start(bf16[256,256]{1,0:T(8,128)(2,1)S(1)} %bitcast.11), channel_id=1, source_target_pairs={{0,16},{8,24},{16,0},{24,8},{1,17},{9,25},{17,1},{25,9},{2,18},{10... | collective-permute-start | bytes 393224 | tf_op jit(solution)/shard_map/ppermute | solution.py:688
  51.1 19.0 %all-to-all-start.1 = ((bf16[32,8,512]{2,1,0:T(8,128)(2,1)}), bf16[32,8,512]{2,1,0:T(8,128)(2,1)S(1)}, u32[]{:S(2)}, u32[]{:S(2)}) async-start(bf16[32,8,512]{2,1,0:T(8,128)(2,1)} %bitcast.8), calls=%async_computation.1 | async-start | bytes 524288 | tf_op jit(solution)/shard_map/all_to_all | solution.py:725
  59.7 1.6 %collective-permute-start.1 = (bf16[2,256,256]{2,1,0:T(8,128)(2,1)S(1)}, bf16[2,256,256]{2,1,0:T(8,128)(2,1)S(1)}, u32[]{:S(2)}, u32[]{:S(2)}) collective-permute-start(bf16[2,256,256]{2,1,0:T(8,128)(2,1)S(1)} %pad_maximum_fusion), channel_id=1, source_target_pairs={{0,8},{8,0},{16,24},{24,16},{1,9},{9,1},{17,25},{25,17},{2,10},{10... | collective-permute-start | bytes 786440 | tf_op jit(solution)/shard_map/ppermute | solution.py:688
  70.6 1.6 %collective-permute-start.9 = (f32[136,512]{1,0:T(8,128)S(1)}, f32[136,512]{1,0:T(8,128)S(1)}, u32[]{:S(2)}, u32[]{:S(2)}) collective-permute-start(f32[136,512]{1,0:T(8,128)S(1)} %gradient.1.own_ref), channel_id=1, source_target_pairs={{0,8},{8,0},{16,24},{24,16},{1,9},{9,1},{17,25},{25,17},{2,10},{10... | collective-permute-start | bytes 835592 | tf_op jit(solution)/shard_map/ppermute | solution.py:688

commit v3 on v2

--- a/solution.py
+++ b/solution.py
@@ -89,19 +89,12 @@
     for s in range(count):
         states[2 * s].wait()
         height, east, north = (last[s, f].astype(F32) for f in range(3))
-        height, east, north = (
-            pltpu.roll(height, 4, 0), pltpu.roll(east, 1, 0), pltpu.roll(north, 7, 0)
-        )
-        low = (row >= 1) & (row < 4)
-        middle = (row >= 4) & (row < 7)
-        up_ref[s] = jnp.where(low, height, jnp.where(middle, north, east)).astype(BF16)
+        height, north = pltpu.roll(height, 3, 0), pltpu.roll(north, 6, 0)
+        up_ref[s] = jnp.where(row < 3, height, jnp.where(row < 6, north, east)).astype(BF16)
         states[2 * s + 1].wait()
         height, east, north = (first[s, f].astype(F32) for f in range(3))
-        height, east, north = (
-            pltpu.roll(height, 4, 0), pltpu.roll(east, 2, 0), pltpu.roll(north, 7, 0)
-        )
-        high = (row >= 2) & (row < 4)
-        down_ref[s] = jnp.where(middle, height, jnp.where(high, east, north)).astype(BF16)
+        east, north = pltpu.roll(east, 6, 0), pltpu.roll(north, 3, 0)
+        down_ref[s] = jnp.where(row < 3, height, jnp.where(row < 6, north, east)).astype(BF16)
     for copy in others:
         copy.wait()
     targets_up = jnp.zeros((TILE, cols), F32)
@@ -111,8 +104,8 @@
         targets_down = jnp.where(row == s, seen[1, s].astype(F32)[:1, :], targets_down)
     up_ref[count] = targets_up.astype(BF16)
     down_ref[count] = targets_down.astype(BF16)
-    up_ref[count + 1] = pltpu.roll(sea[0].astype(F32), 4, 0).astype(BF16)
-    down_ref[count + 1] = pltpu.roll(sea[1].astype(F32), 4, 0).astype(BF16)
+    up_ref[count + 1] = sea[0].astype(F32).astype(BF16)
+    down_ref[count + 1] = sea[1].astype(F32).astype(BF16)
 
 
 def edge_messages(section_index, checkpoints, targets, sea_mask):
@@ -216,6 +209,9 @@
     def put(self, tile, value):
         self.ref[:, TILE * (tile + 1) : TILE * (tile + 2), :] = value
 
+    def put_at(self, start, value):
+        self.ref[:, start : start + value.shape[1], :] = value
+
     def get(self, tile, step=0):
         start = TILE * (tile + 1) + step
         return self.ref[:, start : start + TILE, :]
@@ -230,71 +226,81 @@
         ref[...] = jnp.zeros_like(ref)
 
 
-def add_state(tiles, load, seen, mask, live, padded, partial, gx, gy, pairs_ref):
-    heights, fluxes, mid_fluxes, weights, besides, misfits = (Rows(ref) for ref in padded)
+def add_state(tiles, state, mask, live, padded, plain, sums):
+    heights, easts, norths, seens = state
+    fluxes, mid_fluxes, weights, rights, misfits = (Rows(ref) for ref in padded)
+    lefts, partial = plain
+    push_left, push_right, gy, same, two_x, two_y, up, down = sums
     half = 0.5 * TIME_STEP
     keep = 1.0 - TIME_STEP * FRICTION
     turn = TIME_STEP * CORIOLIS / keep
     slope = half * GRAVITY / keep
 
+    for tile in range(-1, tiles + 1):
+        fluxes.put(tile, (DEPTH + heights.get(tile)) * norths.get(tile))
+
     for tile in range(tiles):
-        height = load(0, tile)
-        heights.put(tile, height)
-        fluxes.put(tile, (DEPTH + height) * load(2, tile))
-
-    for tile in range(tiles):
+        here = rows_of(tile)
         height = heights.get(tile)
-        east = load(1, tile)
-        north = load(2, tile)
+        east = easts.get(tile)
+        north = norths.get(tile)
         flux = dx((DEPTH + height) * east) + (fluxes.get(tile, 1) - fluxes.get(tile, -1))
-        sea = mask[:, rows_of(tile), :]
+        sea = mask[:, here, :]
         height_mid = sea * (height - half * flux)
         weight = DEPTH * sea + height_mid
         east_mid = east + turn * north - slope * dx(height)
         north_mid = north - turn * east - slope * (heights.get(tile, 1) - heights.get(tile, -1))
+        right = shift_cols(weight, 1)
+        left = shift_cols(weight, -1)
         mid_fluxes.put(tile, weight * north_mid)
         weights.put(tile, weight)
-        besides.put(tile, shift_cols(weight, 1))
-        partial[:, rows_of(tile), :] = (
-            height + height_mid - 2.0 * seen(tile) - half * keep * dx(weight * east_mid)
+        rights.put(tile, right)
+        lefts[:, here, :] = left
+        same[:, here, :] += weight * weight
+        two_x[:, here, :] += left * right
+        partial[:, here, :] = (
+            height + height_mid - 2.0 * seens.get(tile) - half * keep * dx(weight * east_mid)
         )
 
     for tile in range(tiles):
+        here = rows_of(tile)
         change = mid_fluxes.get(tile, 1) - mid_fluxes.get(tile, -1)
-        misfit = live[:, rows_of(tile), :] * (partial[:, rows_of(tile), :] - half * keep * change)
+        misfit = live[:, here, :] * (partial[:, here, :] - half * keep * change)
         misfits.put(tile, misfit)
-        gx[:, rows_of(tile), :] += weights.get(tile) * dx(misfit)
+        push_left[:, here, :] += lefts[:, here, :] * misfit
+        push_right[:, here, :] += rights.get(tile) * misfit
 
     for tile in range(tiles):
         here = rows_of(tile)
         weight = weights.get(tile)
         gy[:, here, :] += weight * (misfits.get(tile, 1) - misfits.get(tile, -1))
-        pairs_ref[0, :, here, :] += weight * weight
-        pairs_ref[1, :, here, :] += weight * shift_cols(weight, 2)
-        pairs_ref[2, :, here, :] += weight * weights.get(tile, 2)
-        pairs_ref[3, :, here, :] += weight * besides.get(tile, 1)
-        pairs_ref[4, :, here, :] += weight * besides.get(tile, -1)
-
-
-def inner_states(index_ref, state_ref, targets_ref, sea_ref, basis_ref, gx_ref, gy_ref, pairs_ref, rows_ref, mask, live, partial, *padded):
+        two_y[:, here, :] += weight * weights.get(tile, 2)
+        up[:, here, :] += weight * rights.get(tile, 1)
+        down[:, here, :] += weight * rights.get(tile, -1)
+
+
+def inner_states(index_ref, state_ref, targets_ref, sea_ref, basis_ref, push_ref, pairs_ref, rows_ref, mask, live, *scratch):
     rows = sea_ref.shape[0]
     tiles = rows // TILE
+    plain, padded = scratch[:2], scratch[2:]
 
     @pl.when(pl.program_id(0) == 0)
     def _():
-        clear(gx_ref, gy_ref, pairs_ref, *padded)
+        clear(push_ref, pairs_ref, *padded)
         rows_ref[...] = basis_ref[...]
         for tile in range(tiles):
             mask[:, rows_of(tile), :] = split_lanes(sea_ref[rows_of(tile), :].astype(F32))
         row = lax.broadcasted_iota(jnp.int32, live.shape, 1)
         live[...] = jnp.where((row >= 2) & (row < rows - 2), mask[...], 0.0)
 
-    add_state(
-        tiles,
-        lambda field, tile: split_lanes(state_ref[0, 0, field, rows_of(tile), :].astype(F32)),
-        lambda tile: split_lanes(targets_ref[0, rows_of(tile), :].astype(F32)),
-        mask, live, padded, partial, gx_ref, gy_ref, pairs_ref,
-    )
+    state = [Rows(ref) for ref in padded[:4]]
+    for tile in range(tiles):
+        for field in range(3):
+            value = state_ref[0, 0, field, rows_of(tile), :].astype(F32)
+            state[field].put(tile, split_lanes(value))
+        state[3].put(tile, split_lanes(targets_ref[0, rows_of(tile), :].astype(F32)))
+    sums = [push_ref.at[k] for k in range(3)] + [pairs_ref.at[k] for k in range(PAIRS)]
+    add_state(tiles, state, mask, live, padded[4:], plain, sums)
 
 
 def inner_pass(section_index, checkpoints, targets, sea_mask, basis_rows):
@@ -304,8 +310,7 @@
     padded = pltpu.VMEM((lanes, rows + 2 * TILE, LANES), F32)
     plain = pltpu.VMEM((lanes, rows, LANES), F32)
     outs = (
-        jax.ShapeDtypeStruct((lanes, rows, LANES), F32),
-        jax.ShapeDtypeStruct((lanes, rows, LANES), F32),
+        jax.ShapeDtypeStruct((3, lanes, rows, LANES), F32),
         jax.ShapeDtypeStruct((PAIRS, lanes, rows, LANES), F32),
         jax.ShapeDtypeStruct((rows, width), BF16),
     )
@@ -325,106 +330,99 @@
             out_specs=tuple(
                 pl.BlockSpec(out.shape, lambda s, index, n=len(out.shape): (0,) * n) for out in outs
             ),
-            scratch_shapes=[plain] * 3 + [padded] * 6,
+            scratch_shapes=[plain] * 4 + [padded] * 9,
         ),
         compiler_params=limit(18),
     )(*map(in_hbm, (section_index, checkpoints, targets, sea_mask, basis_rows)))
 
 
-def seam_states(index_ref, last_ref, first_ref, before_ref, after_ref, shared_before_ref, shared_after_ref, seen_last_ref, seen_first_ref, sea_ref, gx_in_ref, gy_in_ref, pairs_in_ref, base_ref, pairs_ref, mask_ref, seen_edge, mask, live, partial, gx, gy, pairs, ring_x, ring_y, *padded):
+def seam_states(index_ref, last_ref, first_ref, before_ref, after_ref, shared_before_ref, shared_after_ref, seen_last_ref, seen_first_ref, sea_ref, push_in_ref, pairs_in_ref, base_ref, pairs_ref, mask_ref, seen_edge, mask, live, lefts, partial, sums_ref, ring_sums, *padded):
     s = pl.program_id(0)
     rows, cols = sea_ref.shape
     row = tile_rows((TILE, cols))
     top = row < 4
 
-    def seam(ends, beyond_after, beyond_before):
-        own_last, own_first = (pltpu.roll(end, 4, 0) for end in ends)
-        return (
-            split_lanes(jnp.where(top, own_last, beyond_after)),
-            split_lanes(jnp.where(top, beyond_before, own_first)),
-        )
-
     @pl.when(s == 0)
     def _():
-        clear(gx, gy, pairs, *padded)
-        seen_edge[0] = shared_before_ref[0].astype(F32)
-        seen_edge[1] = shared_after_ref[0].astype(F32)
-        after = jnp.where(row < 6, shared_after_ref[1].astype(F32), 0.0)
-        before = jnp.where(row >= 2, shared_before_ref[1].astype(F32), 0.0)
-        ends = (sea_ref[rows - TILE :, :].astype(F32), sea_ref[:TILE, :].astype(F32))
-        for tile, value in enumerate(seam(ends, after, before)):
-            mask[:, rows_of(tile), :] = value
+        clear(sums_ref, *padded)
+        seen_edge[0] = split_lanes(shared_before_ref[0].astype(F32))
+        seen_edge[1] = split_lanes(shared_after_ref[0].astype(F32))
+        after = jnp.where(row < 2, shared_after_ref[1].astype(F32), 0.0)
+        before = jnp.where(row >= 6, shared_before_ref[1].astype(F32), 0.0)
+        beyond = after + before
+        turned = pltpu.roll(beyond, 4, 0)
+        last = pltpu.roll(sea_ref[rows - TILE :, :].astype(F32), 4, 0)
+        first = pltpu.roll(sea_ref[:TILE, :].astype(F32), 4, 0)
+        mask[:, :TILE, :] = split_lanes(jnp.where(top, last, turned))
+        mask[:, TILE:, :] = split_lanes(jnp.where(top, turned, first))
         for tile in range(rows // TILE):
             mask_ref[:, rows_of(tile), :] = split_lanes(
                 sea_ref[rows_of(tile), :].astype(F32)
             ).astype(BF16)
-        beyond = jnp.where(top, pltpu.roll(after, 4, 0), pltpu.roll(before, 4, 0))
         mask_ref[:, rows:, :] = split_lanes(beyond).astype(BF16)
         place = lax.broadcasted_iota(jnp.int32, live.shape, 1)
         counts = ((place >= 2) & (place < 5)) | ((place >= 11) & (place < 14))
         live[...] = jnp.where(counts, mask[...], 0.0)
 
-    after = after_ref[0].astype(F32)
-    before = before_ref[0].astype(F32)
-    turned = ((0, 0), (2, 3), (5, 5))
-    fields = []
-    for field, (forward, back) in enumerate(turned):
-        ends = (last_ref[0, 0, field].astype(F32), first_ref[0, 0, field].astype(F32))
-        fields.append(
-            seam(
-                ends,
-                pltpu.roll(after, forward, 0) if forward else after,
-                pltpu.roll(before, back, 0) if back else before,
-            )
-        )
-    ends = (seen_last_ref[0].astype(F32), seen_first_ref[0].astype(F32))
-    seen = seam(ends, seen_edge[1, pl.ds(s, 1), :], seen_edge[0, pl.ds(s, 1), :])
-    add_state(
-        2,
-        lambda field, tile: fields[field][tile],
-        lambda tile: seen[tile],
-        mask, live, padded, partial, gx, gy, pairs,
-    )
+    state = [Rows(ref) for ref in padded[:4]]
+    after = split_lanes(after_ref[0].astype(F32))
+    before = split_lanes(before_ref[0].astype(F32))
+    state[0].put_at(12, after)
+    state[0].put_at(17, before)
+    state[1].put_at(12, before)
+    state[1].put_at(6, after)
+    state[2].put_at(14, before)
+    state[2].put_at(9, after)
+    state[3].put_at(12, seen_edge[1, :, pl.ds(s, 1), :])
+    state[3].put_at(19, seen_edge[0, :, pl.ds(s, 1), :])
+    for field in range(3):
+        state[field].put_at(4, split_lanes(last_ref[0, 0, field].astype(F32)))
+        state[field].put_at(20, split_lanes(first_ref[0, 0, field].astype(F32)))
+    state[3].put_at(4, split_lanes(seen_last_ref[0].astype(F32)))
+    state[3].put_at(20, split_lanes(seen_first_ref[0].astype(F32)))
+    sums = [sums_ref.at[k] for k in range(3 + PAIRS)]
+    add_state(2, state, mask, live, padded[4:], (lefts, partial), sums)
 
     @pl.when(s == pl.num_programs(0) - 1)
     def _():
-        place = lax.broadcasted_iota(jnp.int32, (gx.shape[0], TILE, LANES), 1)
+        place = lax.broadcasted_iota(jnp.int32, (lefts.shape[0], TILE, LANES), 1)
         top = place < 4
         final = rows // TILE - 1
 
-        def ring(inner, outer, out, low):
+        def ring(inner, outer, out, bounds):
             ending = pltpu.roll(outer[:, :TILE, :], 4, 1)
             opening = pltpu.roll(outer[:, TILE:, :], 4, 1)
             for tile in range(1, final):
                 out[:, rows_of(tile), :] = inner[:, rows_of(tile), :]
             head = inner[:, :TILE, :]
             tail = inner[:, rows_of(final), :]
-            if low is None:
+            if bounds is None:
                 head = head + jnp.where(top, opening, 0.0)
                 tail = tail + jnp.where(top, 0.0, ending)
             else:
-                head = jnp.where(place < low, opening, head)
-                tail = jnp.where(place > 4, ending, tail)
+                head = jnp.where(place < bounds[0], opening, head)
+                tail = jnp.where(place > bounds[1], ending, tail)
             out[:, :TILE, :] = head
             out[:, rows_of(final), :] = tail
             out[:, rows:, :] = jnp.where(top, ending, opening)
 
-        ring(gx_in_ref[...], gx[...], ring_x, None)
-        ring(gy_in_ref[...], gy[...], ring_y, None)
+        for k in range(3):
+            ring(push_in_ref[k], sums_ref[k], ring_sums.at[k], None)
         for k in range(PAIRS):
-            ring(pairs_in_ref[k], pairs[k], pairs_ref.at[k], 2 if k == 4 else 1)
+            bounds = (2, 5) if k == PAIRS - 1 else (1, 4)
+            ring(pairs_in_ref[k], sums_ref[3 + k], pairs_ref.at[k], bounds)
         scale = 0.0625 * TIME_STEP * TIME_STEP
-        base_ref[...] = scale * (dy(ring_x[...]) - dx(ring_y[...]))
-
-
-def seam_pass(section_index, checkpoints, before, after, targets, sea_mask, gx, gy, pairs):
+        gx = shift_cols(ring_sums[0], 1) - shift_cols(ring_sums[1], -1)
+        base_ref[...] = scale * (dy(gx) - dx(ring_sums[2]))
+
+
+def seam_pass(section_index, checkpoints, before, after, targets, sea_mask, push, pairs):
     count, _, fields, rows, cols = checkpoints.shape
     lanes = cols // LANES
     final = rows // TILE - 1
     ring = rows + TILE
     plain = pltpu.VMEM((lanes, 2 * TILE, LANES), F32)
     padded = pltpu.VMEM((lanes, 4 * TILE, LANES), F32)
-    whole = pltpu.VMEM((lanes, ring, LANES), F32)
     state = (1, 1, fields, TILE, cols)
     edge = pl.BlockSpec((1, TILE, cols), lambda s, index: (s, 0, 0))
     shared = pl.BlockSpec((2, TILE, cols), lambda s, index: (count // 2, 0, 0))
@@ -454,18 +452,17 @@
                 pl.BlockSpec((1, TILE, cols), lambda s, index: (s, final, 0)),
                 pl.BlockSpec((1, TILE, cols), lambda s, index: (s, 0, 0)),
                 fixed(sea_mask),
-                fixed(gx),
-                fixed(gy),
+                fixed(push),
                 fixed(pairs),
             ],
             out_specs=tuple(fixed(out) for out in outs),
-            scratch_shapes=[pltpu.VMEM((2, TILE, cols), F32)]
-            + [plain] * 5
-            + [pltpu.VMEM((PAIRS, lanes, 2 * TILE, LANES), F32)]
-            + [whole] * 2
-            + [padded] * 6,
+            scratch_shapes=[pltpu.VMEM((2, lanes, TILE, LANES), F32)]
+            + [plain] * 4
+            + [pltpu.VMEM((3 + PAIRS, lanes, 2 * TILE, LANES), F32)]
+            + [pltpu.VMEM((3, lanes, ring, LANES), F32)]
+            + [padded] * 9,
         ),
-        compiler_params=limit(20),
+        compiler_params=limit(22),
     )(
         in_hbm(section_index),
         in_hbm(checkpoints),
@@ -477,8 +474,7 @@
         in_hbm(targets),
         in_hbm(targets),
         in_hbm(sea_mask),
-        gx,
-        gy,
+        push,
         pairs,
     )
 
@@ -536,17 +532,23 @@
     same, two_x, two_y, up, down = (pairs_ref[k] for k in range(5))
     same_x = same * sx
     same_y = same * sy
-    up_x = up * shift_rows(shift_cols(sx, 1), 1)
-    up_y = up * shift_rows(shift_cols(sy, 1), 1)
-    down_x = down * shift_rows(shift_cols(sx, 1), -1)
-    down_y = down * shift_rows(shift_cols(sy, 1), -1)
+    right_x = shift_cols(sx, 1)
+    right_y = shift_cols(sy, 1)
+    up_x = up * shift_rows(right_x, 1)
+    up_y = up * shift_rows(right_y, 1)
+    down_x = down * shift_rows(right_x, -1)
+    down_y = down * shift_rows(right_y, -1)
     back_up_x = shift_rows(shift_cols(up * sx, -1), -1)
     back_up_y = shift_rows(shift_cols(up * sy, -1), -1)
     back_down_x = shift_rows(shift_cols(down * sx, -1), 1)
     back_down_y = shift_rows(shift_cols(down * sy, -1), 1)
-    gx = shift_cols(mask, 1) * (
-        two_x * shift_cols(sx, 2) - same_x + up_y - down_y
-    ) - shift_cols(mask, -1) * (same_x - shift_cols(two_x * sx, -2) + back_down_y - back_up_y)
+    beside = mask * two_x
+    gx = (
+        shift_cols(mask, 1) * (up_y - same_x - down_y)
+        + shift_cols(beside * right_x, 1)
+        - shift_cols(mask, -1) * (same_x + back_down_y - back_up_y)
+        + shift_cols(beside * shift_cols(sx, -1), -1)
+    )
     gy = shift_rows(mask, 1) * (
         up_x - back_down_x + two_y * shift_rows(sy, 2) - same_y
     ) - shift_rows(mask, -1) * (down_x - back_up_x + same_y - shift_rows(two_y * sy, -2))
@@ -706,13 +708,13 @@
     up, down = edge_messages(section_index, checkpoints, targets, sea_mask)
     before = lax.ppermute(up, "space", [(i, i + 1) for i in range(slabs - 1)])
     after = lax.ppermute(down, "space", [(i + 1, i) for i in range(slabs - 1)])
-    gx, gy, pairs, near_rows = inner_pass(section_index, checkpoints, targets, sea_mask, basis_rows)
+    push, pairs, near_rows = inner_pass(section_index, checkpoints, targets, sea_mask, basis_rows)
     own = coeffs_part(slab, near_rows, pieces)
     parts = [own]
     for bits in (1, 2, 3):
         parts.append(partner(own, bits))
     base, pairs, mask = seam_pass(
-        section_index, checkpoints, before, after, targets, sea_mask, gx, gy, pairs
+        section_index, checkpoints, before, after, targets, sea_mask, push, pairs
     )
     keep, give = gradient_halves(member, parts, basis_cols, base, pairs, mask)
 

time: 73.9 us -> 74.1 us (level)
  no operation moved by 1% of the time
where the time goes in v3:
time: 74.1 us; the launch traced here: 73.3 us
  Pallas kernels  33.3 us (45%)
  starting transfers between devices  25.7 us (35%)
  waiting for transfers between devices  14 us (19%)
    pallas_call x1, Pallas kernels, inner_pass(): pl.pallas_call(inner_states, name='inner_states', out_shape=outs, grid_sp...  10.4 us
    pallas_call x1, Pallas kernels, seam_pass(): pl.pallas_call(seam_states, name='seam_states', out_shape=outs, grid_spec...  9.18 us
    all_to_all x1, starting transfers between devices, on_device(): lax.all_to_all(send.reshape(members * slabs, single, half), ('ens', 'spac...  8.58 us
    all_to_all x1, waiting for transfers between devices, on_device(): lax.all_to_all(send.reshape(members * slabs, single, half), ('ens', 'spac...  7.73 us
    all_to_all x1, starting transfers between devices, on_device(): pieces = lax.all_to_all(pieces, 'space', 0, 0)  7.32 us
    ppermute x8, starting transfers between devices, partner(): return lax.ppermute(value, 'ens', [(i, i ^ bit) for i in range(count)])  4.53 us
    ppermute x8, waiting for transfers between devices, partner(): return lax.ppermute(value, 'ens', [(i, i ^ bit) for i in range(count)])  4.32 us
    ppermute x1, starting transfers between devices, on_device(): before = lax.ppermute(up, 'space', [(i, i + 1) for i in range(slabs - 1)])  3.94 us
  transfers between devices with their start and end apart: 12, of which 7 were waited for; matrix products, arithmetic and copies ran while one was open for 0% of the time, Pallas kernels for 38%

profile of v3, /device:TPU:0, one launch (start us, length us, event | category | flops | bytes accessed | tf_op | source)
XLA Modules:
  0.0 73.3 jit_solution(13230022160727438143)
XLA Ops:
  0.0 1.9 %pack_pieces.1 = bf16[8,176,256]{2,1,0:T(8,128)(2,1)} custom-call(s32[1]{0:T(128)} %bitcast.1.member_ref, bf16[32,1024]{1,0:T(8,128)(2,1)} %basis_ref.3, f32[128,1024]{1,0:T(8,128)} %control_ref.3), custom_call_target="tpu_custom_call" | custom-call | tf_op jit(solution)/shard_map/pack_pieces/pallas_call | solution.py:164
  1.9 7.3 %all-to-all-start = ((bf16[8,176,256]{2,1,0:T(8,128)(2,1)}), bf16[8,176,256]{2,1,0:T(8,128)(2,1)S(1)}, u32[]{:S(2)}, u32[]{:S(2)}) async-start(bf16[8,176,256]{2,1,0:T(8,128)(2,1)} %pack_pieces.1), calls=%async_computation | async-start | bytes 1441792 | tf_op jit(solution)/shard_map/all_to_all | solution.py:707
  9.2 3.4 %pack_edges.1 = (bf16[10,8,2048]{2,1,0:T(8,128)(2,1)}, bf16[10,8,2048]{2,1,0:T(8,128)(2,1)}) custom-call(s32[8]{0:T(128)} %index_ref.5, bf16[8,2,3,32,2048]{4,3,2,1,0:T(8,128)(2,1)} %first_ref.1, bf16[8,32,2048]{2,1,0:T(8,128)(2,1)} %seen_first_ref.1, s32[32,2048]{1,0:T(8,128)} %sea_ref.5), custom_call_target="tpu_custom_call" | custom-call | tf_op jit(solution)/shard_map/pack_edges/pallas_call | solution.py:114
  12.6 3.9 %collective-permute-start.5 = (bf16[10,8,2048]{2,1,0:T(8,128)(2,1)}, bf16[10,8,2048]{2,1,0:T(8,128)(2,1)S(1)}, u32[]{:S(2)}, u32[]{:S(2)}) collective-permute-start(bf16[10,8,2048]{2,1,0:T(8,128)(2,1)} %get-tuple-element.20), channel_id=1, source_target_pairs={{0,1},{1,2},{2,3},{3,4},{4,5},{5,6},{6,7},{8,9},{9,10},{10,11},{11... | collective-permute-start | bytes 983048 | tf_op jit(solution)/shard_map/ppermute | solution.py:709
  16.6 1.3 %collective-permute-start.6 = (bf16[10,8,2048]{2,1,0:T(8,128)(2,1)}, bf16[10,8,2048]{2,1,0:T(8,128)(2,1)S(1)}, u32[]{:S(2)}, u32[]{:S(2)}) collective-permute-start(bf16[10,8,2048]{2,1,0:T(8,128)(2,1)} %get-tuple-element.21), channel_id=1, source_target_pairs={{1,0},{2,1},{3,2},{4,3},{5,4},{6,5},{7,6},{9,8},{10,9},{11,10},{12... | collective-permute-start | bytes 983048 | tf_op jit(solution)/shard_map/ppermute | solution.py:710
  17.9 10.4 %inner_states.1 = (f32[3,16,32,128]{3,2,1,0:T(8,128)S(1)}, f32[5,16,32,128]{3,2,1,0:T(8,128)S(1)}, bf16[32,1024]{1,0:T(8,128)(2,1)S(1)}) custom-call(s32[8]{0:T(128)} %index_ref.5, bf16[8,2,3,32,2048]{4,3,2,1,0:T(8,128)(2,1)} %first_ref.1, bf16[8,32,2048]{2,1,0:T(8,128)(2,1)} %seen_first_ref.1, s32[32,2048]{1,0:T(8,128)} %sea_ref.5, bf16[32,1024]{1,0:T(8,128)(2,1)} %basis_ref.3), custom_call_target="tpu_custom_call" | custom-call | tf_op jit(solution)/shard_map/inner_states/pallas_call | solution.py:317
  28.3 1.0 %all-to-all-done.pieces_ref = bf16[8,176,256]{2,1,0:T(8,128)(2,1)S(1)} async-done(((bf16[8,176,256]{2,1,0:T(8,128)(2,1)}), bf16[8,176,256]{2,1,0:T(8,128)(2,1)S(1)}, u32[]{:S(2)}, u32[]{:S(2)}) %all-to-all-start) | async-done | bytes 720928 | tf_op jit(solution)/shard_map/all_to_all | solution.py:707
  29.3 0.2 make_coeffs.1.own_ref
  29.5 0.1 collective-permute-start.2
  29.6 1.6 %collective-permute-start.3 = (bf16[40,256]{1,0:T(8,128)(2,1)S(1)}, bf16[40,256]{1,0:T(8,128)(2,1)S(1)}, u32[]{:S(2)}, u32[]{:S(2)}) collective-permute-start(bf16[40,256]{1,0:T(8,128)(2,1)S(1)} %make_coeffs.1.own_ref), channel_id=1, source_target_pairs={{0,16},{8,24},{16,0},{24,8},{1,17},{9,25},{17,1},{25,9},{2,18},{10... | collective-permute-start | bytes 61448 | tf_op jit(solution)/shard_map/ppermute | solution.py:690
  31.1 0.3 collective-permute-start.4
  31.4 1.0 %collective-permute-done.5.before_ref.shared_before_ref = bf16[10,8,2048]{2,1,0:T(8,128)(2,1)S(1)} collective-permute-done((bf16[10,8,2048]{2,1,0:T(8,128)(2,1)}, bf16[10,8,2048]{2,1,0:T(8,128)(2,1)S(1)}, u32[]{:S(2)}, u32[]{:S(2)}) %collective-permute-start.5) | collective-permute-done | bytes 327712 | tf_op jit(solution)/shard_map/ppermute | solution.py:709
  32.4 0.0 collective-permute-done.6.after_ref.shared_after_ref
  32.4 9.2 %seam_states.1 = (f32[16,40,128]{2,1,0:T(8,128)S(1)}, f32[5,16,40,128]{3,2,1,0:T(8,128)S(1)}, bf16[16,40,128]{2,1,0:T(8,128)(2,1)S(1)}) custom-call(s32[8]{0:T(128)} %index_ref.5, bf16[8,2,3,32,2048]{4,3,2,1,0:T(8,128)(2,1)} %first_ref.1, bf16[8,2,3,32,2048]{4,3,2,1,0:T(8,128)(2,1)} %first_ref.1, ...), custom_call_target="tpu_custom_call" | custom-call | tf_op jit(solution)/shard_map/seam_states/pallas_call | solution.py:438
  41.6 0.0 collective-permute-done.2.near_ref
  41.7 2.1 %apply_potential.1 = (f32[16,2048]{1,0:T(8,128)S(1)}, f32[16,2048]{1,0:T(8,128)S(1)}) custom-call(s32[1]{0:T(128)} %bitcast.1.member_ref, bf16[40,256]{1,0:T(8,128)(2,1)S(1)} %make_coeffs.1.own_ref, bf16[40,256]{1,0:T(8,128)(2,1)S(1)} %collective-permute-done.2.near_ref, bf16[40,256]{1,0:T(8,128)(2,1)S(1)} %collective-permute-done.3.far_ref, ...), custom_call_target="tpu_custom_call" | custom-call | tf_op jit(solution)/shard_map/apply_potential/pallas_call | solution.py:569
  43.8 0.1 collective-permute-start.7
  43.9 1.3 %collective-permute-done.7 = f32[16,2048]{1,0:T(8,128)S(1)} collective-permute-done((f32[16,2048]{1,0:T(8,128)S(1)}, f32[16,2048]{1,0:T(8,128)S(1)}, u32[]{:S(2)}, u32[]{:S(2)}) %collective-permute-start.7) | collective-permute-done | bytes 131104 | tf_op jit(solution)/shard_map/ppermute | solution.py:690
  45.3 1.6 %collective-permute-start.8 = (f32[8,2048]{1,0:T(8,128)S(1)}, f32[8,2048]{1,0:T(8,128)S(1)}, u32[]{:S(2)}, u32[]{:S(2)}) collective-permute-start(f32[8,2048]{1,0:T(8,128)S(1)} %get-tuple-element.29), channel_id=1, source_target_pairs={{0,16},{8,24},{16,0},{24,8},{1,17},{9,25},{17,1},{25,9},{2,18},{10... | collective-permute-start | bytes 196616 | tf_op jit(solution)/shard_map/ppermute | solution.py:690
  46.9 0.6 collective-permute-start
  47.5 2.2 %hold.1.cols_ref = bf16[2048,1024]{1,0:T(8,128)(2,1)S(1)} custom-call(bf16[2048,1024]{1,0:T(8,128)(2,1)} %source_ref.1), custom_call_target="tpu_custom_call" | custom-call | tf_op jit(solution)/shard_map/hold/pallas_call | solution.py:191
  49.7 0.2 collective-permute-done.8.other_ref
  49.8 1.4 %project.1 = bf16[4,8,8,512]{3,2,1,0:T(8,128)(2,1)} custom-call(f32[8,2048]{1,0:T(8,128)S(1)} %get-tuple-element.30.own_ref, f32[8,2048]{1,0:T(8,128)S(1)} %collective-permute-done.8.other_ref, bf16[2048,1024]{1,0:T(8,128)(2,1)S(1)} %hold.1.cols_ref), custom_call_target="tpu_custom_call" | custom-call | tf_op jit(solution)/shard_map/project/pallas_call | solution.py:597
  51.2 8.6 %all-to-all-start.1 = ((bf16[32,8,512]{2,1,0:T(8,128)(2,1)}), bf16[32,8,512]{2,1,0:T(8,128)(2,1)S(1)}, u32[]{:S(2)}, u32[]{:S(2)}) async-start(bf16[32,8,512]{2,1,0:T(8,128)(2,1)} %bitcast.8), calls=%async_computation.1 | async-start | bytes 524288 | tf_op jit(solution)/shard_map/all_to_all | solution.py:727
  59.8 0.3 collective-permute-start.1
  60.1 1.3 %collective-permute-done.1.near_ref = bf16[2,256,256]{2,1,0:T(8,128)(2,1)S(1)} collective-permute-done((bf16[2,256,256]{2,1,0:T(8,128)(2,1)S(1)}, bf16[2,256,256]{2,1,0:T(8,128)(2,1)S(1)}, u32[]{:S(2)}, u32[]{:S(2)}) %collective-permute-start.1) | collective-permute-done | bytes 262176 | tf_op jit(solution)/shard_map/ppermute | solution.py:690
  61.4 1.1 %assemble.1 = (bf16[1024,256]{1,0:T(8,128)(2,1)S(1)}, f32[128,1024]{1,0:T(8,128)S(1)}) custom-call(s32[1]{0:T(128)} %bitcast.1.member_ref, bf16[256,256]{1,0:T(8,128)(2,1)S(1)} %bitcast.13, bf16[256,256]{1,0:T(8,128)(2,1)S(1)} %collective-permute-done.far_ref, bf16[2,256,256]{2,1,0:T(8,128)(2,1)S(1)} %collective-permute-done.1.near_ref, f32[128,1024]{1,0:T(8,128)} %control_ref.3), custom_call_target="tpu_custom_call" | custom-call | tf_op jit(solution)/shard_map/assemble/pallas_call | solution.py:622
  62.5 7.7 %all-to-all-done.1 = bf16[32,8,512]{2,1,0:T(8,128)(2,1)S(1)} async-done(((bf16[32,8,512]{2,1,0:T(8,128)(2,1)}), bf16[32,8,512]{2,1,0:T(8,128)(2,1)S(1)}, u32[]{:S(2)}, u32[]{:S(2)}) %all-to-all-start.1) | async-done | bytes 262176 | tf_op jit(solution)/shard_map/all_to_all | solution.py:727
  70.2 0.5 gradient.1.own_ref
  70.7 0.1 collective-permute-start.9
  70.8 1.5 %collective-permute-done.9.other_ref = f32[136,512]{1,0:T(8,128)S(1)} collective-permute-done((f32[136,512]{1,0:T(8,128)S(1)}, f32[136,512]{1,0:T(8,128)S(1)}, u32[]{:S(2)}, u32[]{:S(2)}) %collective-permute-start.9) | collective-permute-done | bytes 278560 | tf_op jit(solution)/shard_map/ppermute | solution.py:690
  72.3 1.0 %update.1 = f32[128,1024]{1,0:T(8,128)} custom-call(s32[1]{0:T(128)} %bitcast.core_ref, f32[128,1024]{1,0:T(8,128)S(1)} %get-tuple-element.17.control_ref, f32[136,512]{1,0:T(8,128)S(1)} %gradient.1.own_ref, f32[136,512]{1,0:T(8,128)S(1)} %collective-permute-done.9.other_ref), custom_call_target="tpu_custom_call" | custom-call | tf_op jit(solution)/shard_map/update/pallas_call | solution.py:678
  (10 shorter events, 0.1 us)
Async XLA Ops:
  1.9 27.4 %all-to-all-start = ((bf16[8,176,256]{2,1,0:T(8,128)(2,1)}), bf16[8,176,256]{2,1,0:T(8,128)(2,1)S(1)}, u32[]{:S(2)}, u32[]{:S(2)}) async-start(bf16[8,176,256]{2,1,0:T(8,128)(2,1)} %pack_pieces.1), calls=%async_computation | async-start | bytes 1441792 | tf_op jit(solution)/shard_map/all_to_all | solution.py:707
  12.6 19.8 %collective-permute-start.5 = (bf16[10,8,2048]{2,1,0:T(8,128)(2,1)}, bf16[10,8,2048]{2,1,0:T(8,128)(2,1)S(1)}, u32[]{:S(2)}, u32[]{:S(2)}) collective-permute-start(bf16[10,8,2048]{2,1,0:T(8,128)(2,1)} %get-tuple-element.20), channel_id=1, source_target_pairs={{0,1},{1,2},{2,3},{3,4},{4,5},{5,6},{6,7},{8,9},{9,10},{10,11},{11... | collective-permute-start | bytes 983048 | tf_op jit(solution)/shard_map/ppermute | solution.py:709
  16.6 15.9 %collective-permute-start.6 = (bf16[10,8,2048]{2,1,0:T(8,128)(2,1)}, bf16[10,8,2048]{2,1,0:T(8,128)(2,1)S(1)}, u32[]{:S(2)}, u32[]{:S(2)}) collective-permute-start(bf16[10,8,2048]{2,1,0:T(8,128)(2,1)} %get-tuple-element.21), channel_id=1, source_target_pairs={{1,0},{2,1},{3,2},{4,3},{5,4},{6,5},{7,6},{9,8},{10,9},{11,10},{12... | collective-permute-start | bytes 983048 | tf_op jit(solution)/shard_map/ppermute | solution.py:710
  29.5 12.1 %collective-permute-start.2 = (bf16[40,256]{1,0:T(8,128)(2,1)S(1)}, bf16[40,256]{1,0:T(8,128)(2,1)S(1)}, u32[]{:S(2)}, u32[]{:S(2)}) collective-permute-start(bf16[40,256]{1,0:T(8,128)(2,1)S(1)} %make_coeffs.1.own_ref), channel_id=1, source_target_pairs={{0,8},{8,0},{16,24},{24,16},{1,9},{9,1},{17,25},{25,17},{2,10},{10... | collective-permute-start | bytes 61448 | tf_op jit(solution)/shard_map/ppermute | solution.py:690
  29.6 12.1 %collective-permute-start.3 = (bf16[40,256]{1,0:T(8,128)(2,1)S(1)}, bf16[40,256]{1,0:T(8,128)(2,1)S(1)}, u32[]{:S(2)}, u32[]{:S(2)}) collective-permute-start(bf16[40,256]{1,0:T(8,128)(2,1)S(1)} %make_coeffs.1.own_ref), channel_id=1, source_target_pairs={{0,16},{8,24},{16,0},{24,8},{1,17},{9,25},{17,1},{25,9},{2,18},{10... | collective-permute-start | bytes 61448 | tf_op jit(solution)/shard_map/ppermute | solution.py:690
  31.1 10.5 %collective-permute-start.4 = (bf16[40,256]{1,0:T(8,128)(2,1)S(1)}, bf16[40,256]{1,0:T(8,128)(2,1)S(1)}, u32[]{:S(2)}, u32[]{:S(2)}) collective-permute-start(bf16[40,256]{1,0:T(8,128)(2,1)S(1)} %make_coeffs.1.own_ref), channel_id=1, source_target_pairs={{0,24},{8,16},{16,8},{24,0},{1,25},{9,17},{17,9},{25,1},{2,26},{10... | collective-permute-start | bytes 61448 | tf_op jit(solution)/shard_map/ppermute | solution.py:690
  32.4 9.2 %copy-start = (bf16[2048,1024]{1,0:T(8,128)(2,1)S(1)}, bf16[2048,1024]{1,0:T(8,128)(2,1)}, u32[]{:S(2)}) copy-start(bf16[2048,1024]{1,0:T(8,128)(2,1)} %source_ref.1) | copy-start | bytes 12582916
  43.8 1.4 %collective-permute-start.7 = (f32[16,2048]{1,0:T(8,128)S(1)}, f32[16,2048]{1,0:T(8,128)S(1)}, u32[]{:S(2)}, u32[]{:S(2)}) collective-permute-start(f32[16,2048]{1,0:T(8,128)S(1)} %get-tuple-element.28), channel_id=1, source_target_pairs={{0,8},{8,0},{16,24},{24,16},{1,9},{9,1},{17,25},{25,17},{2,10},{10... | collective-permute-start | bytes 393224 | tf_op jit(solution)/shard_map/ppermute | solution.py:690
  45.3 4.5 %collective-permute-start.8 = (f32[8,2048]{1,0:T(8,128)S(1)}, f32[8,2048]{1,0:T(8,128)S(1)}, u32[]{:S(2)}, u32[]{:S(2)}) collective-permute-start(f32[8,2048]{1,0:T(8,128)S(1)} %get-tuple-element.29), channel_id=1, source_target_pairs={{0,16},{8,24},{16,0},{24,8},{1,17},{9,25},{17,1},{25,9},{2,18},{10... | collective-permute-start | bytes 196616 | tf_op jit(solution)/shard_map/ppermute | solution.py:690
  46.9 12.9 %collective-permute-start = (bf16[256,256]{1,0:T(8,128)(2,1)S(1)}, bf16[256,256]{1,0:T(8,128)(2,1)S(1)}, u32[]{:S(2)}, u32[]{:S(2)}) collective-permute-start(bf16[256,256]{1,0:T(8,128)(2,1)S(1)} %bitcast.11), channel_id=1, source_target_pairs={{0,16},{8,24},{16,0},{24,8},{1,17},{9,25},{17,1},{25,9},{2,18},{10... | collective-permute-start | bytes 393224 | tf_op jit(solution)/shard_map/ppermute | solution.py:690
  51.2 19.0 %all-to-all-start.1 = ((bf16[32,8,512]{2,1,0:T(8,128)(2,1)}), bf16[32,8,512]{2,1,0:T(8,128)(2,1)S(1)}, u32[]{:S(2)}, u32[]{:S(2)}) async-start(bf16[32,8,512]{2,1,0:T(8,128)(2,1)} %bitcast.8), calls=%async_computation.1 | async-start | bytes 524288 | tf_op jit(solution)/shard_map/all_to_all | solution.py:727
  59.8 1.6 %collective-permute-start.1 = (bf16[2,256,256]{2,1,0:T(8,128)(2,1)S(1)}, bf16[2,256,256]{2,1,0:T(8,128)(2,1)S(1)}, u32[]{:S(2)}, u32[]{:S(2)}) collective-permute-start(bf16[2,256,256]{2,1,0:T(8,128)(2,1)S(1)} %pad_maximum_fusion), channel_id=1, source_target_pairs={{0,8},{8,0},{16,24},{24,16},{1,9},{9,1},{17,25},{25,17},{2,10},{10... | collective-permute-start | bytes 786440 | tf_op jit(solution)/shard_map/ppermute | solution.py:690
  70.7 1.6 %collective-permute-start.9 = (f32[136,512]{1,0:T(8,128)S(1)}, f32[136,512]{1,0:T(8,128)S(1)}, u32[]{:S(2)}, u32[]{:S(2)}) collective-permute-start(f32[136,512]{1,0:T(8,128)S(1)} %gradient.1.own_ref), channel_id=1, source_target_pairs={{0,8},{8,0},{16,24},{24,16},{1,9},{9,1},{17,25},{25,17},{2,10},{10... | collective-permute-start | bytes 835592 | tf_op jit(solution)/shard_map/ppermute | solution.py:690

commit v4 on v3

--- a/solution.py
+++ b/solution.py
@@ -53,16 +53,8 @@
     return jnp.where(lane < -step, beside, turned)
 
 
-def shift_rows(field, step):
-    return pltpu.roll(field, (-step) % field.shape[1], 1)
-
-
 def dx(field):
     return shift_cols(field, 1) - shift_cols(field, -1)
-
-
-def dy(field):
-    return shift_rows(field, 1) - shift_rows(field, -1)
 
 
 def fetch(source, target, sem):
@@ -217,6 +209,16 @@
         return self.ref[:, start : start + TILE, :]
 
 
+class Ring(Rows):
+    def put(self, tile, value):
+        super().put(tile, value)
+        rows = self.ref.shape[1]
+        if tile == 0:
+            self.ref[:, rows - TILE :, :] = value
+        if TILE * (tile + 3) == rows:
+            self.ref[:, :TILE, :] = value
+
+
 def rows_of(tile):
     return slice(TILE * tile, TILE * (tile + 1))
 
@@ -236,7 +238,7 @@
     turn = TIME_STEP * CORIOLIS / keep
     slope = half * GRAVITY / keep
 
-    for tile in range(-1, tiles + 1):
+    for tile in range(tiles):
         fluxes.put(tile, (DEPTH + heights.get(tile)) * norths.get(tile))
 
     for tile in range(tiles):
@@ -252,20 +254,21 @@
         north_mid = north - turn * east - slope * (heights.get(tile, 1) - heights.get(tile, -1))
         right = shift_cols(weight, 1)
         left = shift_cols(weight, -1)
-        mid_fluxes.put(tile, weight * north_mid)
+        scaled = half * keep * weight
+        mid_fluxes.put(tile, scaled * north_mid)
         weights.put(tile, weight)
         rights.put(tile, right)
         lefts[:, here, :] = left
         same[:, here, :] += weight * weight
         two_x[:, here, :] += left * right
         partial[:, here, :] = (
-            height + height_mid - 2.0 * seens.get(tile) - half * keep * dx(weight * east_mid)
+            height + height_mid - 2.0 * seens.get(tile) - dx(scaled * east_mid)
         )
 
     for tile in range(tiles):
         here = rows_of(tile)
         change = mid_fluxes.get(tile, 1) - mid_fluxes.get(tile, -1)
-        misfit = live[:, here, :] * (partial[:, here, :] - half * keep * change)
+        misfit = live[:, here, :] * (partial[:, here, :] - change)
         misfits.put(tile, misfit)
         push_left[:, here, :] += lefts[:, here, :] * misfit
         push_right[:, here, :] += rights.get(tile) * misfit
@@ -279,28 +282,47 @@
         down[:, here, :] += weight * rights.get(tile, -1)
 
 
-def inner_states(index_ref, state_ref, targets_ref, sea_ref, basis_ref, push_ref, pairs_ref, rows_ref, mask, live, *scratch):
+def inner_states(index_ref, states_ref, targets_ref, sea_ref, basis_ref, push_ref, pairs_ref, rows_ref, sems, sea, held_states, held_targets, mask, live, *scratch):
+    count = states_ref.shape[0]
     rows = sea_ref.shape[0]
     tiles = rows // TILE
     plain, padded = scratch[:2], scratch[2:]
 
-    @pl.when(pl.program_id(0) == 0)
-    def _():
-        clear(push_ref, pairs_ref, *padded)
-        rows_ref[...] = basis_ref[...]
+    def copies_of(k):
+        return (
+            pltpu.make_async_copy(states_ref.at[k, index_ref[k]], held_states.at[k], sems.at[0, k]),
+            pltpu.make_async_copy(targets_ref.at[k], held_targets.at[k], sems.at[1, k]),
+        )
+
+    others = (
+        pltpu.make_async_copy(sea_ref, sea, sems.at[0, count]),
+        pltpu.make_async_copy(basis_ref, rows_ref, sems.at[1, count]),
+    )
+    for copy in others:
+        copy.start()
+    for k in range(count):
+        for copy in copies_of(k):
+            copy.start()
+    clear(push_ref, pairs_ref, *padded)
+    for copy in others:
+        copy.wait()
+    for tile in range(tiles):
+        mask[:, rows_of(tile), :] = split_lanes(sea[rows_of(tile), :].astype(F32))
+    row = lax.broadcasted_iota(jnp.int32, live.shape, 1)
+    live[...] = jnp.where((row >= 2) & (row < rows - 2), mask[...], 0.0)
+
+    @pl.loop(0, count)
+    def _(s):
+        for copy in copies_of(s):
+            copy.wait()
+        state = [Rows(ref) for ref in padded[:4]]
         for tile in range(tiles):
-            mask[:, rows_of(tile), :] = split_lanes(sea_ref[rows_of(tile), :].astype(F32))
-        row = lax.broadcasted_iota(jnp.int32, live.shape, 1)
-        live[...] = jnp.where((row >= 2) & (row < rows - 2), mask[...], 0.0)
-
-    state = [Rows(ref) for ref in padded[:4]]
-    for tile in range(tiles):
-        for field in range(3):
-            value = state_ref[0, 0, field, rows_of(tile), :].astype(F32)
-            state[field].put(tile, split_lanes(value))
-        state[3].put(tile, split_lanes(targets_ref[0, rows_of(tile), :].astype(F32)))
-    sums = [push_ref.at[k] for k in range(3)] + [pairs_ref.at[k] for k in range(PAIRS)]
-    add_state(tiles, state, mask, live, padded[4:], plain, sums)
+            for field in range(3):
+                value = held_states[s, field, rows_of(tile), :].astype(F32)
+                state[field].put(tile, split_lanes(value))
+            state[3].put(tile, split_lanes(held_targets[s, rows_of(tile), :].astype(F32)))
+        sums = [push_ref.at[k] for k in range(3)] + [pairs_ref.at[k] for k in range(PAIRS)]
+        add_state(tiles, state, mask, live, padded[4:], plain, sums)
 
 
 def inner_pass(section_index, checkpoints, targets, sea_mask, basis_rows):
@@ -318,162 +340,146 @@
         inner_states,
         name="inner_states",
         out_shape=outs,
-        grid_spec=pltpu.PrefetchScalarGridSpec(
-            num_scalar_prefetch=1,
-            grid=(count,),
-            in_specs=[
-                pl.BlockSpec((1, 1, fields, rows, cols), lambda s, index: (s, index[s], 0, 0, 0)),
-                pl.BlockSpec((1, rows, cols), lambda s, index: (s, 0, 0)),
-                pl.BlockSpec((rows, cols), lambda s, index: (0, 0)),
-                pl.BlockSpec((rows, width), lambda s, index: (0, 0)),
-            ],
-            out_specs=tuple(
-                pl.BlockSpec(out.shape, lambda s, index, n=len(out.shape): (0,) * n) for out in outs
-            ),
-            scratch_shapes=[plain] * 4 + [padded] * 9,
-        ),
-        compiler_params=limit(18),
+        in_specs=[SMEM] + [HBM] * 4,
+        out_specs=(VMEM,) * 3,
+        scratch_shapes=[
+            pltpu.SemaphoreType.DMA((2, count + 1)),
+            pltpu.VMEM((rows, cols), jnp.int32),
+            pltpu.VMEM((count, fields, rows, cols), BF16),
+            pltpu.VMEM((count, rows, cols), BF16),
+        ]
+        + [plain] * 4
+        + [padded] * 9,
+        compiler_params=limit(24),
     )(*map(in_hbm, (section_index, checkpoints, targets, sea_mask, basis_rows)))
 
 
-def seam_states(index_ref, last_ref, first_ref, before_ref, after_ref, shared_before_ref, shared_after_ref, seen_last_ref, seen_first_ref, sea_ref, push_in_ref, pairs_in_ref, base_ref, pairs_ref, mask_ref, seen_edge, mask, live, lefts, partial, sums_ref, ring_sums, *padded):
-    s = pl.program_id(0)
+def seam_states(index_ref, states_ref, targets_ref, sea_ref, before_ref, after_ref, push_in_ref, pairs_in_ref, push_ref, pairs_ref, mask_ref, sems, sea, ends, seen_ends, seen_edge, mask, live, lefts, partial, sums_ref, *padded):
+    count = states_ref.shape[0]
     rows, cols = sea_ref.shape
     row = tile_rows((TILE, cols))
     top = row < 4
 
-    @pl.when(s == 0)
-    def _():
-        clear(sums_ref, *padded)
-        seen_edge[0] = split_lanes(shared_before_ref[0].astype(F32))
-        seen_edge[1] = split_lanes(shared_after_ref[0].astype(F32))
-        after = jnp.where(row < 2, shared_after_ref[1].astype(F32), 0.0)
-        before = jnp.where(row >= 6, shared_before_ref[1].astype(F32), 0.0)
-        beyond = after + before
-        turned = pltpu.roll(beyond, 4, 0)
-        last = pltpu.roll(sea_ref[rows - TILE :, :].astype(F32), 4, 0)
-        first = pltpu.roll(sea_ref[:TILE, :].astype(F32), 4, 0)
-        mask[:, :TILE, :] = split_lanes(jnp.where(top, last, turned))
-        mask[:, TILE:, :] = split_lanes(jnp.where(top, turned, first))
-        for tile in range(rows // TILE):
-            mask_ref[:, rows_of(tile), :] = split_lanes(
-                sea_ref[rows_of(tile), :].astype(F32)
-            ).astype(BF16)
-        mask_ref[:, rows:, :] = split_lanes(beyond).astype(BF16)
-        place = lax.broadcasted_iota(jnp.int32, live.shape, 1)
-        counts = ((place >= 2) & (place < 5)) | ((place >= 11) & (place < 14))
-        live[...] = jnp.where(counts, mask[...], 0.0)
-
-    state = [Rows(ref) for ref in padded[:4]]
-    after = split_lanes(after_ref[0].astype(F32))
-    before = split_lanes(before_ref[0].astype(F32))
-    state[0].put_at(12, after)
-    state[0].put_at(17, before)
-    state[1].put_at(12, before)
-    state[1].put_at(6, after)
-    state[2].put_at(14, before)
-    state[2].put_at(9, after)
-    state[3].put_at(12, seen_edge[1, :, pl.ds(s, 1), :])
-    state[3].put_at(19, seen_edge[0, :, pl.ds(s, 1), :])
-    for field in range(3):
-        state[field].put_at(4, split_lanes(last_ref[0, 0, field].astype(F32)))
-        state[field].put_at(20, split_lanes(first_ref[0, 0, field].astype(F32)))
-    state[3].put_at(4, split_lanes(seen_last_ref[0].astype(F32)))
-    state[3].put_at(20, split_lanes(seen_first_ref[0].astype(F32)))
-    sums = [sums_ref.at[k] for k in range(3 + PAIRS)]
-    add_state(2, state, mask, live, padded[4:], (lefts, partial), sums)
-
-    @pl.when(s == pl.num_programs(0) - 1)
-    def _():
-        place = lax.broadcasted_iota(jnp.int32, (lefts.shape[0], TILE, LANES), 1)
-        top = place < 4
-        final = rows // TILE - 1
-
-        def ring(inner, outer, out, bounds):
-            ending = pltpu.roll(outer[:, :TILE, :], 4, 1)
-            opening = pltpu.roll(outer[:, TILE:, :], 4, 1)
-            for tile in range(1, final):
-                out[:, rows_of(tile), :] = inner[:, rows_of(tile), :]
-            head = inner[:, :TILE, :]
-            tail = inner[:, rows_of(final), :]
-            if bounds is None:
-                head = head + jnp.where(top, opening, 0.0)
-                tail = tail + jnp.where(top, 0.0, ending)
-            else:
-                head = jnp.where(place < bounds[0], opening, head)
-                tail = jnp.where(place > bounds[1], ending, tail)
-            out[:, :TILE, :] = head
-            out[:, rows_of(final), :] = tail
-            out[:, rows:, :] = jnp.where(top, ending, opening)
-
-        for k in range(3):
-            ring(push_in_ref[k], sums_ref[k], ring_sums.at[k], None)
-        for k in range(PAIRS):
-            bounds = (2, 5) if k == PAIRS - 1 else (1, 4)
-            ring(pairs_in_ref[k], sums_ref[3 + k], pairs_ref.at[k], bounds)
-        scale = 0.0625 * TIME_STEP * TIME_STEP
-        gx = shift_cols(ring_sums[0], 1) - shift_cols(ring_sums[1], -1)
-        base_ref[...] = scale * (dy(gx) - dx(ring_sums[2]))
+    def copies_of(k):
+        for side, start in enumerate((rows - TILE, 0)):
+            here = pl.ds(start, TILE)
+            yield pltpu.make_async_copy(
+                states_ref.at[k, index_ref[k], :, here, :], ends.at[k, side], sems.at[side, k]
+            )
+            yield pltpu.make_async_copy(
+                targets_ref.at[k, here, :], seen_ends.at[k, side], sems.at[2 + side, k]
+            )
+
+    fetched = pltpu.make_async_copy(sea_ref, sea, sems.at[0, count])
+    fetched.start()
+    for k in range(count):
+        for copy in copies_of(k):
+            copy.start()
+    clear(sums_ref, *padded)
+    seen_edge[0] = split_lanes(before_ref[count].astype(F32))
+    seen_edge[1] = split_lanes(after_ref[count].astype(F32))
+    after = jnp.where(row < 2, after_ref[count + 1].astype(F32), 0.0)
+    before = jnp.where(row >= 6, before_ref[count + 1].astype(F32), 0.0)
+    beyond = after + before
+    fetched.wait()
+    turned = pltpu.roll(beyond, 4, 0)
+    last = pltpu.roll(sea[rows - TILE :, :].astype(F32), 4, 0)
+    first = pltpu.roll(sea[:TILE, :].astype(F32), 4, 0)
+    mask[:, :TILE, :] = split_lanes(jnp.where(top, last, turned))
+    mask[:, TILE:, :] = split_lanes(jnp.where(top, turned, first))
+    for tile in range(rows // TILE):
+        mask_ref[:, rows_of(tile), :] = split_lanes(
+            sea[rows_of(tile), :].astype(F32)
+        ).astype(BF16)
+    mask_ref[:, rows:, :] = split_lanes(beyond).astype(BF16)
+    place = lax.broadcasted_iota(jnp.int32, live.shape, 1)
+    counts = ((place >= 2) & (place < 5)) | ((place >= 11) & (place < 14))
+    live[...] = jnp.where(counts, mask[...], 0.0)
+
+    @pl.loop(0, count)
+    def _(s):
+        state = [Rows(ref) for ref in padded[:4]]
+        after = split_lanes(after_ref[s].astype(F32))
+        before = split_lanes(before_ref[s].astype(F32))
+        for copy in copies_of(s):
+            copy.wait()
+        state[0].put_at(12, after)
+        state[0].put_at(17, before)
+        state[1].put_at(12, before)
+        state[1].put_at(6, after)
+        state[2].put_at(14, before)
+        state[2].put_at(9, after)
+        state[3].put_at(12, seen_edge[1, :, pl.ds(s, 1), :])
+        state[3].put_at(19, seen_edge[0, :, pl.ds(s, 1), :])
+        for field in range(3):
+            state[field].put_at(4, split_lanes(ends[s, 0, field].astype(F32)))
+            state[field].put_at(20, split_lanes(ends[s, 1, field].astype(F32)))
+        state[3].put_at(4, split_lanes(seen_ends[s, 0].astype(F32)))
+        state[3].put_at(20, split_lanes(seen_ends[s, 1].astype(F32)))
+        sums = [sums_ref.at[k] for k in range(3 + PAIRS)]
+        add_state(2, state, mask, live, padded[4:], (lefts, partial), sums)
+
+    place = lax.broadcasted_iota(jnp.int32, (lefts.shape[0], TILE, LANES), 1)
+    top = place < 4
+    final = rows // TILE - 1
+
+    def ring(inner, outer, out, bounds):
+        ending = pltpu.roll(outer[:, :TILE, :], 4, 1)
+        opening = pltpu.roll(outer[:, TILE:, :], 4, 1)
+        for tile in range(1, final):
+            out[:, rows_of(tile), :] = inner[:, rows_of(tile), :]
+        head = inner[:, :TILE, :]
+        tail = inner[:, rows_of(final), :]
+        if bounds is None:
+            head = head + jnp.where(top, opening, 0.0)
+            tail = tail + jnp.where(top, 0.0, ending)
+        else:
+            head = jnp.where(place < bounds[0], opening, head)
+            tail = jnp.where(place > bounds[1], ending, tail)
+        out[:, :TILE, :] = head
+        out[:, rows_of(final), :] = tail
+        out[:, rows:, :] = jnp.where(top, ending, opening)
+
+    for k in range(3):
+        ring(push_in_ref[k], sums_ref[k], push_ref.at[k], None)
+    for k in range(PAIRS):
+        bounds = (2, 5) if k == PAIRS - 1 else (1, 4)
+        ring(pairs_in_ref[k], sums_ref[3 + k], pairs_ref.at[k], bounds)
 
 
 def seam_pass(section_index, checkpoints, before, after, targets, sea_mask, push, pairs):
     count, _, fields, rows, cols = checkpoints.shape
     lanes = cols // LANES
-    final = rows // TILE - 1
     ring = rows + TILE
     plain = pltpu.VMEM((lanes, 2 * TILE, LANES), F32)
     padded = pltpu.VMEM((lanes, 4 * TILE, LANES), F32)
-    state = (1, 1, fields, TILE, cols)
-    edge = pl.BlockSpec((1, TILE, cols), lambda s, index: (s, 0, 0))
-    shared = pl.BlockSpec((2, TILE, cols), lambda s, index: (count // 2, 0, 0))
-
-    def fixed(array):
-        return pl.BlockSpec(array.shape, lambda s, index, n=len(array.shape): (0,) * n)
-
     outs = (
-        jax.ShapeDtypeStruct((lanes, ring, LANES), F32),
+        jax.ShapeDtypeStruct((3, lanes, ring, LANES), F32),
         jax.ShapeDtypeStruct((PAIRS, lanes, ring, LANES), F32),
         jax.ShapeDtypeStruct((lanes, ring, LANES), BF16),
     )
+
     return pl.pallas_call(
         seam_states,
         name="seam_states",
         out_shape=outs,
-        grid_spec=pltpu.PrefetchScalarGridSpec(
-            num_scalar_prefetch=1,
-            grid=(count,),
-            in_specs=[
-                pl.BlockSpec(state, lambda s, index: (s, index[s], 0, final, 0)),
-                pl.BlockSpec(state, lambda s, index: (s, index[s], 0, 0, 0)),
-                edge,
-                edge,
-                shared,
-                shared,
-                pl.BlockSpec((1, TILE, cols), lambda s, index: (s, final, 0)),
-                pl.BlockSpec((1, TILE, cols), lambda s, index: (s, 0, 0)),
-                fixed(sea_mask),
-                fixed(push),
-                fixed(pairs),
-            ],
-            out_specs=tuple(fixed(out) for out in outs),
-            scratch_shapes=[pltpu.VMEM((2, lanes, TILE, LANES), F32)]
-            + [plain] * 4
-            + [pltpu.VMEM((3 + PAIRS, lanes, 2 * TILE, LANES), F32)]
-            + [pltpu.VMEM((3, lanes, ring, LANES), F32)]
-            + [padded] * 9,
-        ),
-        compiler_params=limit(22),
+        in_specs=[SMEM] + [HBM] * 3 + [VMEM] * 4,
+        out_specs=(VMEM,) * 3,
+        scratch_shapes=[
+            pltpu.SemaphoreType.DMA((4, count + 1)),
+            pltpu.VMEM((rows, cols), jnp.int32),
+            pltpu.VMEM((count, 2, fields, TILE, cols), BF16),
+            pltpu.VMEM((count, 2, TILE, cols), BF16),
+            pltpu.VMEM((2, lanes, TILE, LANES), F32),
+        ]
+        + [plain] * 4
+        + [pltpu.VMEM((3 + PAIRS, lanes, 2 * TILE, LANES), F32)]
+        + [padded] * 9,
+        compiler_params=limit(24),
     )(
-        in_hbm(section_index),
-        in_hbm(checkpoints),
-        in_hbm(checkpoints),
+        *map(in_hbm, (section_index, checkpoints, targets, sea_mask)),
         before,
         after,
-        before,
-        after,
-        in_hbm(targets),
-        in_hbm(targets),
-        in_hbm(sea_mask),
         push,
         pairs,
     )
@@ -515,54 +521,95 @@
     )(slab.reshape(1), basis_rows, pieces)
 
 
-def apply_potential(member_ref, own_ref, near_ref, far_ref, both_ref, cols_ref, base_ref, pairs_ref, mask_ref, keep_ref, give_ref, coeffs, total):
+def apply_potential(member_ref, own_ref, near_ref, far_ref, both_ref, cols_ref, push_ref, pairs_ref, mask_ref, keep_ref, give_ref, coeffs, total, field, east, part, gy, *rings):
     member = member_ref[0]
     quarter = own_ref.shape[1]
     for bits, ref in enumerate((own_ref, near_ref, far_ref, both_ref)):
         at = pl.multiple_of((member ^ bits) * quarter, quarter)
         coeffs[:, pl.ds(at, quarter)] = ref[...]
-    potential = split_lanes(
-        lax.dot_general(
-            coeffs[...], cols_ref[...], (((1,), (1,)), ((), ())), preferred_element_type=F32
+    field[...] = lax.dot_general(
+        coeffs[...], cols_ref[...], (((1,), (1,)), ((), ())), preferred_element_type=F32
+    )
+    same, two_x, two_y, up, down = (pairs_ref.at[k] for k in range(PAIRS))
+    potential, masks, right_xs, right_ys, norths, two_norths, gx = (
+        Ring(ref) for ref in rings[:7]
+    )
+    back_up_x, back_up_y, back_down_x, back_down_y = (Ring(ref) for ref in rings[7:])
+    tiles = field.shape[0] // TILE
+    own_tiles = tiles - 1
+    unit = -4.0 / TIME_STEP**2
+
+    for tile in range(tiles):
+        potential.put(tile, split_lanes(field[rows_of(tile), :]))
+        masks.put(tile, mask_ref[:, rows_of(tile), :].astype(F32))
+
+    for tile in range(tiles):
+        here = rows_of(tile)
+        sx = potential.get(tile, -1) - potential.get(tile, 1)
+        sy = dx(potential.get(tile))
+        east[:, here, :] = sx
+        right_x = shift_cols(sx, 1)
+        right_xs.put(tile, right_x)
+        right_ys.put(tile, shift_cols(sy, 1))
+        norths.put(tile, sy)
+        two_norths.put(tile, two_y[:, here, :] * sy)
+        up_here = up[:, here, :]
+        down_here = down[:, here, :]
+        back_up_x.put(tile, shift_cols(up_here * sx, -1))
+        back_up_y.put(tile, shift_cols(up_here * sy, -1))
+        back_down_x.put(tile, shift_cols(down_here * sx, -1))
+        back_down_y.put(tile, shift_cols(down_here * sy, -1))
+        beside = masks.get(tile) * two_x[:, here, :]
+        part[:, here, :] = shift_cols(
+            beside * right_x + unit * push_ref[0, :, here, :], 1
+        ) + shift_cols(beside * shift_cols(sx, -1) - unit * push_ref[1, :, here, :], -1)
+
+    for tile in range(tiles):
+        here = rows_of(tile)
+        mask = masks.get(tile)
+        same_x = same[:, here, :] * east[:, here, :]
+        up_here = up[:, here, :]
+        down_here = down[:, here, :]
+        ahead = up_here * right_ys.get(tile, 1) - same_x - down_here * right_ys.get(tile, -1)
+        behind = same_x + back_down_y.get(tile, 1) - back_up_y.get(tile, -1)
+        gx.put(
+            tile,
+            part[:, here, :] + shift_cols(mask, 1) * ahead - shift_cols(mask, -1) * behind,
         )
-    )
-    sx = -dy(potential)
-    sy = dx(potential)
-    mask = mask_ref[...].astype(F32)
-    same, two_x, two_y, up, down = (pairs_ref[k] for k in range(5))
-    same_x = same * sx
-    same_y = same * sy
-    right_x = shift_cols(sx, 1)
-    right_y = shift_cols(sy, 1)
-    up_x = up * shift_rows(right_x, 1)
-    up_y = up * shift_rows(right_y, 1)
-    down_x = down * shift_rows(right_x, -1)
-    down_y = down * shift_rows(right_y, -1)
-    back_up_x = shift_rows(shift_cols(up * sx, -1), -1)
-    back_up_y = shift_rows(shift_cols(up * sy, -1), -1)
-    back_down_x = shift_rows(shift_cols(down * sx, -1), 1)
-    back_down_y = shift_rows(shift_cols(down * sy, -1), 1)
-    beside = mask * two_x
-    gx = (
-        shift_cols(mask, 1) * (up_y - same_x - down_y)
-        + shift_cols(beside * right_x, 1)
-        - shift_cols(mask, -1) * (same_x + back_down_y - back_up_y)
-        + shift_cols(beside * shift_cols(sx, -1), -1)
-    )
-    gy = shift_rows(mask, 1) * (
-        up_x - back_down_x + two_y * shift_rows(sy, 2) - same_y
-    ) - shift_rows(mask, -1) * (down_x - back_up_x + same_y - shift_rows(two_y * sy, -2))
+        if tile < own_tiles:
+            same_y = same[:, here, :] * norths.get(tile)
+            ahead = (
+                up_here * right_xs.get(tile, 1)
+                - back_down_x.get(tile, 1)
+                + two_y[:, here, :] * norths.get(tile, 2)
+                - same_y
+            )
+            behind = (
+                down_here * right_xs.get(tile, -1)
+                - back_up_x.get(tile, -1)
+                + same_y
+                - two_norths.get(tile, -2)
+            )
+            gy[:, here, :] = (
+                unit * push_ref[2, :, here, :]
+                + masks.get(tile, 1) * ahead
+                - masks.get(tile, -1) * behind
+            )
+
     scale = -(TIME_STEP**4) / 64.0
-    grad = base_ref[...] + scale * (dy(gx) - dx(gy))
+    for tile in range(own_tiles):
+        here = rows_of(tile)
+        total[here, :] = join_lanes(
+            scale * (gx.get(tile, 1) - gx.get(tile, -1) - dx(gy[:, here, :]))
+        )
     pair = keep_ref.shape[0]
-    total[...] = join_lanes(grad[:, : 2 * pair, :])
     core = member % 2
     keep_ref[...] = total[pl.ds(pl.multiple_of(core * pair, pair), pair), :]
     give_ref[...] = total[pl.ds(pl.multiple_of((1 - core) * pair, pair), pair), :]
 
 
-def gradient_halves(member, parts, basis_cols, base, pairs, mask):
-    _, ring, _ = base.shape
+def gradient_halves(member, parts, basis_cols, push, pairs, mask):
+    lanes, ring, _ = mask.shape
     cols, width = basis_cols.shape
     pair = (ring - TILE) // 2
     half = jax.ShapeDtypeStruct((pair, cols), F32)
@@ -575,9 +622,12 @@
         scratch_shapes=[
             pltpu.VMEM((ring, width), BF16),
             pltpu.VMEM((2 * pair, cols), F32),
-        ],
+            pltpu.VMEM((ring, cols), F32),
+        ]
+        + [pltpu.VMEM((lanes, ring, LANES), F32)] * 3
+        + [pltpu.VMEM((lanes, ring + 2 * TILE, LANES), F32)] * 11,
         compiler_params=limit(24),
-    )(member.reshape(1), *parts, basis_cols, base, pairs, mask)
+    )(member.reshape(1), *parts, basis_cols, push, pairs, mask)
 
 
 def project(own_ref, other_ref, cols_ref, out_ref):
@@ -713,10 +763,10 @@
     parts = [own]
     for bits in (1, 2, 3):
         parts.append(partner(own, bits))
-    base, pairs, mask = seam_pass(
+    push, pairs, mask = seam_pass(
         section_index, checkpoints, before, after, targets, sea_mask, push, pairs
     )
-    keep, give = gradient_halves(member, parts, basis_cols, base, pairs, mask)
+    keep, give = gradient_halves(member, parts, basis_cols, push, pairs, mask)
 
     keep = keep + partner(give, 1)
     own_rows = lax.dynamic_slice_in_dim(keep, chip * single, single, 0)

time: 74.1 us -> 72.1 us (0.973)
  Pallas kernels: 33.3 us -> 30.7 us
  waiting for transfers between devices: 14 us -> 15 us
    pallas_call x2, Pallas kernels: 19.6 us -> 17.1 us  [the longest x1 9.47 us: inner_pass(): pl.pallas_call(inner_states, name='inner_states', out_shape=outs, in_spec...]
    all_to_all x1, waiting for transfers between devices: 0.99 us -> 1.97 us  [on_device(): pieces = lax.all_to_all(pieces, 'space', 0, 0)]
  transfers between devices with their start and end apart: 12 -> 12, of which waited for: 7 -> 7; matrix products, arithmetic and copies ran while one was open for 0% -> 0% of each run, Pallas kernels for 38% -> 35%
where the time goes in v4:
time: 72.1 us; the launch traced here: 71.7 us
  Pallas kernels  30.7 us (43%)
  starting transfers between devices  25.7 us (36%)
  waiting for transfers between devices  15 us (21%)
    pallas_call x1, Pallas kernels, inner_pass(): pl.pallas_call(inner_states, name='inner_states', out_shape=outs, in_spec...  9.47 us
    all_to_all x1, starting transfers between devices, on_device(): lax.all_to_all(send.reshape(members * slabs, single, half), ('ens', 'spac...  8.58 us
    all_to_all x1, waiting for transfers between devices, on_device(): lax.all_to_all(send.reshape(members * slabs, single, half), ('ens', 'spac...  7.73 us
    pallas_call x1, Pallas kernels, seam_pass(): pl.pallas_call(seam_states, name='seam_states', out_shape=outs, in_specs=...  7.66 us
    all_to_all x1, starting transfers between devices, on_device(): pieces = lax.all_to_all(pieces, 'space', 0, 0)  7.32 us
    ppermute x8, starting transfers between devices, partner(): return lax.ppermute(value, 'ens', [(i, i ^ bit) for i in range(count)])  4.53 us
    ppermute x8, waiting for transfers between devices, partner(): return lax.ppermute(value, 'ens', [(i, i ^ bit) for i in range(count)])  4.32 us
    ppermute x1, starting transfers between devices, on_device(): before = lax.ppermute(up, 'space', [(i, i + 1) for i in range(slabs - 1)])  3.94 us
  transfers between devices with their start and end apart: 12, of which 7 were waited for; matrix products, arithmetic and copies ran while one was open for 0% of the time, Pallas kernels for 35%

profile of v4, /device:TPU:0, one launch (start us, length us, event | category | flops | bytes accessed | tf_op | source)
XLA Modules:
  0.0 71.7 jit_solution(13956434508661633099)
XLA Ops:
  0.0 1.9 %pack_pieces.1 = bf16[8,176,256]{2,1,0:T(8,128)(2,1)} custom-call(s32[1]{0:T(128)} %bitcast.1.member_ref, bf16[32,1024]{1,0:T(8,128)(2,1)} %basis_ref.3, f32[128,1024]{1,0:T(8,128)} %control_ref.3), custom_call_target="tpu_custom_call" | custom-call | tf_op jit(solution)/shard_map/pack_pieces/pallas_call | solution.py:156
  1.9 7.3 %all-to-all-start = ((bf16[8,176,256]{2,1,0:T(8,128)(2,1)}), bf16[8,176,256]{2,1,0:T(8,128)(2,1)S(1)}, u32[]{:S(2)}, u32[]{:S(2)}) async-start(bf16[8,176,256]{2,1,0:T(8,128)(2,1)} %pack_pieces.1), calls=%async_computation | async-start | bytes 1441792 | tf_op jit(solution)/shard_map/all_to_all | solution.py:757
  9.2 3.4 %pack_edges.1 = (bf16[10,8,2048]{2,1,0:T(8,128)(2,1)}, bf16[10,8,2048]{2,1,0:T(8,128)(2,1)}) custom-call(s32[8]{0:T(128)} %index_ref.5, bf16[8,2,3,32,2048]{4,3,2,1,0:T(8,128)(2,1)} %states_ref.5, bf16[8,32,2048]{2,1,0:T(8,128)(2,1)} %targets_ref.5, s32[32,2048]{1,0:T(8,128)} %sea_ref.5), custom_call_target="tpu_custom_call" | custom-call | tf_op jit(solution)/shard_map/pack_edges/pallas_call | solution.py:106
  12.6 3.9 %collective-permute-start.5 = (bf16[10,8,2048]{2,1,0:T(8,128)(2,1)}, bf16[10,8,2048]{2,1,0:T(8,128)(2,1)S(1)}, u32[]{:S(2)}, u32[]{:S(2)}) collective-permute-start(bf16[10,8,2048]{2,1,0:T(8,128)(2,1)} %get-tuple-element.20), channel_id=1, source_target_pairs={{0,1},{1,2},{2,3},{3,4},{4,5},{5,6},{6,7},{8,9},{9,10},{10,11},{11... | collective-permute-start | bytes 983048 | tf_op jit(solution)/shard_map/ppermute | solution.py:759
  16.6 1.3 %collective-permute-start.6 = (bf16[10,8,2048]{2,1,0:T(8,128)(2,1)}, bf16[10,8,2048]{2,1,0:T(8,128)(2,1)S(1)}, u32[]{:S(2)}, u32[]{:S(2)}) collective-permute-start(bf16[10,8,2048]{2,1,0:T(8,128)(2,1)} %get-tuple-element.21), channel_id=1, source_target_pairs={{1,0},{2,1},{3,2},{4,3},{5,4},{6,5},{7,6},{9,8},{10,9},{11,10},{12... | collective-permute-start | bytes 983048 | tf_op jit(solution)/shard_map/ppermute | solution.py:760
  17.9 9.5 %inner_states.1 = (f32[3,16,32,128]{3,2,1,0:T(8,128)S(1)}, f32[5,16,32,128]{3,2,1,0:T(8,128)S(1)}, bf16[32,1024]{1,0:T(8,128)(2,1)S(1)}) custom-call(s32[8]{0:T(128)} %index_ref.5, bf16[8,2,3,32,2048]{4,3,2,1,0:T(8,128)(2,1)} %states_ref.5, bf16[8,32,2048]{2,1,0:T(8,128)(2,1)} %targets_ref.5, s32[32,2048]{1,0:T(8,128)} %sea_ref.5, bf16[32,1024]{1,0:T(8,128)(2,1)} %basis_ref.3), custom_call_target="tpu_custom_call" | custom-call | tf_op jit(solution)/shard_map/inner_states/pallas_call | solution.py:339
  27.3 2.0 %all-to-all-done.pieces_ref = bf16[8,176,256]{2,1,0:T(8,128)(2,1)S(1)} async-done(((bf16[8,176,256]{2,1,0:T(8,128)(2,1)}), bf16[8,176,256]{2,1,0:T(8,128)(2,1)S(1)}, u32[]{:S(2)}, u32[]{:S(2)}) %all-to-all-start) | async-done | bytes 720928 | tf_op jit(solution)/shard_map/all_to_all | solution.py:757
  29.3 0.2 make_coeffs.1.own_ref
  29.5 0.1 collective-permute-start.2
  29.6 1.6 %collective-permute-start.3 = (bf16[40,256]{1,0:T(8,128)(2,1)S(1)}, bf16[40,256]{1,0:T(8,128)(2,1)S(1)}, u32[]{:S(2)}, u32[]{:S(2)}) collective-permute-start(bf16[40,256]{1,0:T(8,128)(2,1)S(1)} %make_coeffs.1.own_ref), channel_id=1, source_target_pairs={{0,16},{8,24},{16,0},{24,8},{1,17},{9,25},{17,1},{25,9},{2,18},{10... | collective-permute-start | bytes 61448 | tf_op jit(solution)/shard_map/ppermute | solution.py:740
  31.1 0.3 collective-permute-start.4
  31.4 1.0 %collective-permute-done.5.before_ref = bf16[10,8,2048]{2,1,0:T(8,128)(2,1)S(1)} collective-permute-done((bf16[10,8,2048]{2,1,0:T(8,128)(2,1)}, bf16[10,8,2048]{2,1,0:T(8,128)(2,1)S(1)}, u32[]{:S(2)}, u32[]{:S(2)}) %collective-permute-start.5) | collective-permute-done | bytes 327712 | tf_op jit(solution)/shard_map/ppermute | solution.py:759
  32.4 7.7 %seam_states.1 = (f32[3,16,40,128]{3,2,1,0:T(8,128)S(1)}, f32[5,16,40,128]{3,2,1,0:T(8,128)S(1)}, bf16[16,40,128]{2,1,0:T(8,128)(2,1)S(1)}) custom-call(s32[8]{0:T(128)} %index_ref.5, bf16[8,2,3,32,2048]{4,3,2,1,0:T(8,128)(2,1)} %states_ref.5, bf16[8,32,2048]{2,1,0:T(8,128)(2,1)} %targets_ref.5, s32[32,2048]{1,0:T(8,128)} %sea_ref.5, ...), custom_call_target="tpu_custom_call" | custom-call | tf_op jit(solution)/shard_map/seam_states/pallas_call | solution.py:462
  40.1 0.0 collective-permute-done.4.both_ref
  40.1 2.0 %apply_potential.1 = (f32[16,2048]{1,0:T(8,128)S(1)}, f32[16,2048]{1,0:T(8,128)S(1)}) custom-call(s32[1]{0:T(128)} %bitcast.1.member_ref, bf16[40,256]{1,0:T(8,128)(2,1)S(1)} %make_coeffs.1.own_ref, bf16[40,256]{1,0:T(8,128)(2,1)S(1)} %collective-permute-done.2.near_ref, bf16[40,256]{1,0:T(8,128)(2,1)S(1)} %collective-permute-done.3.far_ref, ...), custom_call_target="tpu_custom_call" | custom-call | tf_op jit(solution)/shard_map/apply_potential/pallas_call | solution.py:616
  42.1 0.1 collective-permute-start.7
  42.2 1.3 %collective-permute-done.7 = f32[16,2048]{1,0:T(8,128)S(1)} collective-permute-done((f32[16,2048]{1,0:T(8,128)S(1)}, f32[16,2048]{1,0:T(8,128)S(1)}, u32[]{:S(2)}, u32[]{:S(2)}) %collective-permute-start.7) | collective-permute-done | bytes 131104 | tf_op jit(solution)/shard_map/ppermute | solution.py:740
  43.6 1.6 %collective-permute-start.8 = (f32[8,2048]{1,0:T(8,128)S(1)}, f32[8,2048]{1,0:T(8,128)S(1)}, u32[]{:S(2)}, u32[]{:S(2)}) collective-permute-start(f32[8,2048]{1,0:T(8,128)S(1)} %get-tuple-element.29), channel_id=1, source_target_pairs={{0,16},{8,24},{16,0},{24,8},{1,17},{9,25},{17,1},{25,9},{2,18},{10... | collective-permute-start | bytes 196616 | tf_op jit(solution)/shard_map/ppermute | solution.py:740
  45.2 0.6 collective-permute-start
  45.8 2.2 %hold.1.cols_ref = bf16[2048,1024]{1,0:T(8,128)(2,1)S(1)} custom-call(bf16[2048,1024]{1,0:T(8,128)(2,1)} %source_ref.1), custom_call_target="tpu_custom_call" | custom-call | tf_op jit(solution)/shard_map/hold/pallas_call | solution.py:183
  48.0 0.2 collective-permute-done.8.other_ref
  48.1 1.4 %project.1 = bf16[4,8,8,512]{3,2,1,0:T(8,128)(2,1)} custom-call(f32[8,2048]{1,0:T(8,128)S(1)} %get-tuple-element.30.own_ref, f32[8,2048]{1,0:T(8,128)S(1)} %collective-permute-done.8.other_ref, bf16[2048,1024]{1,0:T(8,128)(2,1)S(1)} %hold.1.cols_ref), custom_call_target="tpu_custom_call" | custom-call | tf_op jit(solution)/shard_map/project/pallas_call | solution.py:647
  49.5 8.6 %all-to-all-start.1 = ((bf16[32,8,512]{2,1,0:T(8,128)(2,1)}), bf16[32,8,512]{2,1,0:T(8,128)(2,1)S(1)}, u32[]{:S(2)}, u32[]{:S(2)}) async-start(bf16[32,8,512]{2,1,0:T(8,128)(2,1)} %bitcast.8), calls=%async_computation.1 | async-start | bytes 524288 | tf_op jit(solution)/shard_map/all_to_all | solution.py:777
  58.1 0.0 collective-permute-done.far_ref
  58.1 0.3 collective-permute-start.1
  58.5 1.3 %collective-permute-done.1.near_ref = bf16[2,256,256]{2,1,0:T(8,128)(2,1)S(1)} collective-permute-done((bf16[2,256,256]{2,1,0:T(8,128)(2,1)S(1)}, bf16[2,256,256]{2,1,0:T(8,128)(2,1)S(1)}, u32[]{:S(2)}, u32[]{:S(2)}) %collective-permute-start.1) | collective-permute-done | bytes 262176 | tf_op jit(solution)/shard_map/ppermute | solution.py:740
  59.7 1.1 %assemble.1 = (bf16[1024,256]{1,0:T(8,128)(2,1)S(1)}, f32[128,1024]{1,0:T(8,128)S(1)}) custom-call(s32[1]{0:T(128)} %bitcast.1.member_ref, bf16[256,256]{1,0:T(8,128)(2,1)S(1)} %bitcast.13, bf16[256,256]{1,0:T(8,128)(2,1)S(1)} %collective-permute-done.far_ref, bf16[2,256,256]{2,1,0:T(8,128)(2,1)S(1)} %collective-permute-done.1.near_ref, f32[128,1024]{1,0:T(8,128)} %control_ref.3), custom_call_target="tpu_custom_call" | custom-call | tf_op jit(solution)/shard_map/assemble/pallas_call | solution.py:672
  60.8 7.7 %all-to-all-done.1 = bf16[32,8,512]{2,1,0:T(8,128)(2,1)S(1)} async-done(((bf16[32,8,512]{2,1,0:T(8,128)(2,1)}), bf16[32,8,512]{2,1,0:T(8,128)(2,1)S(1)}, u32[]{:S(2)}, u32[]{:S(2)}) %all-to-all-start.1) | async-done | bytes 262176 | tf_op jit(solution)/shard_map/all_to_all | solution.py:777
  68.5 0.5 gradient.1.own_ref
  69.0 0.1 collective-permute-start.9
  69.1 1.5 %collective-permute-done.9.other_ref = f32[136,512]{1,0:T(8,128)S(1)} collective-permute-done((f32[136,512]{1,0:T(8,128)S(1)}, f32[136,512]{1,0:T(8,128)S(1)}, u32[]{:S(2)}, u32[]{:S(2)}) %collective-permute-start.9) | collective-permute-done | bytes 278560 | tf_op jit(solution)/shard_map/ppermute | solution.py:740
  70.6 1.0 %update.1 = f32[128,1024]{1,0:T(8,128)} custom-call(s32[1]{0:T(128)} %bitcast.core_ref, f32[128,1024]{1,0:T(8,128)S(1)} %get-tuple-element.17.control_ref, f32[136,512]{1,0:T(8,128)S(1)} %gradient.1.own_ref, f32[136,512]{1,0:T(8,128)S(1)} %collective-permute-done.9.other_ref), custom_call_target="tpu_custom_call" | custom-call | tf_op jit(solution)/shard_map/update/pallas_call | solution.py:728
  (10 shorter events, 0.1 us)
Async XLA Ops:
  1.9 27.4 %all-to-all-start = ((bf16[8,176,256]{2,1,0:T(8,128)(2,1)}), bf16[8,176,256]{2,1,0:T(8,128)(2,1)S(1)}, u32[]{:S(2)}, u32[]{:S(2)}) async-start(bf16[8,176,256]{2,1,0:T(8,128)(2,1)} %pack_pieces.1), calls=%async_computation | async-start | bytes 1441792 | tf_op jit(solution)/shard_map/all_to_all | solution.py:757
  12.6 19.8 %collective-permute-start.5 = (bf16[10,8,2048]{2,1,0:T(8,128)(2,1)}, bf16[10,8,2048]{2,1,0:T(8,128)(2,1)S(1)}, u32[]{:S(2)}, u32[]{:S(2)}) collective-permute-start(bf16[10,8,2048]{2,1,0:T(8,128)(2,1)} %get-tuple-element.20), channel_id=1, source_target_pairs={{0,1},{1,2},{2,3},{3,4},{4,5},{5,6},{6,7},{8,9},{9,10},{10,11},{11... | collective-permute-start | bytes 983048 | tf_op jit(solution)/shard_map/ppermute | solution.py:759
  16.6 15.9 %collective-permute-start.6 = (bf16[10,8,2048]{2,1,0:T(8,128)(2,1)}, bf16[10,8,2048]{2,1,0:T(8,128)(2,1)S(1)}, u32[]{:S(2)}, u32[]{:S(2)}) collective-permute-start(bf16[10,8,2048]{2,1,0:T(8,128)(2,1)} %get-tuple-element.21), channel_id=1, source_target_pairs={{1,0},{2,1},{3,2},{4,3},{5,4},{6,5},{7,6},{9,8},{10,9},{11,10},{12... | collective-permute-start | bytes 983048 | tf_op jit(solution)/shard_map/ppermute | solution.py:760
  29.5 10.6 %collective-permute-start.2 = (bf16[40,256]{1,0:T(8,128)(2,1)S(1)}, bf16[40,256]{1,0:T(8,128)(2,1)S(1)}, u32[]{:S(2)}, u32[]{:S(2)}) collective-permute-start(bf16[40,256]{1,0:T(8,128)(2,1)S(1)} %make_coeffs.1.own_ref), channel_id=1, source_target_pairs={{0,8},{8,0},{16,24},{24,16},{1,9},{9,1},{17,25},{25,17},{2,10},{10... | collective-permute-start | bytes 61448 | tf_op jit(solution)/shard_map/ppermute | solution.py:740
  29.6 10.5 %collective-permute-start.3 = (bf16[40,256]{1,0:T(8,128)(2,1)S(1)}, bf16[40,256]{1,0:T(8,128)(2,1)S(1)}, u32[]{:S(2)}, u32[]{:S(2)}) collective-permute-start(bf16[40,256]{1,0:T(8,128)(2,1)S(1)} %make_coeffs.1.own_ref), channel_id=1, source_target_pairs={{0,16},{8,24},{16,0},{24,8},{1,17},{9,25},{17,1},{25,9},{2,18},{10... | collective-permute-start | bytes 61448 | tf_op jit(solution)/shard_map/ppermute | solution.py:740
  31.1 9.0 %collective-permute-start.4 = (bf16[40,256]{1,0:T(8,128)(2,1)S(1)}, bf16[40,256]{1,0:T(8,128)(2,1)S(1)}, u32[]{:S(2)}, u32[]{:S(2)}) collective-permute-start(bf16[40,256]{1,0:T(8,128)(2,1)S(1)} %make_coeffs.1.own_ref), channel_id=1, source_target_pairs={{0,24},{8,16},{16,8},{24,0},{1,25},{9,17},{17,9},{25,1},{2,26},{10... | collective-permute-start | bytes 61448 | tf_op jit(solution)/shard_map/ppermute | solution.py:740
  32.4 7.7 %copy-start = (bf16[2048,1024]{1,0:T(8,128)(2,1)S(1)}, bf16[2048,1024]{1,0:T(8,128)(2,1)}, u32[]{:S(2)}) copy-start(bf16[2048,1024]{1,0:T(8,128)(2,1)} %source_ref.1) | copy-start | bytes 12582916
  42.1 1.4 %collective-permute-start.7 = (f32[16,2048]{1,0:T(8,128)S(1)}, f32[16,2048]{1,0:T(8,128)S(1)}, u32[]{:S(2)}, u32[]{:S(2)}) collective-permute-start(f32[16,2048]{1,0:T(8,128)S(1)} %get-tuple-element.28), channel_id=1, source_target_pairs={{0,8},{8,0},{16,24},{24,16},{1,9},{9,1},{17,25},{25,17},{2,10},{10... | collective-permute-start | bytes 393224 | tf_op jit(solution)/shard_map/ppermute | solution.py:740
  43.6 4.5 %collective-permute-start.8 = (f32[8,2048]{1,0:T(8,128)S(1)}, f32[8,2048]{1,0:T(8,128)S(1)}, u32[]{:S(2)}, u32[]{:S(2)}) collective-permute-start(f32[8,2048]{1,0:T(8,128)S(1)} %get-tuple-element.29), channel_id=1, source_target_pairs={{0,16},{8,24},{16,0},{24,8},{1,17},{9,25},{17,1},{25,9},{2,18},{10... | collective-permute-start | bytes 196616 | tf_op jit(solution)/shard_map/ppermute | solution.py:740
  45.2 12.9 %collective-permute-start = (bf16[256,256]{1,0:T(8,128)(2,1)S(1)}, bf16[256,256]{1,0:T(8,128)(2,1)S(1)}, u32[]{:S(2)}, u32[]{:S(2)}) collective-permute-start(bf16[256,256]{1,0:T(8,128)(2,1)S(1)} %bitcast.11), channel_id=1, source_target_pairs={{0,16},{8,24},{16,0},{24,8},{1,17},{9,25},{17,1},{25,9},{2,18},{10... | collective-permute-start | bytes 393224 | tf_op jit(solution)/shard_map/ppermute | solution.py:740
  49.5 19.0 %all-to-all-start.1 = ((bf16[32,8,512]{2,1,0:T(8,128)(2,1)}), bf16[32,8,512]{2,1,0:T(8,128)(2,1)S(1)}, u32[]{:S(2)}, u32[]{:S(2)}) async-start(bf16[32,8,512]{2,1,0:T(8,128)(2,1)} %bitcast.8), calls=%async_computation.1 | async-start | bytes 524288 | tf_op jit(solution)/shard_map/all_to_all | solution.py:777
  58.1 1.6 %collective-permute-start.1 = (bf16[2,256,256]{2,1,0:T(8,128)(2,1)S(1)}, bf16[2,256,256]{2,1,0:T(8,128)(2,1)S(1)}, u32[]{:S(2)}, u32[]{:S(2)}) collective-permute-start(bf16[2,256,256]{2,1,0:T(8,128)(2,1)S(1)} %pad_maximum_fusion), channel_id=1, source_target_pairs={{0,8},{8,0},{16,24},{24,16},{1,9},{9,1},{17,25},{25,17},{2,10},{10... | collective-permute-start | bytes 786440 | tf_op jit(solution)/shard_map/ppermute | solution.py:740
  69.0 1.6 %collective-permute-start.9 = (f32[136,512]{1,0:T(8,128)S(1)}, f32[136,512]{1,0:T(8,128)S(1)}, u32[]{:S(2)}, u32[]{:S(2)}) collective-permute-start(f32[136,512]{1,0:T(8,128)S(1)} %gradient.1.own_ref), channel_id=1, source_target_pairs={{0,8},{8,0},{16,24},{24,16},{1,9},{9,1},{17,25},{25,17},{2,10},{10... | collective-permute-start | bytes 835592 | tf_op jit(solution)/shard_map/ppermute | solution.py:740

commit v5 on v4

--- a/solution.py
+++ b/solution.py
@@ -354,78 +354,99 @@
     )(*map(in_hbm, (section_index, checkpoints, targets, sea_mask, basis_rows)))
 
 
-def seam_states(index_ref, states_ref, targets_ref, sea_ref, before_ref, after_ref, push_in_ref, pairs_in_ref, push_ref, pairs_ref, mask_ref, sems, sea, ends, seen_ends, seen_edge, mask, live, lefts, partial, sums_ref, *padded):
+def seam_first(index_ref, states_ref, targets_ref, sea_ref, before_ref, sums_ref, sea_out, ends_out, seen_out, sems, ends, seen_ends, seen_edge, mask, live, lefts, partial, *padded):
     count = states_ref.shape[0]
     rows, cols = sea_ref.shape
+    top = tile_rows((TILE, cols)) < 4
+
+    def copies_of(k, side, row, ends, seen_ends):
+        here = pl.ds(row, TILE)
+        return (
+            pltpu.make_async_copy(
+                states_ref.at[k, index_ref[k], :, here, :], ends.at[k], sems.at[side, k]
+            ),
+            pltpu.make_async_copy(targets_ref.at[k, here, :], seen_ends.at[k], sems.at[2 + side, k]),
+        )
+
+    own_ends = (0, 0, ends, seen_ends)
+    next_ends = (1, rows - TILE, ends_out, seen_out)
+    fetched = fetch(sea_ref, sea_out, sems.at[0, count])
+    for which in (own_ends, next_ends):
+        for k in range(count):
+            for copy in copies_of(k, *which):
+                copy.start()
+    clear(sums_ref, *padded)
+    seen_edge[...] = split_lanes(before_ref[count].astype(F32))
+    fetched.wait()
+    beyond = pltpu.roll(before_ref[count + 1].astype(F32), 4, 0)
+    row = tile_rows((TILE, cols))
+    beyond = jnp.where(row >= 2, beyond, 0.0)
+    own = pltpu.roll(sea_out[:TILE, :].astype(F32), 4, 0)
+    mask[...] = split_lanes(jnp.where(top, beyond, own))
+    place = lax.broadcasted_iota(jnp.int32, live.shape, 1)
+    live[...] = jnp.where((place >= 3) & (place < 6), mask[...], 0.0)
+    sums = [sums_ref.at[k] for k in range(3 + PAIRS)]
+    state = [Rows(ref) for ref in padded[:4]]
+
+    @pl.loop(0, count)
+    def _(s):
+        before = split_lanes(before_ref[s].astype(F32))
+        state[0].put_at(9, before)
+        state[1].put_at(4, before)
+        state[2].put_at(6, before)
+        state[3].put_at(11, seen_edge[:, pl.ds(s, 1), :])
+        for copy in copies_of(s, *own_ends):
+            copy.wait()
+        for field in range(3):
+            state[field].put_at(12, split_lanes(ends[s, field].astype(F32)))
+        state[3].put_at(12, split_lanes(seen_ends[s].astype(F32)))
+        add_state(1, state, mask, live, padded[4:], (lefts, partial), sums)
+
+    for k in range(count):
+        for copy in copies_of(k, *next_ends):
+            copy.wait()
+
+
+def seam_last(sea, ends, seen_ends, before_ref, after_ref, first_ref, push_in_ref, pairs_in_ref, push_ref, pairs_ref, mask_ref, seen_edge, mask, live, lefts, partial, sums_ref, *padded):
+    count = ends.shape[0]
+    rows, cols = sea.shape
     row = tile_rows((TILE, cols))
     top = row < 4
-
-    def copies_of(k):
-        for side, start in enumerate((rows - TILE, 0)):
-            here = pl.ds(start, TILE)
-            yield pltpu.make_async_copy(
-                states_ref.at[k, index_ref[k], :, here, :], ends.at[k, side], sems.at[side, k]
-            )
-            yield pltpu.make_async_copy(
-                targets_ref.at[k, here, :], seen_ends.at[k, side], sems.at[2 + side, k]
-            )
-
-    fetched = pltpu.make_async_copy(sea_ref, sea, sems.at[0, count])
-    fetched.start()
-    for k in range(count):
-        for copy in copies_of(k):
-            copy.start()
     clear(sums_ref, *padded)
-    seen_edge[0] = split_lanes(before_ref[count].astype(F32))
-    seen_edge[1] = split_lanes(after_ref[count].astype(F32))
+    seen_edge[...] = split_lanes(after_ref[count].astype(F32))
     after = jnp.where(row < 2, after_ref[count + 1].astype(F32), 0.0)
     before = jnp.where(row >= 6, before_ref[count + 1].astype(F32), 0.0)
-    beyond = after + before
-    fetched.wait()
-    turned = pltpu.roll(beyond, 4, 0)
-    last = pltpu.roll(sea[rows - TILE :, :].astype(F32), 4, 0)
-    first = pltpu.roll(sea[:TILE, :].astype(F32), 4, 0)
-    mask[:, :TILE, :] = split_lanes(jnp.where(top, last, turned))
-    mask[:, TILE:, :] = split_lanes(jnp.where(top, turned, first))
+    own = pltpu.roll(sea[rows - TILE :, :].astype(F32), 4, 0)
+    mask[...] = split_lanes(jnp.where(top, own, pltpu.roll(after, 4, 0)))
     for tile in range(rows // TILE):
         mask_ref[:, rows_of(tile), :] = split_lanes(
             sea[rows_of(tile), :].astype(F32)
         ).astype(BF16)
-    mask_ref[:, rows:, :] = split_lanes(beyond).astype(BF16)
+    mask_ref[:, rows:, :] = split_lanes(after + before).astype(BF16)
     place = lax.broadcasted_iota(jnp.int32, live.shape, 1)
-    counts = ((place >= 2) & (place < 5)) | ((place >= 11) & (place < 14))
-    live[...] = jnp.where(counts, mask[...], 0.0)
+    live[...] = jnp.where((place >= 2) & (place < 5), mask[...], 0.0)
+    sums = [sums_ref.at[k] for k in range(3 + PAIRS)]
+    state = [Rows(ref) for ref in padded[:4]]
 
     @pl.loop(0, count)
     def _(s):
-        state = [Rows(ref) for ref in padded[:4]]
         after = split_lanes(after_ref[s].astype(F32))
-        before = split_lanes(before_ref[s].astype(F32))
-        for copy in copies_of(s):
-            copy.wait()
         state[0].put_at(12, after)
-        state[0].put_at(17, before)
-        state[1].put_at(12, before)
         state[1].put_at(6, after)
-        state[2].put_at(14, before)
         state[2].put_at(9, after)
-        state[3].put_at(12, seen_edge[1, :, pl.ds(s, 1), :])
-        state[3].put_at(19, seen_edge[0, :, pl.ds(s, 1), :])
+        state[3].put_at(12, seen_edge[:, pl.ds(s, 1), :])
         for field in range(3):
-            state[field].put_at(4, split_lanes(ends[s, 0, field].astype(F32)))
-            state[field].put_at(20, split_lanes(ends[s, 1, field].astype(F32)))
-        state[3].put_at(4, split_lanes(seen_ends[s, 0].astype(F32)))
-        state[3].put_at(20, split_lanes(seen_ends[s, 1].astype(F32)))
-        sums = [sums_ref.at[k] for k in range(3 + PAIRS)]
-        add_state(2, state, mask, live, padded[4:], (lefts, partial), sums)
-
-    place = lax.broadcasted_iota(jnp.int32, (lefts.shape[0], TILE, LANES), 1)
+            state[field].put_at(4, split_lanes(ends[s, field].astype(F32)))
+        state[3].put_at(4, split_lanes(seen_ends[s].astype(F32)))
+        add_state(1, state, mask, live, padded[4:], (lefts, partial), sums)
+
+    place = lax.broadcasted_iota(jnp.int32, lefts.shape, 1)
     top = place < 4
     final = rows // TILE - 1
 
-    def ring(inner, outer, out, bounds):
-        ending = pltpu.roll(outer[:, :TILE, :], 4, 1)
-        opening = pltpu.roll(outer[:, TILE:, :], 4, 1)
+    def ring(inner, ending, opening, out, bounds):
+        ending = pltpu.roll(ending, 4, 1)
+        opening = pltpu.roll(opening, 4, 1)
         for tile in range(1, final):
             out[:, rows_of(tile), :] = inner[:, rows_of(tile), :]
         head = inner[:, :TILE, :]
@@ -441,48 +462,62 @@
         out[:, rows:, :] = jnp.where(top, ending, opening)
 
     for k in range(3):
-        ring(push_in_ref[k], sums_ref[k], push_ref.at[k], None)
+        ring(push_in_ref[k], sums_ref[k], first_ref[k], push_ref.at[k], None)
     for k in range(PAIRS):
         bounds = (2, 5) if k == PAIRS - 1 else (1, 4)
-        ring(pairs_in_ref[k], sums_ref[3 + k], pairs_ref.at[k], bounds)
-
-
-def seam_pass(section_index, checkpoints, before, after, targets, sea_mask, push, pairs):
-    count, _, fields, rows, cols = checkpoints.shape
+        ring(pairs_in_ref[k], sums_ref[3 + k], first_ref[3 + k], pairs_ref.at[k], bounds)
+
+
+def seam_first_pass(section_index, checkpoints, before, targets, sea_mask):
+    count, _, fields, _, cols = checkpoints.shape
+    lanes = cols // LANES
+    tile = pltpu.VMEM((lanes, TILE, LANES), F32)
+    padded = pltpu.VMEM((lanes, 3 * TILE, LANES), F32)
+    ends = (count, fields, TILE, cols)
+    seen = (count, TILE, cols)
+    return pl.pallas_call(
+        seam_first,
+        name="seam_first",
+        out_shape=(
+            jax.ShapeDtypeStruct((3 + PAIRS, lanes, TILE, LANES), F32),
+            jax.ShapeDtypeStruct(sea_mask.shape, jnp.int32),
+            jax.ShapeDtypeStruct(ends, BF16),
+            jax.ShapeDtypeStruct(seen, BF16),
+        ),
+        in_specs=[SMEM] + [HBM] * 3 + [VMEM],
+        out_specs=(VMEM,) * 4,
+        scratch_shapes=[
+            pltpu.SemaphoreType.DMA((4, count + 1)),
+            pltpu.VMEM(ends, BF16),
+            pltpu.VMEM(seen, BF16),
+        ]
+        + [tile] * 5
+        + [padded] * 9,
+        compiler_params=limit(14),
+    )(*map(in_hbm, (section_index, checkpoints, targets, sea_mask)), before)
+
+
+def seam_last_pass(sea, ends, seen, before, after, first, push, pairs):
+    rows, cols = sea.shape
     lanes = cols // LANES
     ring = rows + TILE
-    plain = pltpu.VMEM((lanes, 2 * TILE, LANES), F32)
-    padded = pltpu.VMEM((lanes, 4 * TILE, LANES), F32)
-    outs = (
-        jax.ShapeDtypeStruct((3, lanes, ring, LANES), F32),
-        jax.ShapeDtypeStruct((PAIRS, lanes, ring, LANES), F32),
-        jax.ShapeDtypeStruct((lanes, ring, LANES), BF16),
-    )
-
-    return pl.pallas_call(
-        seam_states,
-        name="seam_states",
-        out_shape=outs,
-        in_specs=[SMEM] + [HBM] * 3 + [VMEM] * 4,
+    tile = pltpu.VMEM((lanes, TILE, LANES), F32)
+    padded = pltpu.VMEM((lanes, 3 * TILE, LANES), F32)
+    return pl.pallas_call(
+        seam_last,
+        name="seam_last",
+        out_shape=(
+            jax.ShapeDtypeStruct((3, lanes, ring, LANES), F32),
+            jax.ShapeDtypeStruct((PAIRS, lanes, ring, LANES), F32),
+            jax.ShapeDtypeStruct((lanes, ring, LANES), BF16),
+        ),
+        in_specs=[VMEM] * 8,
         out_specs=(VMEM,) * 3,
-        scratch_shapes=[
-            pltpu.SemaphoreType.DMA((4, count + 1)),
-            pltpu.VMEM((rows, cols), jnp.int32),
-            pltpu.VMEM((count, 2, fields, TILE, cols), BF16),
-            pltpu.VMEM((count, 2, TILE, cols), BF16),
-            pltpu.VMEM((2, lanes, TILE, LANES), F32),
-        ]
-        + [plain] * 4
-        + [pltpu.VMEM((3 + PAIRS, lanes, 2 * TILE, LANES), F32)]
+        scratch_shapes=[tile] * 5
+        + [pltpu.VMEM((3 + PAIRS, lanes, TILE, LANES), F32)]
         + [padded] * 9,
-        compiler_params=limit(24),
-    )(
-        *map(in_hbm, (section_index, checkpoints, targets, sea_mask)),
-        before,
-        after,
-        push,
-        pairs,
-    )
+        compiler_params=limit(20),
+    )(sea, ends, seen, before, after, first, push, pairs)
 
 
 def make_coeffs(slab_ref, basis_ref, pieces_ref, out_ref):
@@ -636,9 +671,9 @@
     half = out_ref.shape[3]
     for core in range(2):
         part = projected[:, core * half : (core + 1) * half]
-        for chip in range(out_ref.shape[0] // 2):
-            for k in range(out_ref.shape[1]):
-                out_ref[2 * chip + core, k] = part
+        for chip in range(out_ref.shape[1] // 2):
+            for k in range(out_ref.shape[0]):
+                out_ref[k, 2 * chip + core] = part
 
 
 def projected_pieces(own, other, basis_cols, members, slabs):
@@ -647,7 +682,7 @@
     return pl.pallas_call(
         project,
         name="project",
-        out_shape=jax.ShapeDtypeStruct((members, slabs, single, half), BF16),
+        out_shape=jax.ShapeDtypeStruct((slabs, members, single, half), BF16),
         in_specs=[VMEM] * 3,
         out_specs=VMEM,
         compiler_params=limit(16),
@@ -763,9 +798,8 @@
     parts = [own]
     for bits in (1, 2, 3):
         parts.append(partner(own, bits))
-    push, pairs, mask = seam_pass(
-        section_index, checkpoints, before, after, targets, sea_mask, push, pairs
-    )
+    first, sea, ends, seen = seam_first_pass(section_index, checkpoints, before, targets, sea_mask)
+    push, pairs, mask = seam_last_pass(sea, ends, seen, before, after, first, push, pairs)
     keep, give = gradient_halves(member, parts, basis_cols, push, pairs, mask)
 
     keep = keep + partner(give, 1)
@@ -774,11 +808,11 @@
     arriving = partner(give, 2)
     cols = held(basis_cols)
     send = projected_pieces(own_rows, arriving, cols, members, slabs)
-    got = lax.all_to_all(send.reshape(members * slabs, single, half), ("ens", "space"), 0, 0)
+    got = lax.all_to_all(send.reshape(members * slabs, single, half), ("space", "ens"), 0, 0)
     projected_half = got.reshape(slabs * rows, half)
 
     part = pieces[:, rows_out : rows_out + rows, :].reshape(slabs, 2, members // 2, single, quarter)
-    part = part.transpose(2, 1, 0, 3, 4).reshape(slabs * rows, quarter)
+    part = part.transpose(0, 2, 1, 3, 4).reshape(slabs * rows, quarter)
     far = partner(part, 2)
     near = partner(jnp.stack([part, far]), 1)
     basis, kept = assembled(member, part, far, near, control)

time: 72.1 us -> 69.2 us (0.960)
  starting transfers between devices: 25.7 us -> 22.9 us
    all_to_all x1, starting transfers between devices: 8.58 us -> 5.86 us  [on_device(): lax.all_to_all(send.reshape(members * slabs, single, half), ('space', 'en...]
    pallas_call x2 -> x3, Pallas kernels: 9.02 us -> 8.68 us  [the longest x1 4.52 us: seam_first_pass(): pl.pallas_call(seam_first, name='seam_first', out_shape=(jax.ShapeDtypeSt...]
  transfers between devices with their start and end apart: 12 -> 12, of which waited for: 7 -> 7; matrix products, arithmetic and copies ran while one was open for 0% -> 0% of each run, Pallas kernels for 35% -> 36%
where the time goes in v5:
time: 69.2 us; the launch traced here: 68.7 us
  Pallas kernels  30.3 us (44%)
  starting transfers between devices  22.9 us (33%)
  waiting for transfers between devices  15.2 us (22%)
    pallas_call x1, Pallas kernels, inner_pass(): pl.pallas_call(inner_states, name='inner_states', out_shape=outs, in_spec...  9.47 us
    all_to_all x1, waiting for transfers between devices, on_device(): lax.all_to_all(send.reshape(members * slabs, single, half), ('space', 'en...  7.86 us
    all_to_all x1, starting transfers between devices, on_device(): pieces = lax.all_to_all(pieces, 'space', 0, 0)  7.32 us
    all_to_all x1, starting transfers between devices, on_device(): lax.all_to_all(send.reshape(members * slabs, single, half), ('space', 'en...  5.86 us
    ppermute x8, starting transfers between devices, partner(): return lax.ppermute(value, 'ens', [(i, i ^ bit) for i in range(count)])  4.53 us
    pallas_call x1, Pallas kernels, seam_first_pass(): pl.pallas_call(seam_first, name='seam_first', out_shape=(jax.ShapeDtypeSt...  4.52 us
    ppermute x8, waiting for transfers between devices, partner(): return lax.ppermute(value, 'ens', [(i, i ^ bit) for i in range(count)])  4.32 us
    ppermute x1, starting transfers between devices, on_device(): before = lax.ppermute(up, 'space', [(i, i + 1) for i in range(slabs - 1)])  3.94 us
  transfers between devices with their start and end apart: 12, of which 7 were waited for; matrix products, arithmetic and copies ran while one was open for 0% of the time, Pallas kernels for 36%

profile of v5, /device:TPU:0, one launch (start us, length us, event | category | flops | bytes accessed | tf_op | source)
XLA Modules:
  0.0 68.7 jit_solution(1940797554583494145)
XLA Ops:
  0.0 1.8 %pack_pieces.1 = bf16[8,176,256]{2,1,0:T(8,128)(2,1)} custom-call(s32[1]{0:T(128)} %bitcast.1.member_ref, bf16[32,1024]{1,0:T(8,128)(2,1)} %basis_ref.3, f32[128,1024]{1,0:T(8,128)} %control_ref.3), custom_call_target="tpu_custom_call" | custom-call | tf_op jit(solution)/shard_map/pack_pieces/pallas_call | solution.py:156
  1.9 7.3 %all-to-all-start = ((bf16[8,176,256]{2,1,0:T(8,128)(2,1)}), bf16[8,176,256]{2,1,0:T(8,128)(2,1)S(1)}, u32[]{:S(2)}, u32[]{:S(2)}) async-start(bf16[8,176,256]{2,1,0:T(8,128)(2,1)} %pack_pieces.1), calls=%async_computation | async-start | bytes 1441792 | tf_op jit(solution)/shard_map/all_to_all | solution.py:792
  9.2 3.4 %pack_edges.1 = (bf16[10,8,2048]{2,1,0:T(8,128)(2,1)}, bf16[10,8,2048]{2,1,0:T(8,128)(2,1)}) custom-call(s32[8]{0:T(128)} %index_ref.5, bf16[8,2,3,32,2048]{4,3,2,1,0:T(8,128)(2,1)} %states_ref.5, bf16[8,32,2048]{2,1,0:T(8,128)(2,1)} %targets_ref.5, s32[32,2048]{1,0:T(8,128)} %sea_ref.5), custom_call_target="tpu_custom_call" | custom-call | tf_op jit(solution)/shard_map/pack_edges/pallas_call | solution.py:106
  12.6 3.9 %collective-permute-start.5 = (bf16[10,8,2048]{2,1,0:T(8,128)(2,1)}, bf16[10,8,2048]{2,1,0:T(8,128)(2,1)S(1)}, u32[]{:S(2)}, u32[]{:S(2)}) collective-permute-start(bf16[10,8,2048]{2,1,0:T(8,128)(2,1)} %get-tuple-element.24), channel_id=1, source_target_pairs={{0,1},{1,2},{2,3},{3,4},{4,5},{5,6},{6,7},{8,9},{9,10},{10,11},{11... | collective-permute-start | bytes 983048 | tf_op jit(solution)/shard_map/ppermute | solution.py:794
  16.5 1.3 %collective-permute-start.6 = (bf16[10,8,2048]{2,1,0:T(8,128)(2,1)}, bf16[10,8,2048]{2,1,0:T(8,128)(2,1)S(1)}, u32[]{:S(2)}, u32[]{:S(2)}) collective-permute-start(bf16[10,8,2048]{2,1,0:T(8,128)(2,1)} %get-tuple-element.28), channel_id=1, source_target_pairs={{1,0},{2,1},{3,2},{4,3},{5,4},{6,5},{7,6},{9,8},{10,9},{11,10},{12... | collective-permute-start | bytes 983048 | tf_op jit(solution)/shard_map/ppermute | solution.py:795
  17.8 9.5 %inner_states.1 = (f32[3,16,32,128]{3,2,1,0:T(8,128)S(1)}, f32[5,16,32,128]{3,2,1,0:T(8,128)S(1)}, bf16[32,1024]{1,0:T(8,128)(2,1)S(1)}) custom-call(s32[8]{0:T(128)} %index_ref.5, bf16[8,2,3,32,2048]{4,3,2,1,0:T(8,128)(2,1)} %states_ref.5, bf16[8,32,2048]{2,1,0:T(8,128)(2,1)} %targets_ref.5, s32[32,2048]{1,0:T(8,128)} %sea_ref.5, bf16[32,1024]{1,0:T(8,128)(2,1)} %basis_ref.3), custom_call_target="tpu_custom_call" | custom-call | tf_op jit(solution)/shard_map/inner_states/pallas_call | solution.py:339
  27.3 2.0 %all-to-all-done.pieces_ref = bf16[8,176,256]{2,1,0:T(8,128)(2,1)S(1)} async-done(((bf16[8,176,256]{2,1,0:T(8,128)(2,1)}), bf16[8,176,256]{2,1,0:T(8,128)(2,1)S(1)}, u32[]{:S(2)}, u32[]{:S(2)}) %all-to-all-start) | async-done | bytes 720928 | tf_op jit(solution)/shard_map/all_to_all | solution.py:792
  29.3 0.2 make_coeffs.1.own_ref
  29.5 0.1 collective-permute-start.2
  29.6 1.6 %collective-permute-start.3 = (bf16[40,256]{1,0:T(8,128)(2,1)S(1)}, bf16[40,256]{1,0:T(8,128)(2,1)S(1)}, u32[]{:S(2)}, u32[]{:S(2)}) collective-permute-start(bf16[40,256]{1,0:T(8,128)(2,1)S(1)} %make_coeffs.1.own_ref), channel_id=1, source_target_pairs={{0,16},{8,24},{16,0},{24,8},{1,17},{9,25},{17,1},{25,9},{2,18},{10... | collective-permute-start | bytes 61448 | tf_op jit(solution)/shard_map/ppermute | solution.py:775
  31.1 0.3 collective-permute-start.4
  31.4 1.0 %collective-permute-done.5.before_ref = bf16[10,8,2048]{2,1,0:T(8,128)(2,1)S(1)} collective-permute-done((bf16[10,8,2048]{2,1,0:T(8,128)(2,1)}, bf16[10,8,2048]{2,1,0:T(8,128)(2,1)S(1)}, u32[]{:S(2)}, u32[]{:S(2)}) %collective-permute-start.5) | collective-permute-done | bytes 327712 | tf_op jit(solution)/shard_map/ppermute | solution.py:794
  32.4 4.5 %seam_first.1 = (f32[8,16,8,128]{3,2,1,0:T(8,128)S(1)}, s32[32,2048]{1,0:T(8,128)S(1)}, bf16[8,3,8,2048]{3,2,1,0:T(8,128)(2,1)S(1)}, bf16[8,8,2048]{2,1,0:T(8,128)(2,1)S(1)}) custom-call(s32[8]{0:T(128)} %index_ref.5, bf16[8,2,3,32,2048]{4,3,2,1,0:T(8,128)(2,1)} %states_ref.5, bf16[8,32,2048]{2,1,0:T(8,128)(2,1)} %targets_ref.5, s32[32,2048]{1,0:T(8,128)} %sea_ref.5, ...), custom_call_target="tpu_custom_call" | custom-call | tf_op jit(solution)/shard_map/seam_first/pallas_call | solution.py:478
  37.0 0.0 copy-start
  37.0 2.8 %seam_last.1 = (f32[3,16,40,128]{3,2,1,0:T(8,128)S(1)}, f32[5,16,40,128]{3,2,1,0:T(8,128)S(1)}, bf16[16,40,128]{2,1,0:T(8,128)(2,1)S(1)}) custom-call(s32[32,2048]{1,0:T(8,128)S(1)} %get-tuple-element.25.sea, bf16[8,3,8,2048]{3,2,1,0:T(8,128)(2,1)S(1)} %get-tuple-element.26.ends, bf16[8,8,2048]{2,1,0:T(8,128)(2,1)S(1)} %get-tuple-element.27.seen_ends, ...), custom_call_target="tpu_custom_call" | custom-call | tf_op jit(solution)/shard_map/seam_last/pallas_call | solution.py:506
  39.8 2.0 %apply_potential.1 = (f32[16,2048]{1,0:T(8,128)S(1)}, f32[16,2048]{1,0:T(8,128)S(1)}) custom-call(s32[1]{0:T(128)} %bitcast.1.member_ref, bf16[40,256]{1,0:T(8,128)(2,1)S(1)} %make_coeffs.1.own_ref, bf16[40,256]{1,0:T(8,128)(2,1)S(1)} %collective-permute-done.2.near_ref, bf16[40,256]{1,0:T(8,128)(2,1)S(1)} %collective-permute-done.3.far_ref, ...), custom_call_target="tpu_custom_call" | custom-call | tf_op jit(solution)/shard_map/apply_potential/pallas_call | solution.py:651
  41.8 0.1 collective-permute-start.7
  41.9 1.3 %collective-permute-done.7 = f32[16,2048]{1,0:T(8,128)S(1)} collective-permute-done((f32[16,2048]{1,0:T(8,128)S(1)}, f32[16,2048]{1,0:T(8,128)S(1)}, u32[]{:S(2)}, u32[]{:S(2)}) %collective-permute-start.7) | collective-permute-done | bytes 131104 | tf_op jit(solution)/shard_map/ppermute | solution.py:775
  43.3 1.6 %collective-permute-start.8 = (f32[8,2048]{1,0:T(8,128)S(1)}, f32[8,2048]{1,0:T(8,128)S(1)}, u32[]{:S(2)}, u32[]{:S(2)}) collective-permute-start(f32[8,2048]{1,0:T(8,128)S(1)} %get-tuple-element.37), channel_id=1, source_target_pairs={{0,16},{8,24},{16,0},{24,8},{1,17},{9,25},{17,1},{25,9},{2,18},{10... | collective-permute-start | bytes 196616 | tf_op jit(solution)/shard_map/ppermute | solution.py:775
  44.9 0.6 collective-permute-start
  45.5 2.2 %hold.1.cols_ref = bf16[2048,1024]{1,0:T(8,128)(2,1)S(1)} custom-call(bf16[2048,1024]{1,0:T(8,128)(2,1)} %source_ref.1), custom_call_target="tpu_custom_call" | custom-call | tf_op jit(solution)/shard_map/hold/pallas_call | solution.py:183
  47.7 0.2 collective-permute-done.8.other_ref
  47.8 1.4 %project.1 = bf16[8,4,8,512]{3,2,1,0:T(8,128)(2,1)} custom-call(f32[8,2048]{1,0:T(8,128)S(1)} %get-tuple-element.38.own_ref, f32[8,2048]{1,0:T(8,128)S(1)} %collective-permute-done.8.other_ref, bf16[2048,1024]{1,0:T(8,128)(2,1)S(1)} %hold.1.cols_ref), custom_call_target="tpu_custom_call" | custom-call | tf_op jit(solution)/shard_map/project/pallas_call | solution.py:682
  49.2 5.9 %all-to-all-start.1 = ((bf16[32,8,512]{2,1,0:T(8,128)(2,1)}), bf16[32,8,512]{2,1,0:T(8,128)(2,1)S(1)}, u32[]{:S(2)}, u32[]{:S(2)}) async-start(bf16[32,8,512]{2,1,0:T(8,128)(2,1)} %bitcast.8), calls=%async_computation.1 | async-start | bytes 524288 | tf_op jit(solution)/shard_map/all_to_all | solution.py:811
  55.1 0.3 collective-permute-start.1
  55.4 1.3 %collective-permute-done.1.near_ref = bf16[2,256,256]{2,1,0:T(8,128)(2,1)S(1)} collective-permute-done((bf16[2,256,256]{2,1,0:T(8,128)(2,1)S(1)}, bf16[2,256,256]{2,1,0:T(8,128)(2,1)S(1)}, u32[]{:S(2)}, u32[]{:S(2)}) %collective-permute-start.1) | collective-permute-done | bytes 262176 | tf_op jit(solution)/shard_map/ppermute | solution.py:775
  56.7 1.1 %assemble.1 = (bf16[1024,256]{1,0:T(8,128)(2,1)S(1)}, f32[128,1024]{1,0:T(8,128)S(1)}) custom-call(s32[1]{0:T(128)} %bitcast.1.member_ref, bf16[256,256]{1,0:T(8,128)(2,1)S(1)} %bitcast.13, bf16[256,256]{1,0:T(8,128)(2,1)S(1)} %collective-permute-done.far_ref, bf16[2,256,256]{2,1,0:T(8,128)(2,1)S(1)} %collective-permute-done.1.near_ref, f32[128,1024]{1,0:T(8,128)} %control_ref.3), custom_call_target="tpu_custom_call" | custom-call | tf_op jit(solution)/shard_map/assemble/pallas_call | solution.py:707
  57.8 7.9 %all-to-all-done.1 = bf16[32,8,512]{2,1,0:T(8,128)(2,1)S(1)} async-done(((bf16[32,8,512]{2,1,0:T(8,128)(2,1)}), bf16[32,8,512]{2,1,0:T(8,128)(2,1)S(1)}, u32[]{:S(2)}, u32[]{:S(2)}) %all-to-all-start.1) | async-done | bytes 262176 | tf_op jit(solution)/shard_map/all_to_all | solution.py:811
  65.6 0.5 gradient.1.own_ref
  66.1 0.1 collective-permute-start.9
  66.2 1.5 %collective-permute-done.9.other_ref = f32[136,512]{1,0:T(8,128)S(1)} collective-permute-done((f32[136,512]{1,0:T(8,128)S(1)}, f32[136,512]{1,0:T(8,128)S(1)}, u32[]{:S(2)}, u32[]{:S(2)}) %collective-permute-start.9) | collective-permute-done | bytes 278560 | tf_op jit(solution)/shard_map/ppermute | solution.py:775
  67.7 1.0 %update.1 = f32[128,1024]{1,0:T(8,128)} custom-call(s32[1]{0:T(128)} %bitcast.core_ref, f32[128,1024]{1,0:T(8,128)S(1)} %get-tuple-element.21.control_ref, f32[136,512]{1,0:T(8,128)S(1)} %gradient.1.own_ref, f32[136,512]{1,0:T(8,128)S(1)} %collective-permute-done.9.other_ref), custom_call_target="tpu_custom_call" | custom-call | tf_op jit(solution)/shard_map/update/pallas_call | solution.py:763
  (11 shorter events, 0.1 us)
Async XLA Ops:
  1.9 27.4 %all-to-all-start = ((bf16[8,176,256]{2,1,0:T(8,128)(2,1)}), bf16[8,176,256]{2,1,0:T(8,128)(2,1)S(1)}, u32[]{:S(2)}, u32[]{:S(2)}) async-start(bf16[8,176,256]{2,1,0:T(8,128)(2,1)} %pack_pieces.1), calls=%async_computation | async-start | bytes 1441792 | tf_op jit(solution)/shard_map/all_to_all | solution.py:792
  12.6 19.8 %collective-permute-start.5 = (bf16[10,8,2048]{2,1,0:T(8,128)(2,1)}, bf16[10,8,2048]{2,1,0:T(8,128)(2,1)S(1)}, u32[]{:S(2)}, u32[]{:S(2)}) collective-permute-start(bf16[10,8,2048]{2,1,0:T(8,128)(2,1)} %get-tuple-element.24), channel_id=1, source_target_pairs={{0,1},{1,2},{2,3},{3,4},{4,5},{5,6},{6,7},{8,9},{9,10},{10,11},{11... | collective-permute-start | bytes 983048 | tf_op jit(solution)/shard_map/ppermute | solution.py:794
  16.5 20.4 %collective-permute-start.6 = (bf16[10,8,2048]{2,1,0:T(8,128)(2,1)}, bf16[10,8,2048]{2,1,0:T(8,128)(2,1)S(1)}, u32[]{:S(2)}, u32[]{:S(2)}) collective-permute-start(bf16[10,8,2048]{2,1,0:T(8,128)(2,1)} %get-tuple-element.28), channel_id=1, source_target_pairs={{1,0},{2,1},{3,2},{4,3},{5,4},{6,5},{7,6},{9,8},{10,9},{11,10},{12... | collective-permute-start | bytes 983048 | tf_op jit(solution)/shard_map/ppermute | solution.py:795
  29.5 10.3 %collective-permute-start.2 = (bf16[40,256]{1,0:T(8,128)(2,1)S(1)}, bf16[40,256]{1,0:T(8,128)(2,1)S(1)}, u32[]{:S(2)}, u32[]{:S(2)}) collective-permute-start(bf16[40,256]{1,0:T(8,128)(2,1)S(1)} %make_coeffs.1.own_ref), channel_id=1, source_target_pairs={{0,8},{8,0},{16,24},{24,16},{1,9},{9,1},{17,25},{25,17},{2,10},{10... | collective-permute-start | bytes 61448 | tf_op jit(solution)/shard_map/ppermute | solution.py:775
  29.6 10.2 %collective-permute-start.3 = (bf16[40,256]{1,0:T(8,128)(2,1)S(1)}, bf16[40,256]{1,0:T(8,128)(2,1)S(1)}, u32[]{:S(2)}, u32[]{:S(2)}) collective-permute-start(bf16[40,256]{1,0:T(8,128)(2,1)S(1)} %make_coeffs.1.own_ref), channel_id=1, source_target_pairs={{0,16},{8,24},{16,0},{24,8},{1,17},{9,25},{17,1},{25,9},{2,18},{10... | collective-permute-start | bytes 61448 | tf_op jit(solution)/shard_map/ppermute | solution.py:775
  31.1 8.7 %collective-permute-start.4 = (bf16[40,256]{1,0:T(8,128)(2,1)S(1)}, bf16[40,256]{1,0:T(8,128)(2,1)S(1)}, u32[]{:S(2)}, u32[]{:S(2)}) collective-permute-start(bf16[40,256]{1,0:T(8,128)(2,1)S(1)} %make_coeffs.1.own_ref), channel_id=1, source_target_pairs={{0,24},{8,16},{16,8},{24,0},{1,25},{9,17},{17,9},{25,1},{2,26},{10... | collective-permute-start | bytes 61448 | tf_op jit(solution)/shard_map/ppermute | solution.py:775
  37.0 2.9 %copy-start = (bf16[2048,1024]{1,0:T(8,128)(2,1)S(1)}, bf16[2048,1024]{1,0:T(8,128)(2,1)}, u32[]{:S(2)}) copy-start(bf16[2048,1024]{1,0:T(8,128)(2,1)} %source_ref.1) | copy-start | bytes 12582916
  41.8 1.4 %collective-permute-start.7 = (f32[16,2048]{1,0:T(8,128)S(1)}, f32[16,2048]{1,0:T(8,128)S(1)}, u32[]{:S(2)}, u32[]{:S(2)}) collective-permute-start(f32[16,2048]{1,0:T(8,128)S(1)} %get-tuple-element.36), channel_id=1, source_target_pairs={{0,8},{8,0},{16,24},{24,16},{1,9},{9,1},{17,25},{25,17},{2,10},{10... | collective-permute-start | bytes 393224 | tf_op jit(solution)/shard_map/ppermute | solution.py:775
  43.3 4.5 %collective-permute-start.8 = (f32[8,2048]{1,0:T(8,128)S(1)}, f32[8,2048]{1,0:T(8,128)S(1)}, u32[]{:S(2)}, u32[]{:S(2)}) collective-permute-start(f32[8,2048]{1,0:T(8,128)S(1)} %get-tuple-element.37), channel_id=1, source_target_pairs={{0,16},{8,24},{16,0},{24,8},{1,17},{9,25},{17,1},{25,9},{2,18},{10... | collective-permute-start | bytes 196616 | tf_op jit(solution)/shard_map/ppermute | solution.py:775
  44.9 10.2 %collective-permute-start = (bf16[256,256]{1,0:T(8,128)(2,1)S(1)}, bf16[256,256]{1,0:T(8,128)(2,1)S(1)}, u32[]{:S(2)}, u32[]{:S(2)}) collective-permute-start(bf16[256,256]{1,0:T(8,128)(2,1)S(1)} %bitcast.11), channel_id=1, source_target_pairs={{0,16},{8,24},{16,0},{24,8},{1,17},{9,25},{17,1},{25,9},{2,18},{10... | collective-permute-start | bytes 393224 | tf_op jit(solution)/shard_map/ppermute | solution.py:775
  49.2 16.4 %all-to-all-start.1 = ((bf16[32,8,512]{2,1,0:T(8,128)(2,1)}), bf16[32,8,512]{2,1,0:T(8,128)(2,1)S(1)}, u32[]{:S(2)}, u32[]{:S(2)}) async-start(bf16[32,8,512]{2,1,0:T(8,128)(2,1)} %bitcast.8), calls=%async_computation.1 | async-start | bytes 524288 | tf_op jit(solution)/shard_map/all_to_all | solution.py:811
  55.1 1.6 %collective-permute-start.1 = (bf16[2,256,256]{2,1,0:T(8,128)(2,1)S(1)}, bf16[2,256,256]{2,1,0:T(8,128)(2,1)S(1)}, u32[]{:S(2)}, u32[]{:S(2)}) collective-permute-start(bf16[2,256,256]{2,1,0:T(8,128)(2,1)S(1)} %pad_maximum_fusion), channel_id=1, source_target_pairs={{0,8},{8,0},{16,24},{24,16},{1,9},{9,1},{17,25},{25,17},{2,10},{10... | collective-permute-start | bytes 786440 | tf_op jit(solution)/shard_map/ppermute | solution.py:775
  66.1 1.6 %collective-permute-start.9 = (f32[136,512]{1,0:T(8,128)S(1)}, f32[136,512]{1,0:T(8,128)S(1)}, u32[]{:S(2)}, u32[]{:S(2)}) collective-permute-start(f32[136,512]{1,0:T(8,128)S(1)} %gradient.1.own_ref), channel_id=1, source_target_pairs={{0,8},{8,0},{16,24},{24,16},{1,9},{9,1},{17,25},{25,17},{2,10},{10... | collective-permute-start | bytes 835592 | tf_op jit(solution)/shard_map/ppermute | solution.py:775

commit v6 on v5

--- a/solution.py
+++ b/solution.py
@@ -354,34 +354,58 @@
     )(*map(in_hbm, (section_index, checkpoints, targets, sea_mask, basis_rows)))
 
 
-def seam_first(index_ref, states_ref, targets_ref, sea_ref, before_ref, sums_ref, sea_out, ends_out, seen_out, sems, ends, seen_ends, seen_edge, mask, live, lefts, partial, *padded):
+def end_copies(index_ref, states_ref, targets_ref, row, ends_out, seen_out, sems):
+    here = pl.ds(row, TILE)
     count = states_ref.shape[0]
-    rows, cols = sea_ref.shape
+    copies = [fetch(targets_ref.at[:, here, :], seen_out, sems.at[count])]
+    for k in range(count):
+        source = states_ref.at[k, index_ref[k], :, here, :]
+        copies.append(fetch(source, ends_out.at[k], sems.at[k]))
+    return copies
+
+
+def fetch_ends(index_ref, states_ref, targets_ref, sea_ref, sea_out, ends_out, seen_out, sems):
+    count = states_ref.shape[0]
+    copies = [fetch(sea_ref, sea_out, sems.at[count + 1])]
+    copies += end_copies(index_ref, states_ref, targets_ref, 0, ends_out, seen_out, sems)
+    for copy in copies:
+        copy.wait()
+
+
+def end_shapes(checkpoints):
+    count, _, fields, _, cols = checkpoints.shape
+    return (
+        jax.ShapeDtypeStruct((count, fields, TILE, cols), BF16),
+        jax.ShapeDtypeStruct((count, TILE, cols), BF16),
+    )
+
+
+def fetched_ends(section_index, checkpoints, targets, sea_mask):
+    count = checkpoints.shape[0]
+    return pl.pallas_call(
+        fetch_ends,
+        name="fetch_ends",
+        out_shape=(jax.ShapeDtypeStruct(sea_mask.shape, jnp.int32),) + end_shapes(checkpoints),
+        in_specs=[SMEM] + [HBM] * 3,
+        out_specs=(VMEM,) * 3,
+        scratch_shapes=[pltpu.SemaphoreType.DMA((count + 2,))],
+        compiler_params=limit(6),
+    )(*map(in_hbm, (section_index, checkpoints, targets, sea_mask)))
+
+
+def seam_first(index_ref, states_ref, targets_ref, sea, ends, seen_ends, before_ref, sums_ref, ends_out, seen_out, sems, seen_edge, mask, live, lefts, partial, *padded):
+    count = ends.shape[0]
+    rows, cols = sea.shape
     top = tile_rows((TILE, cols)) < 4
-
-    def copies_of(k, side, row, ends, seen_ends):
-        here = pl.ds(row, TILE)
-        return (
-            pltpu.make_async_copy(
-                states_ref.at[k, index_ref[k], :, here, :], ends.at[k], sems.at[side, k]
-            ),
-            pltpu.make_async_copy(targets_ref.at[k, here, :], seen_ends.at[k], sems.at[2 + side, k]),
-        )
-
-    own_ends = (0, 0, ends, seen_ends)
-    next_ends = (1, rows - TILE, ends_out, seen_out)
-    fetched = fetch(sea_ref, sea_out, sems.at[0, count])
-    for which in (own_ends, next_ends):
-        for k in range(count):
-            for copy in copies_of(k, *which):
-                copy.start()
+    copies = end_copies(
+        index_ref, states_ref, targets_ref, rows - TILE, ends_out, seen_out, sems
+    )
     clear(sums_ref, *padded)
     seen_edge[...] = split_lanes(before_ref[count].astype(F32))
-    fetched.wait()
     beyond = pltpu.roll(before_ref[count + 1].astype(F32), 4, 0)
     row = tile_rows((TILE, cols))
     beyond = jnp.where(row >= 2, beyond, 0.0)
-    own = pltpu.roll(sea_out[:TILE, :].astype(F32), 4, 0)
+    own = pltpu.roll(sea[:TILE, :].astype(F32), 4, 0)
     mask[...] = split_lanes(jnp.where(top, beyond, own))
     place = lax.broadcasted_iota(jnp.int32, live.shape, 1)
     live[...] = jnp.where((place >= 3) & (place < 6), mask[...], 0.0)
@@ -395,16 +419,13 @@
         state[1].put_at(4, before)
         state[2].put_at(6, before)
         state[3].put_at(11, seen_edge[:, pl.ds(s, 1), :])
-        for copy in copies_of(s, *own_ends):
-            copy.wait()
         for field in range(3):
             state[field].put_at(12, split_lanes(ends[s, field].astype(F32)))
         state[3].put_at(12, split_lanes(seen_ends[s].astype(F32)))
         add_state(1, state, mask, live, padded[4:], (lefts, partial), sums)
 
-    for k in range(count):
-        for copy in copies_of(k, *next_ends):
-            copy.wait()
+    for copy in copies:
+        copy.wait()
 
 
 def seam_last(sea, ends, seen_ends, before_ref, after_ref, first_ref, push_in_ref, pairs_in_ref, push_ref, pairs_ref, mask_ref, seen_edge, mask, live, lefts, partial, sums_ref, *padded):
@@ -468,33 +489,21 @@
         ring(pairs_in_ref[k], sums_ref[3 + k], first_ref[3 + k], pairs_ref.at[k], bounds)
 
 
-def seam_first_pass(section_index, checkpoints, before, targets, sea_mask):
-    count, _, fields, _, cols = checkpoints.shape
-    lanes = cols // LANES
+def seam_first_pass(section_index, checkpoints, targets, sea, ends, seen, before):
+    count = checkpoints.shape[0]
+    lanes = sea.shape[1] // LANES
     tile = pltpu.VMEM((lanes, TILE, LANES), F32)
     padded = pltpu.VMEM((lanes, 3 * TILE, LANES), F32)
-    ends = (count, fields, TILE, cols)
-    seen = (count, TILE, cols)
+    sums = jax.ShapeDtypeStruct((3 + PAIRS, lanes, TILE, LANES), F32)
     return pl.pallas_call(
         seam_first,
         name="seam_first",
-        out_shape=(
-            jax.ShapeDtypeStruct((3 + PAIRS, lanes, TILE, LANES), F32),
-            jax.ShapeDtypeStruct(sea_mask.shape, jnp.int32),
-            jax.ShapeDtypeStruct(ends, BF16),
-            jax.ShapeDtypeStruct(seen, BF16),
-        ),
-        in_specs=[SMEM] + [HBM] * 3 + [VMEM],
-        out_specs=(VMEM,) * 4,
-        scratch_shapes=[
-            pltpu.SemaphoreType.DMA((4, count + 1)),
-            pltpu.VMEM(ends, BF16),
-            pltpu.VMEM(seen, BF16),
-        ]
-        + [tile] * 5
-        + [padded] * 9,
-        compiler_params=limit(14),
-    )(*map(in_hbm, (section_index, checkpoints, targets, sea_mask)), before)
+        out_shape=(sums,) + end_shapes(checkpoints),
+        in_specs=[SMEM] + [HBM] * 2 + [VMEM] * 4,
+        out_specs=(VMEM,) * 3,
+        scratch_shapes=[pltpu.SemaphoreType.DMA((count + 1,))] + [tile] * 5 + [padded] * 9,
+        compiler_params=limit(12),
+    )(*map(in_hbm, (section_index, checkpoints, targets)), sea, ends, seen, before)
 
 
 def seam_last_pass(sea, ends, seen, before, after, first, push, pairs):
@@ -798,7 +807,10 @@
     parts = [own]
     for bits in (1, 2, 3):
         parts.append(partner(own, bits))
-    first, sea, ends, seen = seam_first_pass(section_index, checkpoints, before, targets, sea_mask)
+    sea, ends, seen = fetched_ends(section_index, checkpoints, targets, sea_mask)
+    first, ends, seen = seam_first_pass(
+        section_index, checkpoints, targets, sea, ends, seen, before
+    )
     push, pairs, mask = seam_last_pass(sea, ends, seen, before, after, first, push, pairs)
     keep, give = gradient_halves(member, parts, basis_cols, push, pairs, mask)
 

time: 69.2 us -> 68.4 us (0.988)
  waiting for transfers between devices: 15.2 us -> 13.8 us
  Pallas kernels: 30.3 us -> 31.2 us
    ppermute x1, waiting for transfers between devices: 1 us -> 0.01 us  [on_device(): before = lax.ppermute(up, 'space', [(i, i + 1) for i in range(slabs - 1)])]
    pallas_call x1 -> x2, Pallas kernels: 4.52 us -> 5.35 us  [the longest x1 3.33 us: seam_first_pass(): pl.pallas_call(seam_first, name='seam_first', out_shape=(sums,) + end_sha...]
  transfers between devices with their start and end apart: 12 -> 12, of which waited for: 7 -> 6; matrix products, arithmetic and copies ran while one was open for 0% -> 0% of each run, Pallas kernels for 36% -> 38%
where the time goes in v6:
time: 68.4 us; the launch traced here: 67.9 us
  Pallas kernels  31.2 us (46%)
  starting transfers between devices  22.6 us (33%)
  waiting for transfers between devices  13.8 us (20%)
    pallas_call x1, Pallas kernels, inner_pass(): pl.pallas_call(inner_states, name='inner_states', out_shape=outs, in_spec...  9.47 us
    all_to_all x1, waiting for transfers between devices, on_device(): lax.all_to_all(send.reshape(members * slabs, single, half), ('space', 'en...  7.86 us
    all_to_all x1, starting transfers between devices, on_device(): pieces = lax.all_to_all(pieces, 'space', 0, 0)  7.32 us
    all_to_all x1, starting transfers between devices, on_device(): lax.all_to_all(send.reshape(members * slabs, single, half), ('space', 'en...  5.2 us
    ppermute x8, starting transfers between devices, partner(): return lax.ppermute(value, 'ens', [(i, i ^ bit) for i in range(count)])  4.88 us
    ppermute x8, waiting for transfers between devices, partner(): return lax.ppermute(value, 'ens', [(i, i ^ bit) for i in range(count)])  3.95 us
    ppermute x1, starting transfers between devices, on_device(): before = lax.ppermute(up, 'space', [(i, i + 1) for i in range(slabs - 1)])  3.94 us
    pallas_call x1, Pallas kernels, edge_messages(): pl.pallas_call(pack_edges, name='pack_edges', out_shape=(edges, edges), i...  3.41 us
  transfers between devices with their start and end apart: 12, of which 6 were waited for; matrix products, arithmetic and copies ran while one was open for 0% of the time, Pallas kernels for 38%

profile of v6, /device:TPU:0, one launch (start us, length us, event | category | flops | bytes accessed | tf_op | source)
XLA Modules:
  0.0 67.9 jit_solution(8692305700140796846)
XLA Ops:
  0.0 1.8 %pack_pieces.1 = bf16[8,176,256]{2,1,0:T(8,128)(2,1)} custom-call(s32[1]{0:T(128)} %bitcast.1.member_ref, bf16[32,1024]{1,0:T(8,128)(2,1)} %basis_ref.3, f32[128,1024]{1,0:T(8,128)} %control_ref.3), custom_call_target="tpu_custom_call" | custom-call | tf_op jit(solution)/shard_map/pack_pieces/pallas_call | solution.py:156
  1.8 7.3 %all-to-all-start = ((bf16[8,176,256]{2,1,0:T(8,128)(2,1)}), bf16[8,176,256]{2,1,0:T(8,128)(2,1)S(1)}, u32[]{:S(2)}, u32[]{:S(2)}) async-start(bf16[8,176,256]{2,1,0:T(8,128)(2,1)} %pack_pieces.1), calls=%async_computation | async-start | bytes 1441792 | tf_op jit(solution)/shard_map/all_to_all | solution.py:801
  9.2 3.4 %pack_edges.1 = (bf16[10,8,2048]{2,1,0:T(8,128)(2,1)}, bf16[10,8,2048]{2,1,0:T(8,128)(2,1)}) custom-call(s32[8]{0:T(128)} %index_ref.7, bf16[8,2,3,32,2048]{4,3,2,1,0:T(8,128)(2,1)} %states_ref.7, bf16[8,32,2048]{2,1,0:T(8,128)(2,1)} %targets_ref.7, s32[32,2048]{1,0:T(8,128)} %sea_ref.5), custom_call_target="tpu_custom_call" | custom-call | tf_op jit(solution)/shard_map/pack_edges/pallas_call | solution.py:106
  12.6 3.9 %collective-permute-start.5 = (bf16[10,8,2048]{2,1,0:T(8,128)(2,1)}, bf16[10,8,2048]{2,1,0:T(8,128)(2,1)S(1)}, u32[]{:S(2)}, u32[]{:S(2)}) collective-permute-start(bf16[10,8,2048]{2,1,0:T(8,128)(2,1)} %get-tuple-element.29), channel_id=1, source_target_pairs={{0,1},{1,2},{2,3},{3,4},{4,5},{5,6},{6,7},{8,9},{9,10},{10,11},{11... | collective-permute-start | bytes 983048 | tf_op jit(solution)/shard_map/ppermute | solution.py:803
  16.5 1.3 %collective-permute-start.6 = (bf16[10,8,2048]{2,1,0:T(8,128)(2,1)}, bf16[10,8,2048]{2,1,0:T(8,128)(2,1)S(1)}, u32[]{:S(2)}, u32[]{:S(2)}) collective-permute-start(bf16[10,8,2048]{2,1,0:T(8,128)(2,1)} %get-tuple-element.32), channel_id=1, source_target_pairs={{1,0},{2,1},{3,2},{4,3},{5,4},{6,5},{7,6},{9,8},{10,9},{11,10},{12... | collective-permute-start | bytes 983048 | tf_op jit(solution)/shard_map/ppermute | solution.py:804
  17.8 9.5 %inner_states.1 = (f32[3,16,32,128]{3,2,1,0:T(8,128)S(1)}, f32[5,16,32,128]{3,2,1,0:T(8,128)S(1)}, bf16[32,1024]{1,0:T(8,128)(2,1)S(1)}) custom-call(s32[8]{0:T(128)} %index_ref.7, bf16[8,2,3,32,2048]{4,3,2,1,0:T(8,128)(2,1)} %states_ref.7, bf16[8,32,2048]{2,1,0:T(8,128)(2,1)} %targets_ref.7, s32[32,2048]{1,0:T(8,128)} %sea_ref.5, bf16[32,1024]{1,0:T(8,128)(2,1)} %basis_ref.3), custom_call_target="tpu_custom_call" | custom-call | tf_op jit(solution)/shard_map/inner_states/pallas_call | solution.py:339
  27.3 2.0 %all-to-all-done.pieces_ref = bf16[8,176,256]{2,1,0:T(8,128)(2,1)S(1)} async-done(((bf16[8,176,256]{2,1,0:T(8,128)(2,1)}), bf16[8,176,256]{2,1,0:T(8,128)(2,1)S(1)}, u32[]{:S(2)}, u32[]{:S(2)}) %all-to-all-start) | async-done | bytes 720928 | tf_op jit(solution)/shard_map/all_to_all | solution.py:801
  29.3 0.2 make_coeffs.1.own_ref
  29.5 0.1 collective-permute-start.2
  29.6 1.6 %collective-permute-start.3 = (bf16[40,256]{1,0:T(8,128)(2,1)S(1)}, bf16[40,256]{1,0:T(8,128)(2,1)S(1)}, u32[]{:S(2)}, u32[]{:S(2)}) collective-permute-start(bf16[40,256]{1,0:T(8,128)(2,1)S(1)} %make_coeffs.1.own_ref), channel_id=1, source_target_pairs={{0,16},{8,24},{16,0},{24,8},{1,17},{9,25},{17,1},{25,9},{2,18},{10... | collective-permute-start | bytes 61448 | tf_op jit(solution)/shard_map/ppermute | solution.py:784
  31.1 0.3 collective-permute-start.4
  31.4 2.0 %fetch_ends.1 = (s32[32,2048]{1,0:T(8,128)S(1)}, bf16[8,3,8,2048]{3,2,1,0:T(8,128)(2,1)S(1)}, bf16[8,8,2048]{2,1,0:T(8,128)(2,1)S(1)}) custom-call(s32[8]{0:T(128)} %index_ref.7, bf16[8,2,3,32,2048]{4,3,2,1,0:T(8,128)(2,1)} %states_ref.7, bf16[8,32,2048]{2,1,0:T(8,128)(2,1)} %targets_ref.7, s32[32,2048]{1,0:T(8,128)} %sea_ref.5), custom_call_target="tpu_custom_call" | custom-call | tf_op jit(solution)/shard_map/fetch_ends/pallas_call | solution.py:385
  33.5 3.3 %seam_first.1 = (f32[8,16,8,128]{3,2,1,0:T(8,128)S(1)}, bf16[8,3,8,2048]{3,2,1,0:T(8,128)(2,1)S(1)}, bf16[8,8,2048]{2,1,0:T(8,128)(2,1)S(1)}) custom-call(s32[8]{0:T(128)} %index_ref.7, bf16[8,2,3,32,2048]{4,3,2,1,0:T(8,128)(2,1)} %states_ref.7, bf16[8,32,2048]{2,1,0:T(8,128)(2,1)} %targets_ref.7, s32[32,2048]{1,0:T(8,128)S(1)} %get-tuple-element.26.sea, ...), custom_call_target="tpu_custom_call" | custom-call | tf_op jit(solution)/shard_map/seam_first/pallas_call | solution.py:498
  36.8 0.0 copy-start
  36.8 2.8 %seam_last.1 = (f32[3,16,40,128]{3,2,1,0:T(8,128)S(1)}, f32[5,16,40,128]{3,2,1,0:T(8,128)S(1)}, bf16[16,40,128]{2,1,0:T(8,128)(2,1)S(1)}) custom-call(s32[32,2048]{1,0:T(8,128)S(1)} %get-tuple-element.26.sea, bf16[8,3,8,2048]{3,2,1,0:T(8,128)(2,1)S(1)} %get-tuple-element.30.ends, bf16[8,8,2048]{2,1,0:T(8,128)(2,1)S(1)} %get-tuple-element.31.seen_ends, ...), custom_call_target="tpu_custom_call" | custom-call | tf_op jit(solution)/shard_map/seam_last/pallas_call | solution.py:515
  39.7 2.0 %apply_potential.1 = (f32[16,2048]{1,0:T(8,128)S(1)}, f32[16,2048]{1,0:T(8,128)S(1)}) custom-call(s32[1]{0:T(128)} %bitcast.1.member_ref, bf16[40,256]{1,0:T(8,128)(2,1)S(1)} %make_coeffs.1.own_ref, bf16[40,256]{1,0:T(8,128)(2,1)S(1)} %collective-permute-done.2.near_ref, bf16[40,256]{1,0:T(8,128)(2,1)S(1)} %collective-permute-done.3.far_ref, ...), custom_call_target="tpu_custom_call" | custom-call | tf_op jit(solution)/shard_map/apply_potential/pallas_call | solution.py:660
  41.6 0.4 collective-permute-start.7
  42.1 1.0 %collective-permute-done.7 = f32[16,2048]{1,0:T(8,128)S(1)} collective-permute-done((f32[16,2048]{1,0:T(8,128)S(1)}, f32[16,2048]{1,0:T(8,128)S(1)}, u32[]{:S(2)}, u32[]{:S(2)}) %collective-permute-start.7) | collective-permute-done | bytes 131104 | tf_op jit(solution)/shard_map/ppermute | solution.py:784
  43.1 1.6 %collective-permute-start.8 = (f32[8,2048]{1,0:T(8,128)S(1)}, f32[8,2048]{1,0:T(8,128)S(1)}, u32[]{:S(2)}, u32[]{:S(2)}) collective-permute-start(f32[8,2048]{1,0:T(8,128)S(1)} %get-tuple-element.41), channel_id=1, source_target_pairs={{0,16},{8,24},{16,0},{24,8},{1,17},{9,25},{17,1},{25,9},{2,18},{10... | collective-permute-start | bytes 196616 | tf_op jit(solution)/shard_map/ppermute | solution.py:784
  44.7 0.6 collective-permute-start
  45.3 2.2 %hold.1.cols_ref = bf16[2048,1024]{1,0:T(8,128)(2,1)S(1)} custom-call(bf16[2048,1024]{1,0:T(8,128)(2,1)} %source_ref.1), custom_call_target="tpu_custom_call" | custom-call | tf_op jit(solution)/shard_map/hold/pallas_call | solution.py:183
  47.5 0.1 collective-permute-done.8.other_ref
  47.6 1.4 %project.1 = bf16[8,4,8,512]{3,2,1,0:T(8,128)(2,1)} custom-call(f32[8,2048]{1,0:T(8,128)S(1)} %get-tuple-element.42.own_ref, f32[8,2048]{1,0:T(8,128)S(1)} %collective-permute-done.8.other_ref, bf16[2048,1024]{1,0:T(8,128)(2,1)S(1)} %hold.1.cols_ref), custom_call_target="tpu_custom_call" | custom-call | tf_op jit(solution)/shard_map/project/pallas_call | solution.py:691
  49.0 5.2 %all-to-all-start.1 = ((bf16[32,8,512]{2,1,0:T(8,128)(2,1)}), bf16[32,8,512]{2,1,0:T(8,128)(2,1)S(1)}, u32[]{:S(2)}, u32[]{:S(2)}) async-start(bf16[32,8,512]{2,1,0:T(8,128)(2,1)} %bitcast.8), calls=%async_computation.1 | async-start | bytes 524288 | tf_op jit(solution)/shard_map/all_to_all | solution.py:823
  54.2 0.3 collective-permute-start.1
  54.6 1.3 %collective-permute-done.1.near_ref = bf16[2,256,256]{2,1,0:T(8,128)(2,1)S(1)} collective-permute-done((bf16[2,256,256]{2,1,0:T(8,128)(2,1)S(1)}, bf16[2,256,256]{2,1,0:T(8,128)(2,1)S(1)}, u32[]{:S(2)}, u32[]{:S(2)}) %collective-permute-start.1) | collective-permute-done | bytes 262176 | tf_op jit(solution)/shard_map/ppermute | solution.py:784
  55.9 1.1 %assemble.1 = (bf16[1024,256]{1,0:T(8,128)(2,1)S(1)}, f32[128,1024]{1,0:T(8,128)S(1)}) custom-call(s32[1]{0:T(128)} %bitcast.1.member_ref, bf16[256,256]{1,0:T(8,128)(2,1)S(1)} %bitcast.13, bf16[256,256]{1,0:T(8,128)(2,1)S(1)} %collective-permute-done.far_ref, bf16[2,256,256]{2,1,0:T(8,128)(2,1)S(1)} %collective-permute-done.1.near_ref, f32[128,1024]{1,0:T(8,128)} %control_ref.3), custom_call_target="tpu_custom_call" | custom-call | tf_op jit(solution)/shard_map/assemble/pallas_call | solution.py:716
  56.9 7.9 %all-to-all-done.1 = bf16[32,8,512]{2,1,0:T(8,128)(2,1)S(1)} async-done(((bf16[32,8,512]{2,1,0:T(8,128)(2,1)}), bf16[32,8,512]{2,1,0:T(8,128)(2,1)S(1)}, u32[]{:S(2)}, u32[]{:S(2)}) %all-to-all-start.1) | async-done | bytes 262176 | tf_op jit(solution)/shard_map/all_to_all | solution.py:823
  64.8 0.5 gradient.1.own_ref
  65.2 0.1 collective-permute-start.9
  65.3 1.5 %collective-permute-done.9.other_ref = f32[136,512]{1,0:T(8,128)S(1)} collective-permute-done((f32[136,512]{1,0:T(8,128)S(1)}, f32[136,512]{1,0:T(8,128)S(1)}, u32[]{:S(2)}, u32[]{:S(2)}) %collective-permute-start.9) | collective-permute-done | bytes 278560 | tf_op jit(solution)/shard_map/ppermute | solution.py:784
  66.9 1.0 %update.1 = f32[128,1024]{1,0:T(8,128)} custom-call(s32[1]{0:T(128)} %bitcast.core_ref, f32[128,1024]{1,0:T(8,128)S(1)} %get-tuple-element.23.control_ref, f32[136,512]{1,0:T(8,128)S(1)} %gradient.1.own_ref, f32[136,512]{1,0:T(8,128)S(1)} %collective-permute-done.9.other_ref), custom_call_target="tpu_custom_call" | custom-call | tf_op jit(solution)/shard_map/update/pallas_call | solution.py:772
  (12 shorter events, 0.1 us)
Async XLA Ops:
  1.8 27.4 %all-to-all-start = ((bf16[8,176,256]{2,1,0:T(8,128)(2,1)}), bf16[8,176,256]{2,1,0:T(8,128)(2,1)S(1)}, u32[]{:S(2)}, u32[]{:S(2)}) async-start(bf16[8,176,256]{2,1,0:T(8,128)(2,1)} %pack_pieces.1), calls=%async_computation | async-start | bytes 1441792 | tf_op jit(solution)/shard_map/all_to_all | solution.py:801
  12.6 20.9 %collective-permute-start.5 = (bf16[10,8,2048]{2,1,0:T(8,128)(2,1)}, bf16[10,8,2048]{2,1,0:T(8,128)(2,1)S(1)}, u32[]{:S(2)}, u32[]{:S(2)}) collective-permute-start(bf16[10,8,2048]{2,1,0:T(8,128)(2,1)} %get-tuple-element.29), channel_id=1, source_target_pairs={{0,1},{1,2},{2,3},{3,4},{4,5},{5,6},{6,7},{8,9},{9,10},{10,11},{11... | collective-permute-start | bytes 983048 | tf_op jit(solution)/shard_map/ppermute | solution.py:803
  16.5 20.3 %collective-permute-start.6 = (bf16[10,8,2048]{2,1,0:T(8,128)(2,1)}, bf16[10,8,2048]{2,1,0:T(8,128)(2,1)S(1)}, u32[]{:S(2)}, u32[]{:S(2)}) collective-permute-start(bf16[10,8,2048]{2,1,0:T(8,128)(2,1)} %get-tuple-element.32), channel_id=1, source_target_pairs={{1,0},{2,1},{3,2},{4,3},{5,4},{6,5},{7,6},{9,8},{10,9},{11,10},{12... | collective-permute-start | bytes 983048 | tf_op jit(solution)/shard_map/ppermute | solution.py:804
  29.5 10.1 %collective-permute-start.2 = (bf16[40,256]{1,0:T(8,128)(2,1)S(1)}, bf16[40,256]{1,0:T(8,128)(2,1)S(1)}, u32[]{:S(2)}, u32[]{:S(2)}) collective-permute-start(bf16[40,256]{1,0:T(8,128)(2,1)S(1)} %make_coeffs.1.own_ref), channel_id=1, source_target_pairs={{0,8},{8,0},{16,24},{24,16},{1,9},{9,1},{17,25},{25,17},{2,10},{10... | collective-permute-start | bytes 61448 | tf_op jit(solution)/shard_map/ppermute | solution.py:784
  29.6 10.1 %collective-permute-start.3 = (bf16[40,256]{1,0:T(8,128)(2,1)S(1)}, bf16[40,256]{1,0:T(8,128)(2,1)S(1)}, u32[]{:S(2)}, u32[]{:S(2)}) collective-permute-start(bf16[40,256]{1,0:T(8,128)(2,1)S(1)} %make_coeffs.1.own_ref), channel_id=1, source_target_pairs={{0,16},{8,24},{16,0},{24,8},{1,17},{9,25},{17,1},{25,9},{2,18},{10... | collective-permute-start | bytes 61448 | tf_op jit(solution)/shard_map/ppermute | solution.py:784
  31.1 8.5 %collective-permute-start.4 = (bf16[40,256]{1,0:T(8,128)(2,1)S(1)}, bf16[40,256]{1,0:T(8,128)(2,1)S(1)}, u32[]{:S(2)}, u32[]{:S(2)}) collective-permute-start(bf16[40,256]{1,0:T(8,128)(2,1)S(1)} %make_coeffs.1.own_ref), channel_id=1, source_target_pairs={{0,24},{8,16},{16,8},{24,0},{1,25},{9,17},{17,9},{25,1},{2,26},{10... | collective-permute-start | bytes 61448 | tf_op jit(solution)/shard_map/ppermute | solution.py:784
  36.8 2.9 %copy-start = (bf16[2048,1024]{1,0:T(8,128)(2,1)S(1)}, bf16[2048,1024]{1,0:T(8,128)(2,1)}, u32[]{:S(2)}) copy-start(bf16[2048,1024]{1,0:T(8,128)(2,1)} %source_ref.1) | copy-start | bytes 12582916
  41.6 1.4 %collective-permute-start.7 = (f32[16,2048]{1,0:T(8,128)S(1)}, f32[16,2048]{1,0:T(8,128)S(1)}, u32[]{:S(2)}, u32[]{:S(2)}) collective-permute-start(f32[16,2048]{1,0:T(8,128)S(1)} %get-tuple-element.40), channel_id=1, source_target_pairs={{0,8},{8,0},{16,24},{24,16},{1,9},{9,1},{17,25},{25,17},{2,10},{10... | collective-permute-start | bytes 393224 | tf_op jit(solution)/shard_map/ppermute | solution.py:784
  43.1 4.5 %collective-permute-start.8 = (f32[8,2048]{1,0:T(8,128)S(1)}, f32[8,2048]{1,0:T(8,128)S(1)}, u32[]{:S(2)}, u32[]{:S(2)}) collective-permute-start(f32[8,2048]{1,0:T(8,128)S(1)} %get-tuple-element.41), channel_id=1, source_target_pairs={{0,16},{8,24},{16,0},{24,8},{1,17},{9,25},{17,1},{25,9},{2,18},{10... | collective-permute-start | bytes 196616 | tf_op jit(solution)/shard_map/ppermute | solution.py:784
  44.7 9.5 %collective-permute-start = (bf16[256,256]{1,0:T(8,128)(2,1)S(1)}, bf16[256,256]{1,0:T(8,128)(2,1)S(1)}, u32[]{:S(2)}, u32[]{:S(2)}) collective-permute-start(bf16[256,256]{1,0:T(8,128)(2,1)S(1)} %bitcast.11), channel_id=1, source_target_pairs={{0,16},{8,24},{16,0},{24,8},{1,17},{9,25},{17,1},{25,9},{2,18},{10... | collective-permute-start | bytes 393224 | tf_op jit(solution)/shard_map/ppermute | solution.py:784
  49.0 15.8 %all-to-all-start.1 = ((bf16[32,8,512]{2,1,0:T(8,128)(2,1)}), bf16[32,8,512]{2,1,0:T(8,128)(2,1)S(1)}, u32[]{:S(2)}, u32[]{:S(2)}) async-start(bf16[32,8,512]{2,1,0:T(8,128)(2,1)} %bitcast.8), calls=%async_computation.1 | async-start | bytes 524288 | tf_op jit(solution)/shard_map/all_to_all | solution.py:823
  54.2 1.6 %collective-permute-start.1 = (bf16[2,256,256]{2,1,0:T(8,128)(2,1)S(1)}, bf16[2,256,256]{2,1,0:T(8,128)(2,1)S(1)}, u32[]{:S(2)}, u32[]{:S(2)}) collective-permute-start(bf16[2,256,256]{2,1,0:T(8,128)(2,1)S(1)} %pad_maximum_fusion), channel_id=1, source_target_pairs={{0,8},{8,0},{16,24},{24,16},{1,9},{9,1},{17,25},{25,17},{2,10},{10... | collective-permute-start | bytes 786440 | tf_op jit(solution)/shard_map/ppermute | solution.py:784
  65.2 1.6 %collective-permute-start.9 = (f32[136,512]{1,0:T(8,128)S(1)}, f32[136,512]{1,0:T(8,128)S(1)}, u32[]{:S(2)}, u32[]{:S(2)}) collective-permute-start(f32[136,512]{1,0:T(8,128)S(1)} %gradient.1.own_ref), channel_id=1, source_target_pairs={{0,8},{8,0},{16,24},{24,16},{1,9},{9,1},{17,25},{25,17},{2,10},{10... | collective-permute-start | bytes 835592 | tf_op jit(solution)/shard_map/ppermute | solution.py:784

commit v7 on v6

--- a/solution.py
+++ b/solution.py
@@ -698,19 +698,19 @@
     )(own, other, basis_cols)
 
 
-def assemble(member_ref, own_ref, far_ref, near_ref, control_ref, basis_ref, kept_ref, sem):
+def assemble(member_ref, own_ref, far_ref, near_ref, both_ref, control_ref, basis_ref, kept_ref, sem):
     copy = pltpu.make_async_copy(control_ref, kept_ref, sem)
     copy.start()
     member = member_ref[0]
     quarter = own_ref.shape[1]
-    parts = (own_ref[...], near_ref[0], far_ref[...], near_ref[1])
+    parts = (own_ref[...], near_ref[...], far_ref[...], both_ref[...])
     for bits, part in enumerate(parts):
         at = pl.multiple_of((member ^ bits) * quarter, quarter)
         basis_ref[pl.ds(at, quarter), :] = part.astype(F32).T.astype(BF16)
     copy.wait()
 
 
-def assembled(member, own, far, near, control):
+def assembled(member, own, far, near, both, control):
     rows, _ = own.shape
     width = control.shape[1]
     return pl.pallas_call(
@@ -720,11 +720,11 @@
             jax.ShapeDtypeStruct((width, rows), BF16),
             jax.ShapeDtypeStruct(control.shape, F32),
         ),
-        in_specs=[SMEM, VMEM, VMEM, VMEM, HBM],
+        in_specs=[SMEM, VMEM, VMEM, VMEM, VMEM, HBM],
         out_specs=(VMEM, VMEM),
         scratch_shapes=[pltpu.SemaphoreType.DMA],
         compiler_params=limit(24),
-    )(member.reshape(1), own, far, near, in_hbm(control))
+    )(member.reshape(1), own, far, near, both, in_hbm(control))
 
 
 def gradient(slab_ref, basis_ref, projected_ref, out_ref):
@@ -826,8 +826,9 @@
     part = pieces[:, rows_out : rows_out + rows, :].reshape(slabs, 2, members // 2, single, quarter)
     part = part.transpose(0, 2, 1, 3, 4).reshape(slabs * rows, quarter)
     far = partner(part, 2)
-    near = partner(jnp.stack([part, far]), 1)
-    basis, kept = assembled(member, part, far, near, control)
+    near = partner(part, 1)
+    both = partner(far, 1)
+    basis, kept = assembled(member, part, far, near, both, control)
     block = gradient_block(slab, basis, projected_half, rows_out)
     other = partner(block, 1)
     return updated(core, kept, block, other)

time: 68.4 us -> 67.8 us (level)
  waiting for transfers between devices: 13.8 us -> 12.8 us
    all_to_all x1, waiting for transfers between devices: 7.86 us -> 0.16 us  [on_device(): lax.all_to_all(send.reshape(members * slabs, single, half), ('space', 'en...]
    ppermute x8 -> x9, waiting for transfers between devices: 3.95 us -> 10.7 us  [partner(): return lax.ppermute(value, 'ens', [(i, i ^ bit) for i in range(count)])]
    ppermute x8 -> x9, starting transfers between devices: 4.88 us -> 5.8 us  [partner(): return lax.ppermute(value, 'ens', [(i, i ^ bit) for i in range(count)])]
  transfers between devices with their start and end apart: 12 -> 13, of which waited for: 6 -> 7; matrix products, arithmetic and copies ran while one was open for 0% -> 0% of each run, Pallas kernels for 38% -> 36%
where the time goes in v7:
time: 67.8 us; the launch traced here: 67.3 us
  Pallas kernels  31.2 us (46%)
  starting transfers between devices  23 us (34%)
  waiting for transfers between devices  12.8 us (19%)
    ppermute x9, waiting for transfers between devices, partner(): return lax.ppermute(value, 'ens', [(i, i ^ bit) for i in range(count)])  10.7 us
    pallas_call x1, Pallas kernels, inner_pass(): pl.pallas_call(inner_states, name='inner_states', out_shape=outs, in_spec...  9.47 us
    all_to_all x1, starting transfers between devices, on_device(): pieces = lax.all_to_all(pieces, 'space', 0, 0)  7.32 us
    ppermute x9, starting transfers between devices, partner(): return lax.ppermute(value, 'ens', [(i, i ^ bit) for i in range(count)])  5.8 us
    all_to_all x1, starting transfers between devices, on_device(): lax.all_to_all(send.reshape(members * slabs, single, half), ('space', 'en...  4.68 us
    ppermute x1, starting transfers between devices, on_device(): before = lax.ppermute(up, 'space', [(i, i + 1) for i in range(slabs - 1)])  3.94 us
    pallas_call x1, Pallas kernels, edge_messages(): pl.pallas_call(pack_edges, name='pack_edges', out_shape=(edges, edges), i...  3.41 us
    pallas_call x1, Pallas kernels, seam_first_pass(): pl.pallas_call(seam_first, name='seam_first', out_shape=(sums,) + end_sha...  3.33 us
  transfers between devices with their start and end apart: 13, of which 7 were waited for; matrix products, arithmetic and copies ran while one was open for 0% of the time, Pallas kernels for 36%

profile of v7, /device:TPU:0, one launch (start us, length us, event | category | flops | bytes accessed | tf_op | source)
XLA Modules:
  0.0 67.3 jit_solution(15557619649502684285)
XLA Ops:
  0.0 1.8 %pack_pieces.1 = bf16[8,176,256]{2,1,0:T(8,128)(2,1)} custom-call(s32[1]{0:T(128)} %bitcast.1.member_ref, bf16[32,1024]{1,0:T(8,128)(2,1)} %basis_ref.3, f32[128,1024]{1,0:T(8,128)} %control_ref.3), custom_call_target="tpu_custom_call" | custom-call | tf_op jit(solution)/shard_map/pack_pieces/pallas_call | solution.py:156
  1.8 7.3 %all-to-all-start = ((bf16[8,176,256]{2,1,0:T(8,128)(2,1)}), bf16[8,176,256]{2,1,0:T(8,128)(2,1)S(1)}, u32[]{:S(2)}, u32[]{:S(2)}) async-start(bf16[8,176,256]{2,1,0:T(8,128)(2,1)} %pack_pieces.1), calls=%async_computation | async-start | bytes 1441792 | tf_op jit(solution)/shard_map/all_to_all | solution.py:801
  9.2 3.4 %pack_edges.1 = (bf16[10,8,2048]{2,1,0:T(8,128)(2,1)}, bf16[10,8,2048]{2,1,0:T(8,128)(2,1)}) custom-call(s32[8]{0:T(128)} %index_ref.7, bf16[8,2,3,32,2048]{4,3,2,1,0:T(8,128)(2,1)} %states_ref.7, bf16[8,32,2048]{2,1,0:T(8,128)(2,1)} %targets_ref.7, s32[32,2048]{1,0:T(8,128)} %sea_ref.5), custom_call_target="tpu_custom_call" | custom-call | tf_op jit(solution)/shard_map/pack_edges/pallas_call | solution.py:106
  12.6 3.9 %collective-permute-start.6 = (bf16[10,8,2048]{2,1,0:T(8,128)(2,1)}, bf16[10,8,2048]{2,1,0:T(8,128)(2,1)S(1)}, u32[]{:S(2)}, u32[]{:S(2)}) collective-permute-start(bf16[10,8,2048]{2,1,0:T(8,128)(2,1)} %get-tuple-element.29), channel_id=1, source_target_pairs={{0,1},{1,2},{2,3},{3,4},{4,5},{5,6},{6,7},{8,9},{9,10},{10,11},{11... | collective-permute-start | bytes 983048 | tf_op jit(solution)/shard_map/ppermute | solution.py:803
  16.5 1.3 %collective-permute-start.7 = (bf16[10,8,2048]{2,1,0:T(8,128)(2,1)}, bf16[10,8,2048]{2,1,0:T(8,128)(2,1)S(1)}, u32[]{:S(2)}, u32[]{:S(2)}) collective-permute-start(bf16[10,8,2048]{2,1,0:T(8,128)(2,1)} %get-tuple-element.32), channel_id=1, source_target_pairs={{1,0},{2,1},{3,2},{4,3},{5,4},{6,5},{7,6},{9,8},{10,9},{11,10},{12... | collective-permute-start | bytes 983048 | tf_op jit(solution)/shard_map/ppermute | solution.py:804
  17.8 9.5 %inner_states.1 = (f32[3,16,32,128]{3,2,1,0:T(8,128)S(1)}, f32[5,16,32,128]{3,2,1,0:T(8,128)S(1)}, bf16[32,1024]{1,0:T(8,128)(2,1)S(1)}) custom-call(s32[8]{0:T(128)} %index_ref.7, bf16[8,2,3,32,2048]{4,3,2,1,0:T(8,128)(2,1)} %states_ref.7, bf16[8,32,2048]{2,1,0:T(8,128)(2,1)} %targets_ref.7, s32[32,2048]{1,0:T(8,128)} %sea_ref.5, bf16[32,1024]{1,0:T(8,128)(2,1)} %basis_ref.3), custom_call_target="tpu_custom_call" | custom-call | tf_op jit(solution)/shard_map/inner_states/pallas_call | solution.py:339
  27.3 2.0 %all-to-all-done.pieces_ref = bf16[8,176,256]{2,1,0:T(8,128)(2,1)S(1)} async-done(((bf16[8,176,256]{2,1,0:T(8,128)(2,1)}), bf16[8,176,256]{2,1,0:T(8,128)(2,1)S(1)}, u32[]{:S(2)}, u32[]{:S(2)}) %all-to-all-start) | async-done | bytes 720928 | tf_op jit(solution)/shard_map/all_to_all | solution.py:801
  29.3 0.2 make_coeffs.1.own_ref
  29.5 0.1 collective-permute-start.3
  29.6 1.6 %collective-permute-start.4 = (bf16[40,256]{1,0:T(8,128)(2,1)S(1)}, bf16[40,256]{1,0:T(8,128)(2,1)S(1)}, u32[]{:S(2)}, u32[]{:S(2)}) collective-permute-start(bf16[40,256]{1,0:T(8,128)(2,1)S(1)} %make_coeffs.1.own_ref), channel_id=1, source_target_pairs={{0,16},{8,24},{16,0},{24,8},{1,17},{9,25},{17,1},{25,9},{2,18},{10... | collective-permute-start | bytes 61448 | tf_op jit(solution)/shard_map/ppermute | solution.py:784
  31.1 0.3 collective-permute-start.5
  31.4 2.0 %fetch_ends.1 = (s32[32,2048]{1,0:T(8,128)S(1)}, bf16[8,3,8,2048]{3,2,1,0:T(8,128)(2,1)S(1)}, bf16[8,8,2048]{2,1,0:T(8,128)(2,1)S(1)}) custom-call(s32[8]{0:T(128)} %index_ref.7, bf16[8,2,3,32,2048]{4,3,2,1,0:T(8,128)(2,1)} %states_ref.7, bf16[8,32,2048]{2,1,0:T(8,128)(2,1)} %targets_ref.7, s32[32,2048]{1,0:T(8,128)} %sea_ref.5), custom_call_target="tpu_custom_call" | custom-call | tf_op jit(solution)/shard_map/fetch_ends/pallas_call | solution.py:385
  33.4 3.3 %seam_first.1 = (f32[8,16,8,128]{3,2,1,0:T(8,128)S(1)}, bf16[8,3,8,2048]{3,2,1,0:T(8,128)(2,1)S(1)}, bf16[8,8,2048]{2,1,0:T(8,128)(2,1)S(1)}) custom-call(s32[8]{0:T(128)} %index_ref.7, bf16[8,2,3,32,2048]{4,3,2,1,0:T(8,128)(2,1)} %states_ref.7, bf16[8,32,2048]{2,1,0:T(8,128)(2,1)} %targets_ref.7, s32[32,2048]{1,0:T(8,128)S(1)} %get-tuple-element.26.sea, ...), custom_call_target="tpu_custom_call" | custom-call | tf_op jit(solution)/shard_map/seam_first/pallas_call | solution.py:498
  36.8 0.0 copy-start
  36.8 2.8 %seam_last.1 = (f32[3,16,40,128]{3,2,1,0:T(8,128)S(1)}, f32[5,16,40,128]{3,2,1,0:T(8,128)S(1)}, bf16[16,40,128]{2,1,0:T(8,128)(2,1)S(1)}) custom-call(s32[32,2048]{1,0:T(8,128)S(1)} %get-tuple-element.26.sea, bf16[8,3,8,2048]{3,2,1,0:T(8,128)(2,1)S(1)} %get-tuple-element.30.ends, bf16[8,8,2048]{2,1,0:T(8,128)(2,1)S(1)} %get-tuple-element.31.seen_ends, ...), custom_call_target="tpu_custom_call" | custom-call | tf_op jit(solution)/shard_map/seam_last/pallas_call | solution.py:515
  39.6 2.0 %apply_potential.1 = (f32[16,2048]{1,0:T(8,128)S(1)}, f32[16,2048]{1,0:T(8,128)S(1)}) custom-call(s32[1]{0:T(128)} %bitcast.1.member_ref, bf16[40,256]{1,0:T(8,128)(2,1)S(1)} %make_coeffs.1.own_ref, bf16[40,256]{1,0:T(8,128)(2,1)S(1)} %collective-permute-done.3.near_ref, bf16[40,256]{1,0:T(8,128)(2,1)S(1)} %collective-permute-done.4.far_ref, ...), custom_call_target="tpu_custom_call" | custom-call | tf_op jit(solution)/shard_map/apply_potential/pallas_call | solution.py:660
  41.6 0.4 collective-permute-start.8
  42.1 1.0 %collective-permute-done.8 = f32[16,2048]{1,0:T(8,128)S(1)} collective-permute-done((f32[16,2048]{1,0:T(8,128)S(1)}, f32[16,2048]{1,0:T(8,128)S(1)}, u32[]{:S(2)}, u32[]{:S(2)}) %collective-permute-start.8) | collective-permute-done | bytes 131104 | tf_op jit(solution)/shard_map/ppermute | solution.py:784
  43.1 1.6 %collective-permute-start.9 = (f32[8,2048]{1,0:T(8,128)S(1)}, f32[8,2048]{1,0:T(8,128)S(1)}, u32[]{:S(2)}, u32[]{:S(2)}) collective-permute-start(f32[8,2048]{1,0:T(8,128)S(1)} %get-tuple-element.41), channel_id=1, source_target_pairs={{0,16},{8,24},{16,0},{24,8},{1,17},{9,25},{17,1},{25,9},{2,18},{10... | collective-permute-start | bytes 196616 | tf_op jit(solution)/shard_map/ppermute | solution.py:784
  44.7 2.2 %hold.1.cols_ref = bf16[2048,1024]{1,0:T(8,128)(2,1)S(1)} custom-call(bf16[2048,1024]{1,0:T(8,128)(2,1)} %source_ref.1), custom_call_target="tpu_custom_call" | custom-call | tf_op jit(solution)/shard_map/hold/pallas_call | solution.py:183
  46.9 0.7 collective-permute-done.9.other_ref
  47.5 1.4 %project.1 = bf16[8,4,8,512]{3,2,1,0:T(8,128)(2,1)} custom-call(f32[8,2048]{1,0:T(8,128)S(1)} %get-tuple-element.42.own_ref, f32[8,2048]{1,0:T(8,128)S(1)} %collective-permute-done.9.other_ref, bf16[2048,1024]{1,0:T(8,128)(2,1)S(1)} %hold.1.cols_ref), custom_call_target="tpu_custom_call" | custom-call | tf_op jit(solution)/shard_map/project/pallas_call | solution.py:691
  48.9 4.7 %all-to-all-start.1 = ((bf16[32,8,512]{2,1,0:T(8,128)(2,1)}), bf16[32,8,512]{2,1,0:T(8,128)(2,1)S(1)}, u32[]{:S(2)}, u32[]{:S(2)}) async-start(bf16[32,8,512]{2,1,0:T(8,128)(2,1)} %bitcast.6), calls=%async_computation.1 | async-start | bytes 524288 | tf_op jit(solution)/shard_map/all_to_all | solution.py:823
  53.6 1.8 %collective-permute-start = (bf16[256,256]{1,0:T(8,128)(2,1)S(1)}, bf16[256,256]{1,0:T(8,128)(2,1)S(1)}, u32[]{:S(2)}, u32[]{:S(2)}) collective-permute-start(bf16[256,256]{1,0:T(8,128)(2,1)S(1)} %bitcast.10), channel_id=1, source_target_pairs={{0,16},{8,24},{16,0},{24,8},{1,17},{9,25},{17,1},{25,9},{2,18},{10... | collective-permute-start | bytes 393224 | tf_op jit(solution)/shard_map/ppermute | solution.py:784
  55.5 6.1 %collective-permute-done.far_ref = bf16[256,256]{1,0:T(8,128)(2,1)S(1)} collective-permute-done((bf16[256,256]{1,0:T(8,128)(2,1)S(1)}, bf16[256,256]{1,0:T(8,128)(2,1)S(1)}, u32[]{:S(2)}, u32[]{:S(2)}) %collective-permute-start) | collective-permute-done | bytes 131104 | tf_op jit(solution)/shard_map/ppermute | solution.py:784
  61.6 1.3 %collective-permute-done.2.both_ref = bf16[256,256]{1,0:T(8,128)(2,1)S(1)} collective-permute-done((bf16[256,256]{1,0:T(8,128)(2,1)S(1)}, bf16[256,256]{1,0:T(8,128)(2,1)S(1)}, u32[]{:S(2)}, u32[]{:S(2)}) %collective-permute-start.2) | collective-permute-done | bytes 131104 | tf_op jit(solution)/shard_map/ppermute | solution.py:784
  62.9 1.1 %assemble.1 = (bf16[1024,256]{1,0:T(8,128)(2,1)S(1)}, f32[128,1024]{1,0:T(8,128)S(1)}) custom-call(s32[1]{0:T(128)} %bitcast.1.member_ref, bf16[256,256]{1,0:T(8,128)(2,1)S(1)} %bitcast.12, bf16[256,256]{1,0:T(8,128)(2,1)S(1)} %collective-permute-done.far_ref, bf16[256,256]{1,0:T(8,128)(2,1)S(1)} %collective-permute-done.1.near_ref, ...), custom_call_target="tpu_custom_call" | custom-call | tf_op jit(solution)/shard_map/assemble/pallas_call | solution.py:716
  64.0 0.2 all-to-all-done.1
  64.2 0.5 gradient.1.own_ref
  64.6 0.1 collective-permute-start.10
  64.7 1.5 %collective-permute-done.10.other_ref = f32[136,512]{1,0:T(8,128)S(1)} collective-permute-done((f32[136,512]{1,0:T(8,128)S(1)}, f32[136,512]{1,0:T(8,128)S(1)}, u32[]{:S(2)}, u32[]{:S(2)}) %collective-permute-start.10) | collective-permute-done | bytes 278560 | tf_op jit(solution)/shard_map/ppermute | solution.py:784
  66.3 1.0 %update.1 = f32[128,1024]{1,0:T(8,128)} custom-call(s32[1]{0:T(128)} %bitcast.core_ref, f32[128,1024]{1,0:T(8,128)S(1)} %get-tuple-element.23.control_ref, f32[136,512]{1,0:T(8,128)S(1)} %gradient.1.own_ref, f32[136,512]{1,0:T(8,128)S(1)} %collective-permute-done.10.other_ref), custom_call_target="tpu_custom_call" | custom-call | tf_op jit(solution)/shard_map/update/pallas_call | solution.py:772
  (13 shorter events, 0.1 us)
Async XLA Ops:
  1.8 27.4 %all-to-all-start = ((bf16[8,176,256]{2,1,0:T(8,128)(2,1)}), bf16[8,176,256]{2,1,0:T(8,128)(2,1)S(1)}, u32[]{:S(2)}, u32[]{:S(2)}) async-start(bf16[8,176,256]{2,1,0:T(8,128)(2,1)} %pack_pieces.1), calls=%async_computation | async-start | bytes 1441792 | tf_op jit(solution)/shard_map/all_to_all | solution.py:801
  12.6 20.9 %collective-permute-start.6 = (bf16[10,8,2048]{2,1,0:T(8,128)(2,1)}, bf16[10,8,2048]{2,1,0:T(8,128)(2,1)S(1)}, u32[]{:S(2)}, u32[]{:S(2)}) collective-permute-start(bf16[10,8,2048]{2,1,0:T(8,128)(2,1)} %get-tuple-element.29), channel_id=1, source_target_pairs={{0,1},{1,2},{2,3},{3,4},{4,5},{5,6},{6,7},{8,9},{9,10},{10,11},{11... | collective-permute-start | bytes 983048 | tf_op jit(solution)/shard_map/ppermute | solution.py:803
  16.5 20.3 %collective-permute-start.7 = (bf16[10,8,2048]{2,1,0:T(8,128)(2,1)}, bf16[10,8,2048]{2,1,0:T(8,128)(2,1)S(1)}, u32[]{:S(2)}, u32[]{:S(2)}) collective-permute-start(bf16[10,8,2048]{2,1,0:T(8,128)(2,1)} %get-tuple-element.32), channel_id=1, source_target_pairs={{1,0},{2,1},{3,2},{4,3},{5,4},{6,5},{7,6},{9,8},{10,9},{11,10},{12... | collective-permute-start | bytes 983048 | tf_op jit(solution)/shard_map/ppermute | solution.py:804
  29.5 10.1 %collective-permute-start.3 = (bf16[40,256]{1,0:T(8,128)(2,1)S(1)}, bf16[40,256]{1,0:T(8,128)(2,1)S(1)}, u32[]{:S(2)}, u32[]{:S(2)}) collective-permute-start(bf16[40,256]{1,0:T(8,128)(2,1)S(1)} %make_coeffs.1.own_ref), channel_id=1, source_target_pairs={{0,8},{8,0},{16,24},{24,16},{1,9},{9,1},{17,25},{25,17},{2,10},{10... | collective-permute-start | bytes 61448 | tf_op jit(solution)/shard_map/ppermute | solution.py:784
  29.6 10.1 %collective-permute-start.4 = (bf16[40,256]{1,0:T(8,128)(2,1)S(1)}, bf16[40,256]{1,0:T(8,128)(2,1)S(1)}, u32[]{:S(2)}, u32[]{:S(2)}) collective-permute-start(bf16[40,256]{1,0:T(8,128)(2,1)S(1)} %make_coeffs.1.own_ref), channel_id=1, source_target_pairs={{0,16},{8,24},{16,0},{24,8},{1,17},{9,25},{17,1},{25,9},{2,18},{10... | collective-permute-start | bytes 61448 | tf_op jit(solution)/shard_map/ppermute | solution.py:784
  31.1 8.5 %collective-permute-start.5 = (bf16[40,256]{1,0:T(8,128)(2,1)S(1)}, bf16[40,256]{1,0:T(8,128)(2,1)S(1)}, u32[]{:S(2)}, u32[]{:S(2)}) collective-permute-start(bf16[40,256]{1,0:T(8,128)(2,1)S(1)} %make_coeffs.1.own_ref), channel_id=1, source_target_pairs={{0,24},{8,16},{16,8},{24,0},{1,25},{9,17},{17,9},{25,1},{2,26},{10... | collective-permute-start | bytes 61448 | tf_op jit(solution)/shard_map/ppermute | solution.py:784
  36.8 2.9 %copy-start = (bf16[2048,1024]{1,0:T(8,128)(2,1)S(1)}, bf16[2048,1024]{1,0:T(8,128)(2,1)}, u32[]{:S(2)}) copy-start(bf16[2048,1024]{1,0:T(8,128)(2,1)} %source_ref.1) | copy-start | bytes 12582916
  41.6 1.4 %collective-permute-start.8 = (f32[16,2048]{1,0:T(8,128)S(1)}, f32[16,2048]{1,0:T(8,128)S(1)}, u32[]{:S(2)}, u32[]{:S(2)}) collective-permute-start(f32[16,2048]{1,0:T(8,128)S(1)} %get-tuple-element.40), channel_id=1, source_target_pairs={{0,8},{8,0},{16,24},{24,16},{1,9},{9,1},{17,25},{25,17},{2,10},{10... | collective-permute-start | bytes 393224 | tf_op jit(solution)/shard_map/ppermute | solution.py:784
  43.1 4.4 %collective-permute-start.9 = (f32[8,2048]{1,0:T(8,128)S(1)}, f32[8,2048]{1,0:T(8,128)S(1)}, u32[]{:S(2)}, u32[]{:S(2)}) collective-permute-start(f32[8,2048]{1,0:T(8,128)S(1)} %get-tuple-element.41), channel_id=1, source_target_pairs={{0,16},{8,24},{16,0},{24,8},{1,17},{9,25},{17,1},{25,9},{2,18},{10... | collective-permute-start | bytes 196616 | tf_op jit(solution)/shard_map/ppermute | solution.py:784
  48.9 15.3 %all-to-all-start.1 = ((bf16[32,8,512]{2,1,0:T(8,128)(2,1)}), bf16[32,8,512]{2,1,0:T(8,128)(2,1)S(1)}, u32[]{:S(2)}, u32[]{:S(2)}) async-start(bf16[32,8,512]{2,1,0:T(8,128)(2,1)} %bitcast.6), calls=%async_computation.1 | async-start | bytes 524288 | tf_op jit(solution)/shard_map/all_to_all | solution.py:823
  53.6 8.0 %collective-permute-start = (bf16[256,256]{1,0:T(8,128)(2,1)S(1)}, bf16[256,256]{1,0:T(8,128)(2,1)S(1)}, u32[]{:S(2)}, u32[]{:S(2)}) collective-permute-start(bf16[256,256]{1,0:T(8,128)(2,1)S(1)} %bitcast.10), channel_id=1, source_target_pairs={{0,16},{8,24},{16,0},{24,8},{1,17},{9,25},{17,1},{25,9},{2,18},{10... | collective-permute-start | bytes 393224 | tf_op jit(solution)/shard_map/ppermute | solution.py:784
  55.5 6.1 %collective-permute-start.1 = (bf16[256,256]{1,0:T(8,128)(2,1)S(1)}, bf16[256,256]{1,0:T(8,128)(2,1)S(1)}, u32[]{:S(2)}, u32[]{:S(2)}) collective-permute-start(bf16[256,256]{1,0:T(8,128)(2,1)S(1)} %bitcast.11), channel_id=1, source_target_pairs={{0,8},{8,0},{16,24},{24,16},{1,9},{9,1},{17,25},{25,17},{2,10},{10... | collective-permute-start | bytes 393224 | tf_op jit(solution)/shard_map/ppermute | solution.py:784
  61.6 1.3 %collective-permute-start.2 = (bf16[256,256]{1,0:T(8,128)(2,1)S(1)}, bf16[256,256]{1,0:T(8,128)(2,1)S(1)}, u32[]{:S(2)}, u32[]{:S(2)}) collective-permute-start(bf16[256,256]{1,0:T(8,128)(2,1)S(1)} %collective-permute-done.far_ref), channel_id=1, source_target_pairs={{0,8},{8,0},{16,24},{24,16},{1,9},{9,1},{17,25},{25,17},{2,10},{10... | collective-permute-start | bytes 393224 | tf_op jit(solution)/shard_map/ppermute | solution.py:784
  64.6 1.6 %collective-permute-start.10 = (f32[136,512]{1,0:T(8,128)S(1)}, f32[136,512]{1,0:T(8,128)S(1)}, u32[]{:S(2)}, u32[]{:S(2)}) collective-permute-start(f32[136,512]{1,0:T(8,128)S(1)} %gradient.1.own_ref), channel_id=1, source_target_pairs={{0,8},{8,0},{16,24},{24,16},{1,9},{9,1},{17,25},{25,17},{2,10},{10... | collective-permute-start | bytes 835592 | tf_op jit(solution)/shard_map/ppermute | solution.py:784
